TPU v7x, 32 devices: a whole 2x2x4 slice. The times are simulated.
32 devices in a mesh: outer: 8 (over z, x), inner: 4 (over y, core).
Axes of the slice: x: 2, y: 2, z: 4, core: 2. Of those that a mesh axis runs over, the one named last changes fastest.
Arguments:
- images: bfloat16 [32, 14, 14, 768], P(('outer', 'inner')), may hold values from -6 to 6
- cotangent: bfloat16 [32, 14, 14, 768], P(('outer', 'inner')), may hold values from -20 to 20
- conv_weight: float32 [7, 7, 768], replicated, may hold values from -0.875 to 0.875
- conv_bias: float32 [768], replicated, may hold values from -3 to 3
- norm_gain: float32 [768], replicated, may hold values from 0.1 to 1.9
- norm_bias: float32 [768], replicated, may hold values from -2 to 2
- expand_weight: bfloat16 [768, 3072], replicated, may hold values from -0.21875 to 0.21875
- expand_bias: float32 [3072], replicated, may hold values from -3 to 3
- reduce_weight: bfloat16 [3072, 768], replicated, may hold values from -0.109375 to 0.109375
- layer_scale: float32 [768], replicated, may hold values from 0.2 to 2
- right_first: float32 [3072, 32], replicated, may hold values from -5 to 5
- right_second: float32 [768, 32], replicated, may hold values from -5 to 5
Outputs:
- next_first: float32 [3072, 32], replicated
- next_second: float32 [768, 32], replicated
All inputs are finite; a program needn't handle non-finite values.
Results may differ from a plain program's by a relative error of at most 0.009.
Values may be sent and summed in bfloat16 or wider, within the bound.
No kernel may reach another device: no remote copies, remote signals or barrier semaphores. Data moves between devices by JAX's collectives and lax.ppermute only.
A program may use at most 64 MiB of HBM per device.

v0:
```python
import jax
import jax.numpy as jnp
from jax import lax
from jax.sharding import PartitionSpec as P


def depthwise(images, conv_weight, conv_bias):
    kernel = conv_weight.shape[0]
    margin = kernel // 2
    extent = images.shape[1]
    widened = jnp.pad(
        images.astype(jnp.float32), ((0, 0), (margin, margin), (margin, margin), (0, 0))
    )
    summed = jnp.zeros(images.shape, jnp.float32) + conv_bias
    for tap_row in range(kernel):
        for tap_col in range(kernel):
            summed = (
                summed
                + widened[:, tap_row : tap_row + extent, tap_col : tap_col + extent, :]
                * conv_weight[tap_row, tap_col]
            )
    return summed


def layer_norm(values, norm_gain, norm_bias):
    center = jnp.mean(values, axis=-1, keepdims=True)
    spread = jnp.mean((values - center) ** 2, axis=-1, keepdims=True)
    return ((values - center) * lax.rsqrt(spread + 1e-06) * norm_gain + norm_bias).astype(
        jnp.bfloat16
    )


def gelu_slope(hidden):
    return (
        0.5 * (1.0 + lax.erf(hidden * 0.7071067811865476))
        + hidden * jnp.exp(-0.5 * hidden * hidden) * 0.3989422804014327
    )


def project(rows_left, rows_right, right):
    thin = jnp.dot(
        rows_right, right.astype(jnp.bfloat16), preferred_element_type=jnp.float32
    ).astype(jnp.bfloat16)
    return lax.dot_general(
        rows_left, thin, (((0,), (0,)), ((), ())), preferred_element_type=jnp.float32
    )


def back_project(rows_left, rows_right, basis):
    rounded = basis.astype(jnp.bfloat16)
    thin = jnp.dot(rows_left, rounded, preferred_element_type=jnp.float32).astype(jnp.bfloat16)
    return lax.dot_general(
        rows_right, thin, (((0,), (0,)), ((), ())), preferred_element_type=jnp.float32
    )


def gram_of(partial_value):
    return lax.dot_general(
        partial_value, partial_value, (((0,), (0,)), ((), ())), precision=lax.Precision.HIGHEST
    )


def apply_factor(gram_matrix, partial_value):
    factor = jnp.linalg.cholesky(gram_matrix)
    return jax.scipy.linalg.solve_triangular(factor, partial_value.T, lower=True).T


def refine_layer(partial_value, rows_left, rows_right, scale):
    summed = lax.psum(partial_value, ("outer", "inner"))
    basis = apply_factor(gram_of(summed), summed)
    term = back_project(rows_left, rows_right, basis)
    return lax.psum(term, ("outer", "inner")) * scale


def shards(
    images,
    cotangent,
    conv_weight,
    conv_bias,
    norm_gain,
    norm_bias,
    expand_weight,
    expand_bias,
    reduce_weight,
    layer_scale,
    right_first,
    right_second,
):
    count = lax.axis_size("outer") * lax.axis_size("inner")
    scale = jnp.float32(1.0) / count
    width = images.shape[-1]
    conv_out = depthwise(images, conv_weight, conv_bias).reshape((-1, width))
    normed = layer_norm(conv_out, norm_gain, norm_bias)
    hidden = jnp.dot(normed, expand_weight, preferred_element_type=jnp.float32) + expand_bias
    activated = jax.nn.gelu(hidden, approximate=False).astype(jnp.bfloat16)
    out_grad = (cotangent.reshape((-1, width)).astype(jnp.float32) * layer_scale).astype(
        jnp.bfloat16
    )
    p_second = project(activated, out_grad, right_second)
    back = lax.dot_general(
        out_grad, reduce_weight, (((1,), (1,)), ((), ())), preferred_element_type=jnp.float32
    )
    hid_grad = (back * gelu_slope(hidden)).astype(jnp.bfloat16)
    p_first = project(normed, hid_grad, right_first)
    next_second = refine_layer(p_second, activated, out_grad, scale)
    next_first = refine_layer(p_first, normed, hid_grad, scale)
    return (next_first, next_second)


def solution(mesh):
    in_specs = (
        P(("outer", "inner"), None, None, None),
        P(("outer", "inner"), None, None, None),
        P(),
        P(),
        P(),
        P(),
        P(),
        P(),
        P(),
        P(),
        P(),
        P(),
    )
    out_specs = (P(), P())
    return jax.shard_map(shards, mesh=mesh, in_specs=in_specs, out_specs=out_specs, check_vma=False)
```

profile of v0, /device:TPU:0, one launch (start us, length us, event | category | flops | bytes accessed | tf_op | source)
XLA Modules:
  0.0 326.7 jit_solution(6438249491796293082)
XLA Ops:
  7.2 1.1 slice_reduce_fusion.46
  8.3 1.4 slice_reduce_fusion.48
  9.7 1.4 slice_reduce_fusion.47
  11.1 1.0 convert_element_type.50
  12.2 6.3 %fusion.126 = (f32[14,14]{1,0:T(8,128)S(1)}, f32[1,14,14,768]{3,2,1,0:T(8,128)S(1)}) fusion(f32[768]{0:T(1024)S(1)} %get-tuple-element.50, f32[768]{0:T(1024)S(1)} %get-tuple-element.51, f32[768]{0:T(1024)S(1)} %get-tuple-element.4, f32[768]{0:T(1024)S(1)} %get-tuple-element.5, f32[768]{0:T(1024)S(1)} %get-tuple-element.6, f32[768]{0:T(1024)S(1)} %get-tuple-element.7, ...), kind=kLoop, calls=%fused_computation.256 | loop fusion | flops 14902076 | bytes 1358608 | tf_op jit(solution)/shard_map/reduce_sum | solution.py:26
  18.4 0.1 div.15
  18.5 0.2 multiply_reduce_fusion
  18.9 0.1 reshape.212
  19.0 0.1 rsqrt.12
  19.2 8.0 %fusion.7 = (bf16[196,3072]{1,0:T(8,128)(2,1)S(1)}, f32[196,3072]{1,0:T(8,128)S(1)}) fusion(f32[3072]{0:T(1024)S(1)} %copy-done.7, bf16[768,3072]{1,0:T(8,128)(2,1)} %param.19, f32[196,768]{1,0:T(8,128)S(1)} %reshape.211, f32[768]{0:T(1024)S(1)} %copy-done.3, f32[768]{0:T(1024)S(1)} %copy-done.4, f32[196]{0:T(256)S(1)} %rsqrt.12, f32[196]{0:T(256)S(1)} %div.15), kind=kOutput, calls=%fused_computation.60 | convolution fusion | flops 965336064 | bytes 8953376 | tf_op jit(solution)/shard_map/dot_general | solution.py:94
  27.2 2.0 fusion
  29.2 2.4 fusion.15
  31.6 1.4 fusion.17
  33.1 0.2 all-reduce.6.cloned.1.call-start
  33.3 130.9 %all-reduce.8.cloned.1.call-done = (f32[768,32]{0,1:T(8,128)}, f32[3072,32]{0,1:T(8,128)}) async-done(((f32[768,32]{0,1:T(8,128)}, f32[3072,32]{0,1:T(8,128)}), (f32[768,32]{0,1:T(8,128)}, f32[3072,32]{0,1:T(8,128)})) %all-reduce.8.cloned.1.call-update) | async-done | bytes 491536 | tf_op jit(solution)/shard_map/psum | solution.py:69
  164.2 1.3 fusion.128
  165.5 1.6 fusion.129
  167.1 2.9 cholesky.55
  170.1 0.6 compare_reduce_fusion
  170.7 0.7 fusion.121
  171.4 2.4 custom-call.11
  173.8 2.2 convolution_convert_fusion
  176.0 2.3 fusion.16
  178.4 2.9 cholesky.44
  181.3 0.6 compare_reduce_fusion.1
  182.0 0.7 fusion.120
  182.6 2.4 custom-call.10
  185.1 0.8 convolution_convert_fusion.1
  185.9 2.1 fusion.18
  188.1 128.5 %all-reduce.6.cloned.1.call-done = (f32[3072,32]{0,1:T(8,128)}, f32[768,32]{0,1:T(8,128)}) async-done(((f32[3072,32]{0,1:T(8,128)}, f32[768,32]{0,1:T(8,128)}), (f32[3072,32]{0,1:T(8,128)}, f32[768,32]{0,1:T(8,128)})) %all-reduce.6.cloned.1.call-update) | async-done | bytes 491536 | tf_op jit(solution)/shard_map/psum | solution.py:72
  316.6 1.8 broadcast_multiply_fusion
  318.3 1.5 broadcast_multiply_fusion.1
  (34 shorter events, 0.5 us)
Async XLA Ops:
  7.2 157.0 %all-reduce.8.cloned.1.call-start = ((), (), s32[]{:S(2)}) async-start(), calls=%async_computation.1 | async-start | bytes 983040 | tf_op jit(solution)/shard_map/psum | solution.py:69
  9.7 9.2 %copy-start.1 = (bf16[1,14,14,768]{3,2,1,0:T(8,128)(2,1)S(1)}, bf16[1,14,14,768]{3,2,1,0:T(8,128)(2,1)}, u32[]{:S(2)}) copy-start(bf16[1,14,14,768]{3,2,1,0:T(8,128)(2,1)} %param.14) | copy-start | bytes 903172
  12.1 6.9 %copy-start.6 = (f32[768]{0:T(1024)S(1)}, f32[768]{0:T(1024)}, u32[]{:S(2)}) copy-start(f32[768]{0:T(1024)} %param.22) | copy-start | bytes 9220
  12.1 7.0 %copy-start.3 = (f32[768]{0:T(1024)S(1)}, f32[768]{0:T(1024)}, u32[]{:S(2)}) copy-start(f32[768]{0:T(1024)} %param.18) | copy-start | bytes 9220
  12.1 7.0 %copy-start.4 = (f32[768]{0:T(1024)S(1)}, f32[768]{0:T(1024)}, u32[]{:S(2)}) copy-start(f32[768]{0:T(1024)} %param.17) | copy-start | bytes 9220
  12.1 7.0 %copy-start.7 = (f32[3072]{0:T(1024)S(1)}, f32[3072]{0:T(1024)}, u32[]{:S(2)}) copy-start(f32[3072]{0:T(1024)} %param.20) | copy-start | bytes 36868
  19.0 10.2 %copy-start.5 = (f32[196]{0:T(256)}, f32[196]{0:T(256)S(1)}, u32[]{:S(2)}) copy-start(f32[196]{0:T(256)S(1)} %rsqrt.12) | copy-start | bytes 2356
  19.1 8.1 %slice-start = ((s8[4718592]{0:T(1024)(128)(4,1)}), s8[4194304]{0:T(1024)(128)(4,1)S(1)}, s32[]{:S(2)}) async-start(s8[4718592]{0:T(1024)(128)(4,1)} %bitcast.35), calls=%async_computation.2 | async-start | bytes 8388608
  19.1 8.1 %slice-start.1 = ((s8[4718592]{0:T(1024)(128)(4,1)}), s8[524288]{0:T(1024)(128)(4,1)S(1)}, s32[]{:S(2)}) async-start(s8[4718592]{0:T(1024)(128)(4,1)} %bitcast.35), calls=%async_computation.3 | async-start | bytes 1048576
  27.2 4.4 %copy-start.2 = (f32[768,32]{0,1:T(8,128)S(1)}, f32[768,32]{0,1:T(8,128)}, u32[]{:S(2)}) copy-start(f32[768,32]{0,1:T(8,128)} %param.24) | copy-start | bytes 294916
  33.1 283.5 %all-reduce.6.cloned.1.call-start = ((), (), s32[]{:S(2)}) async-start(), calls=%async_computation | async-start | bytes 983040 | tf_op jit(solution)/shard_map/psum | solution.py:72
  164.2 20.9 %copy-start = (f32[768,32]{0,1:T(8,128)S(1)}, f32[768,32]{0,1:T(8,128)}, u32[]{:S(2)}) copy-start(f32[768,32]{0,1:T(8,128)} %get-tuple-element.54) | copy-start | bytes 294916
Sparse Core Ops, SparseCore 0:
  33.2 130.9 all-reduce.7
  188.2 128.3 all-reduce.5
where the time goes:
time: 327 us
  waiting for transfers between devices  259 us (79%)
  other arithmetic  24.2 us (7%)
  matrix products  24.1 us (7%)
  between operations  14.3 us (4%)
  local copies, waits for them, and re-layouts  4.39 us (1%)
    psum x1, waiting for transfers between devices, refine_layer(): summed = lax.psum(partial_value, ('outer', 'inner'))  131 us
    psum x1, waiting for transfers between devices, refine_layer(): return lax.psum(term, ('outer', 'inner')) * scale  129 us
    dot_general x1, matrix products, shards(): jnp.dot(normed, expand_weight, preferred_element_type=jnp.float32)  8.02 us
    another operation x6, other arithmetic, apply_factor(): factor = jnp.linalg.cholesky(gram_matrix)  7.19 us
  transfers between devices with their start and end apart: 2, of which 2 were waited for; matrix products, arithmetic and copies ran while one was open for 0% of the time, Pallas kernels for 0%

commit v1 on v0

--- a/solution.py
+++ b/solution.py
@@ -65,11 +65,89 @@
     return jax.scipy.linalg.solve_triangular(factor, partial_value.T, lower=True).T
 
 
-def refine_layer(partial_value, rows_left, rows_right, scale):
-    summed = lax.psum(partial_value, ("outer", "inner"))
-    basis = apply_factor(gram_of(summed), summed)
-    term = back_project(rows_left, rows_right, basis)
-    return lax.psum(term, ("outer", "inner")) * scale
+def digits(size):
+    found = []
+    factor = 2
+    while size > 1:
+        while size % factor == 0:
+            found.append(factor)
+            size //= factor
+        factor += 1
+    return found
+
+
+def plan(n_outer, n_inner):
+    steps = []
+    stride = 1
+    for size in (n_inner, n_outer):
+        for radix in digits(size):
+            steps.append((stride, radix))
+            stride *= radix
+    return steps
+
+
+def linear_index():
+    return lax.axis_index("outer") * lax.axis_size("inner") + lax.axis_index("inner")
+
+
+def shifted(value, count, stride, radix, amount):
+    perm = []
+    for source in range(count):
+        digit = (source // stride) % radix
+        target = source + ((digit + amount) % radix - digit) * stride
+        perm.append((source, target))
+    return lax.ppermute(value, ("outer", "inner"), perm)
+
+
+def step_sum(value, count, stride, radix, mirror):
+    sent = value.astype(jnp.bfloat16)
+    if radix == 2:
+        mask = stride | mirror
+        perm = [(source, source ^ mask) for source in range(count)]
+        got = lax.ppermute(sent, ("outer", "inner"), perm)
+        return sent.astype(jnp.float32) + got.astype(jnp.float32)
+    mine = (linear_index() // stride) % radix
+    parts = jnp.stack([sent] + [shifted(sent, count, stride, radix, k) for k in range(1, radix)])
+    total = jnp.zeros(value.shape, jnp.float32)
+    for owner in range(radix):
+        total = total + parts[(mine - owner) % radix].astype(jnp.float32)
+    return total
+
+
+def exchange_sum(stacked):
+    n_outer, n_inner = lax.axis_size("outer"), lax.axis_size("inner")
+    count = n_outer * n_inner
+    steps = plan(n_outer, n_inner)
+    paired = bool(steps) and steps[0][1] == 2 and stacked.shape[0] % 32 == 0
+    value = stacked
+    if paired:
+        half = stacked.shape[0] // 2
+        mine = linear_index() % 2
+        pair = [(source, source ^ 1) for source in range(count)]
+        sent = stacked.astype(jnp.bfloat16)
+        keep = lax.dynamic_slice_in_dim(sent, mine * half, half, 0)
+        give = lax.dynamic_slice_in_dim(sent, (1 - mine) * half, half, 0)
+        got = lax.ppermute(give, ("outer", "inner"), pair)
+        value = keep.astype(jnp.float32) + got.astype(jnp.float32)
+        steps = steps[1:]
+    for place, (stride, radix) in enumerate(steps):
+        before = steps[place - 1] if place else None
+        last = place == len(steps) - 1 and radix == 2 and before is not None
+        mirror = before[0] if last and before[1] == 2 and stride > n_inner else 0
+        value = step_sum(value, count, stride, radix, mirror)
+    value = value.astype(jnp.bfloat16)
+    if paired:
+        other = lax.ppermute(value, ("outer", "inner"), pair)
+        low = jnp.where(mine == 0, value, other)
+        high = jnp.where(mine == 0, other, value)
+        value = jnp.concatenate([low, high], axis=0)
+    return value.astype(jnp.float32)
+
+
+def sum_layers(first, second):
+    total = exchange_sum(jnp.concatenate([first.T, second.T], axis=1))
+    cut = first.shape[0]
+    return total[:, :cut].T, total[:, cut:].T
 
 
 def shards(
@@ -102,9 +180,13 @@
     )
     hid_grad = (back * gelu_slope(hidden)).astype(jnp.bfloat16)
     p_first = project(normed, hid_grad, right_first)
-    next_second = refine_layer(p_second, activated, out_grad, scale)
-    next_first = refine_layer(p_first, normed, hid_grad, scale)
-    return (next_first, next_second)
+    p_first, p_second = sum_layers(p_first, p_second)
+    basis_first = apply_factor(gram_of(p_first), p_first)
+    basis_second = apply_factor(gram_of(p_second), p_second)
+    term_first = back_project(normed, hid_grad, basis_first)
+    term_second = back_project(activated, out_grad, basis_second)
+    next_first, next_second = sum_layers(term_first, term_second)
+    return (next_first * scale, next_second * scale)
 
 
 def solution(mesh):

time: 327 us -> 111 us (0.34)
  waiting for transfers between devices: 259 us -> 31 us
  starting transfers between devices: 0.26 us -> 20 us
  between operations: 14.3 us -> 1.05 us
  other arithmetic: 24.2 us -> 32.2 us
  matrix products: 24.1 us -> 19.5 us
    psum x2 -> x0, waiting for transfers between devices: 259 us -> none  [the longest x1 131 us: refine_layer(): summed = lax.psum(partial_value, ('outer', 'inner'))]
    ppermute x0 -> x12, waiting for transfers between devices: none -> 31 us  [the longest x8 26.3 us: step_sum(): got = lax.ppermute(sent, ('outer', 'inner'), perm)]
    ppermute x0 -> x12, starting transfers between devices: none -> 20 us  [the longest x8 19.1 us: step_sum(): got = lax.ppermute(sent, ('outer', 'inner'), perm)]
    another operation x4 -> x5, other arithmetic: 6.17 us -> 8.85 us  [apply_factor(): jax.scipy.linalg.solve_triangular(factor, partial_value.T, lower=True)]
  transfers between devices with their start and end apart: 2 -> 12, of which waited for: 2 -> 12; matrix products, arithmetic and copies ran while one was open for 0% -> 0% of each run, Pallas kernels for 0% -> 0%
where the time goes in v1:
time: 111 us; the launch traced here: 110 us
  other arithmetic  32.2 us (29%)
  waiting for transfers between devices  31 us (28%)
  starting transfers between devices  20 us (18%)
  matrix products  19.5 us (18%)
  local copies, waits for them, and re-layouts  6.28 us (6%)
    ppermute x8, waiting for transfers between devices, step_sum(): got = lax.ppermute(sent, ('outer', 'inner'), perm)  26.3 us
    ppermute x8, starting transfers between devices, step_sum(): got = lax.ppermute(sent, ('outer', 'inner'), perm)  19.1 us
    another operation x6, other arithmetic, apply_factor(): factor = jnp.linalg.cholesky(gram_matrix)  9.22 us
    another operation x5, other arithmetic, apply_factor(): jax.scipy.linalg.solve_triangular(factor, partial_value.T, lower=True)  8.85 us
    dot_general x1, matrix products, shards(): jnp.dot(normed, expand_weight, preferred_element_type=jnp.float32)  8.02 us
    reduce_sum x1, other arithmetic, layer_norm(): center = jnp.mean(values, axis=-1, keepdims=True)  6.23 us
    slice x3, local copies, waits for them, and re-layouts, depthwise(): conv_weight[tap_row, tap_col]  3.83 us
    dot_general x2, matrix products, project(): lax.dot_general(rows_left, thin, (((0,), (0,)), ((), ())), preferred_elem...  3.12 us
  transfers between devices with their start and end apart: 12, of which 12 were waited for; matrix products, arithmetic and copies ran while one was open for 0% of the time, Pallas kernels for 0%

profile of v1, /device:TPU:0, one launch (start us, length us, event | category | flops | bytes accessed | tf_op | source)
XLA Modules:
  0.0 109.9 jit_solution(3247917899803509002)
XLA Ops:
  0.6 1.4 %slice_reduce_fusion.48 = (f32[768]{0:T(1024)S(1)}, f32[768]{0:T(1024)S(1)}, f32[768]{0:T(1024)S(1)}, f32[768]{0:T(1024)S(1)}, f32[768]{0:T(1024)S(1)}, /*index=...) fusion(f32[7,7,768]{2,1,0:T(8,128)} %param.15), kind=kLoop, calls=%fused_computation.285 | loop fusion | bytes 116736 | tf_op jit(solution)/shard_map/slice | solution.py:20
  2.0 1.4 %slice_reduce_fusion.47 = (f32[768]{0:T(1024)S(1)}, f32[768]{0:T(1024)S(1)}, f32[768]{0:T(1024)S(1)}, f32[768]{0:T(1024)S(1)}, f32[768]{0:T(1024)S(1)}, /*index=...) fusion(f32[7,7,768]{2,1,0:T(8,128)} %param.15), kind=kLoop, calls=%fused_computation.284 | loop fusion | bytes 116736 | tf_op jit(solution)/shard_map/slice | solution.py:20
  5.6 6.2 %fusion.131 = (f32[14,14]{1,0:T(8,128)S(1)}, f32[1,14,14,768]{3,2,1,0:T(8,128)S(1)}) fusion(f32[768]{0:T(1024)S(1)} %get-tuple-element.50, f32[768]{0:T(1024)S(1)} %get-tuple-element.51, f32[768]{0:T(1024)S(1)} %get-tuple-element.4, f32[768]{0:T(1024)S(1)} %get-tuple-element.5, f32[768]{0:T(1024)S(1)} %get-tuple-element.6, f32[768]{0:T(1024)S(1)} %get-tuple-element.7, ...), kind=kLoop, calls=%fused_computation.290 | loop fusion | flops 14902076 | bytes 1358608 | tf_op jit(solution)/shard_map/reduce_sum | solution.py:26
  12.6 8.0 %fusion.7 = (bf16[196,3072]{1,0:T(8,128)(2,1)S(1)}, f32[196,3072]{1,0:T(8,128)S(1)}) fusion(f32[3072]{0:T(1024)S(1)} %copy-done.9, bf16[768,3072]{1,0:T(8,128)(2,1)} %param.19, f32[196,768]{1,0:T(8,128)S(1)} %reshape.211, f32[768]{0:T(1024)S(1)} %copy-done.4, f32[768]{0:T(1024)S(1)} %copy-done.5, f32[196]{0:T(256)S(1)} %rsqrt.12, f32[196]{0:T(256)S(1)} %div.15), kind=kOutput, calls=%fused_computation.62 | convolution fusion | flops 965336064 | bytes 8953376 | tf_op jit(solution)/shard_map/dot_general | solution.py:172
  20.6 2.0 %fusion = bf16[196,3072]{1,0:T(8,128)(2,1)S(1)} fusion(bf16[196,768]{1,0:T(8,128)(2,1)S(1)} %multiply_convert_fusion, bf16[3072,768]{1,0:T(8,128)(2,1)S(1)} %bitcast.37, f32[196,3072]{1,0:T(8,128)S(1)} %get-tuple-element.59), kind=kOutput, calls=%fused_computation.50 | convolution fusion | flops 930865152 | bytes 8632320 | tf_op jit(solution)/shard_map/dot_general | solution.py:178
  22.7 1.7 %convolution_convert_fusion.9 = bf16[32,768]{1,0:T(8,128)(2,1)S(1)} fusion(bf16[196,3072]{1,0:T(8,128)(2,1)S(1)} %fusion, f32[3072,32]{0,1:T(8,128)} %param.23, f32[196,768]{1,0:T(8,128)S(1)} %reshape.211, f32[768]{0:T(1024)S(1)} %copy-done.4, f32[768]{0:T(1024)S(1)} %copy-done.5, f32[196]{0:T(256)S(1)} %rsqrt.12, f32[196]{0:T(256)S(1)} %div.15), kind=kOutput, calls=%fused_computation.84 | convolution fusion | flops 49050752 | bytes 2256416 | tf_op jit(solution)/shard_map/dot_general | solution.py:44
  24.4 1.4 %convolution_convert_fusion.2 = bf16[32,3072]{1,0:T(8,128)(2,1)} fusion(bf16[196,3072]{1,0:T(8,128)(2,1)S(1)} %get-tuple-element.58, bf16[196,768]{1,0:T(8,128)(2,1)S(1)} %multiply_convert_fusion, f32[768,32]{0,1:T(8,128)S(1)} %copy-done.3), kind=kOutput, calls=%fused_computation.55 | convolution fusion | flops 48298112 | bytes 1800192 | tf_op jit(solution)/shard_map/dot_general | solution.py:44
  25.8 1.5 %fusion.117 = bf16[16,3840]{1,0:T(8,128)(2,1)} fusion(s32[]{:T(128)S(6)} %select_n.43, bf16[32,3072]{1,0:T(8,128)(2,1)} %convolution_convert_fusion.2, bf16[32,768]{1,0:T(8,128)(2,1)S(1)} %convolution_convert_fusion.9), kind=kLoop, calls=%fused_computation.210 | loop fusion | flops 245760 | bytes 368644 | tf_op jit(solution)/shard_map/concatenate | solution.py:148
  30.0 2.9 %collective-permute-start.1 = (bf16[16,3840]{1,0:T(8,128)(2,1)S(1)}, bf16[16,3840]{1,0:T(8,128)(2,1)S(1)}, u32[]{:S(2)}, u32[]{:S(2)}) collective-permute-start(bf16[16,3840]{1,0:T(8,128)(2,1)S(1)} %add_convert_fusion.10), channel_id=1, source_target_pairs={{0,2},{1,3},{2,0},{3,1},{4,6},{5,7},{6,4},{7,5},{8,10},{9,11},{10,... | collective-permute-start | bytes 368648 | tf_op jit(solution)/shard_map/ppermute | solution.py:107
  32.9 3.6 %collective-permute-done.1 = bf16[16,3840]{1,0:T(8,128)(2,1)S(1)} collective-permute-done((bf16[16,3840]{1,0:T(8,128)(2,1)S(1)}, bf16[16,3840]{1,0:T(8,128)(2,1)S(1)}, u32[]{:S(2)}, u32[]{:S(2)}) %collective-permute-start.1) | collective-permute-done | bytes 122912 | tf_op jit(solution)/shard_map/ppermute | solution.py:107
  36.6 1.8 %collective-permute-start.2 = (bf16[16,3840]{1,0:T(8,128)(2,1)S(1)}, bf16[16,3840]{1,0:T(8,128)(2,1)S(1)}, u32[]{:S(2)}, u32[]{:S(2)}) collective-permute-start(bf16[16,3840]{1,0:T(8,128)(2,1)S(1)} %add_convert_fusion.9), channel_id=1, source_target_pairs={{0,4},{1,5},{2,6},{3,7},{4,0},{5,1},{6,2},{7,3},{8,12},{9,13},{10,... | collective-permute-start | bytes 368648 | tf_op jit(solution)/shard_map/ppermute | solution.py:107
  38.3 3.2 %collective-permute-done.2 = bf16[16,3840]{1,0:T(8,128)(2,1)S(1)} collective-permute-done((bf16[16,3840]{1,0:T(8,128)(2,1)S(1)}, bf16[16,3840]{1,0:T(8,128)(2,1)S(1)}, u32[]{:S(2)}, u32[]{:S(2)}) %collective-permute-start.2) | collective-permute-done | bytes 122912 | tf_op jit(solution)/shard_map/ppermute | solution.py:107
  41.5 1.9 %collective-permute-start.3 = (bf16[16,3840]{1,0:T(8,128)(2,1)S(1)}, bf16[16,3840]{1,0:T(8,128)(2,1)S(1)}, u32[]{:S(2)}, u32[]{:S(2)}) collective-permute-start(bf16[16,3840]{1,0:T(8,128)(2,1)S(1)} %add_convert_fusion.8), channel_id=1, source_target_pairs={{0,8},{1,9},{2,10},{3,11},{4,12},{5,13},{6,14},{7,15},{8,0},{9,1},... | collective-permute-start | bytes 368648 | tf_op jit(solution)/shard_map/ppermute | solution.py:107
  43.4 3.1 %collective-permute-done.3 = bf16[16,3840]{1,0:T(8,128)(2,1)S(1)} collective-permute-done((bf16[16,3840]{1,0:T(8,128)(2,1)S(1)}, bf16[16,3840]{1,0:T(8,128)(2,1)S(1)}, u32[]{:S(2)}, u32[]{:S(2)}) %collective-permute-start.3) | collective-permute-done | bytes 122912 | tf_op jit(solution)/shard_map/ppermute | solution.py:107
  46.5 3.9 %collective-permute-start.4 = (bf16[16,3840]{1,0:T(8,128)(2,1)S(1)}, bf16[16,3840]{1,0:T(8,128)(2,1)S(1)}, u32[]{:S(2)}, u32[]{:S(2)}) collective-permute-start(bf16[16,3840]{1,0:T(8,128)(2,1)S(1)} %add_convert_fusion.7), channel_id=1, source_target_pairs={{0,24},{1,25},{2,26},{3,27},{4,28},{5,29},{6,30},{7,31},{8,16},{9,... | collective-permute-start | bytes 368648 | tf_op jit(solution)/shard_map/ppermute | solution.py:107
  50.4 3.0 %collective-permute-done.4 = bf16[16,3840]{1,0:T(8,128)(2,1)S(1)} collective-permute-done((bf16[16,3840]{1,0:T(8,128)(2,1)S(1)}, bf16[16,3840]{1,0:T(8,128)(2,1)S(1)}, u32[]{:S(2)}, u32[]{:S(2)}) %collective-permute-start.4) | collective-permute-done | bytes 122912 | tf_op jit(solution)/shard_map/ppermute | solution.py:107
  56.8 1.4 %copy.17 = f32[32,32]{0,1:T(8,128)} copy(f32[32,32]{1,0:T(8,128)} %fusion.119) | data formatting | bytes 8192 | tf_op jit(solution)/shard_map/dot_general | solution.py:58
  59.5 4.2 %cholesky.55 = f32[32,32]{1,0:T(8,128)} custom-call(f32[32,32]{1,0:T(8,128)} %fusion.126), custom_call_target="Cholesky" | custom-call | tf_op jit(solution)/shard_map/jit(cholesky)/cholesky | solution.py:64
  65.1 2.0 %fusion.124 = f32[1,32,32]{2,1,0:T(8,128)} fusion(f32[32,32]{1,0:T(8,128)} %cholesky.55, pred[]{:T(512)} %compare_reduce_fusion), kind=kLoop, calls=%fused_computation.224 | loop fusion | flops 4096 | bytes 8193 | tf_op jit(solution)/shard_map/jit(_solve_triangular)/triangular_solve | solution.py:65
  67.1 3.8 %custom-call.11 = f32[1,32,32]{1,2,0:T(8,128)} custom-call(f32[1,32,32]{2,1,0:T(8,128)} %fusion.124), custom_call_target="InvertDiagBlocksLowerTriangular" | custom-call | tf_op jit(solution)/shard_map/jit(_solve_triangular)/triangular_solve | solution.py:65
  70.9 1.9 %convolution_convert_fusion = bf16[3072,32]{0,1:T(8,128)(2,1)} fusion(bf16[16,3840]{1,0:T(8,128)(2,1)} %copy-done, bf16[16,3840]{1,0:T(8,128)(2,1)S(1)} %get-tuple-element.56, f32[1,32,32]{1,2,0:T(8,128)} %custom-call.11), kind=kOutput, calls=%fused_computation.53 | convolution fusion | flops 38240256 | bytes 446464 | tf_op jit(solution)/shard_map/jit(_solve_triangular)/triangular_solve | solution.py:65
  72.8 1.6 %convolution_convert_fusion.8 = bf16[32,768]{1,0:T(8,128)(2,1)S(1)} fusion(bf16[196,768]{1,0:T(8,128)(2,1)S(1)} %multiply_convert_fusion, bf16[196,3072]{1,0:T(8,128)(2,1)S(1)} %get-tuple-element.58, bf16[3072,32]{0,1:T(8,128)(2,1)} %convolution_convert_fusion), kind=kOutput, calls=%fused_computation.83 | convolution fusion | flops 48199808 | bytes 1751040 | tf_op jit(solution)/shard_map/dot_general | solution.py:52
  74.7 2.9 %cholesky.44 = f32[32,32]{1,0:T(8,128)S(1)} custom-call(f32[32,32]{1,0:T(8,128)S(1)} %fusion.128), custom_call_target="Cholesky" | custom-call | tf_op jit(solution)/shard_map/jit(cholesky)/cholesky | solution.py:64
  79.0 2.4 %custom-call.10 = f32[1,32,32]{1,2,0:T(8,128)S(1)} custom-call(f32[1,32,32]{2,1,0:T(8,128)S(1)} %fusion.123), custom_call_target="InvertDiagBlocksLowerTriangular" | custom-call | tf_op jit(solution)/shard_map/jit(_solve_triangular)/triangular_solve | solution.py:65
  81.8 1.5 %convolution_convert_fusion.1 = bf16[32,3072]{1,0:T(8,128)(2,1)S(1)} fusion(bf16[196,3072]{1,0:T(8,128)(2,1)S(1)} %fusion, bf16[768,32]{1,0:T(8,128)(2,1)S(1)} %convolution_convert_fusion.3, f32[196,768]{1,0:T(8,128)S(1)} %reshape.211, f32[768]{0:T(1024)S(1)} %copy-done.4, f32[768]{0:T(1024)} %param.17, f32[196]{0:T(256)} %copy-done.7, f32[196]{0:T(256)} %copy-done.6), kind=kOutput, calls=%fused_computation.54 | convolution fusion | flops 49026176 | bytes 2059808 | tf_op jit(solution)/shard_map/dot_general | solution.py:52
  84.7 1.8 %collective-permute-start.7 = (bf16[16,3840]{1,0:T(8,128)(2,1)S(1)}, bf16[16,3840]{1,0:T(8,128)(2,1)S(1)}, u32[]{:S(2)}, u32[]{:S(2)}) collective-permute-start(bf16[16,3840]{1,0:T(8,128)(2,1)S(1)} %add_convert_fusion.5), channel_id=1, source_target_pairs={{0,2},{1,3},{2,0},{3,1},{4,6},{5,7},{6,4},{7,5},{8,10},{9,11},{10,... | collective-permute-start | bytes 368648 | tf_op jit(solution)/shard_map/ppermute | solution.py:107
  86.5 3.6 %collective-permute-done.7 = bf16[16,3840]{1,0:T(8,128)(2,1)S(1)} collective-permute-done((bf16[16,3840]{1,0:T(8,128)(2,1)S(1)}, bf16[16,3840]{1,0:T(8,128)(2,1)S(1)}, u32[]{:S(2)}, u32[]{:S(2)}) %collective-permute-start.7) | collective-permute-done | bytes 122912 | tf_op jit(solution)/shard_map/ppermute | solution.py:107
  90.2 1.8 %collective-permute-start.8 = (bf16[16,3840]{1,0:T(8,128)(2,1)S(1)}, bf16[16,3840]{1,0:T(8,128)(2,1)S(1)}, u32[]{:S(2)}, u32[]{:S(2)}) collective-permute-start(bf16[16,3840]{1,0:T(8,128)(2,1)S(1)} %add_convert_fusion.4), channel_id=1, source_target_pairs={{0,4},{1,5},{2,6},{3,7},{4,0},{5,1},{6,2},{7,3},{8,12},{9,13},{10,... | collective-permute-start | bytes 368648 | tf_op jit(solution)/shard_map/ppermute | solution.py:107
  92.0 3.2 %collective-permute-done.8 = bf16[16,3840]{1,0:T(8,128)(2,1)S(1)} collective-permute-done((bf16[16,3840]{1,0:T(8,128)(2,1)S(1)}, bf16[16,3840]{1,0:T(8,128)(2,1)S(1)}, u32[]{:S(2)}, u32[]{:S(2)}) %collective-permute-start.8) | collective-permute-done | bytes 122912 | tf_op jit(solution)/shard_map/ppermute | solution.py:107
  96.5 3.6 %collective-permute-done.9 = bf16[16,3840]{1,0:T(8,128)(2,1)S(1)} collective-permute-done((bf16[16,3840]{1,0:T(8,128)(2,1)S(1)}, bf16[16,3840]{1,0:T(8,128)(2,1)S(1)}, u32[]{:S(2)}, u32[]{:S(2)}) %collective-permute-start.9) | collective-permute-done | bytes 122912 | tf_op jit(solution)/shard_map/ppermute | solution.py:107
  100.1 3.8 %collective-permute-start.10 = (bf16[16,3840]{1,0:T(8,128)(2,1)S(1)}, bf16[16,3840]{1,0:T(8,128)(2,1)S(1)}, u32[]{:S(2)}, u32[]{:S(2)}) collective-permute-start(bf16[16,3840]{1,0:T(8,128)(2,1)S(1)} %add_convert_fusion.2), channel_id=1, source_target_pairs={{0,24},{1,25},{2,26},{3,27},{4,28},{5,29},{6,30},{7,31},{8,16},{9,... | collective-permute-start | bytes 368648 | tf_op jit(solution)/shard_map/ppermute | solution.py:107
  103.9 3.1 %collective-permute-done.10 = bf16[16,3840]{1,0:T(8,128)(2,1)S(1)} collective-permute-done((bf16[16,3840]{1,0:T(8,128)(2,1)S(1)}, bf16[16,3840]{1,0:T(8,128)(2,1)S(1)}, u32[]{:S(2)}, u32[]{:S(2)}) %collective-permute-start.10) | collective-permute-done | bytes 122912 | tf_op jit(solution)/shard_map/ppermute | solution.py:107
  (72 shorter events, 19.3 us)
Async XLA Ops:
  3.4 9.0 %copy-start.2 = (bf16[1,14,14,768]{3,2,1,0:T(8,128)(2,1)S(1)}, bf16[1,14,14,768]{3,2,1,0:T(8,128)(2,1)}, u32[]{:S(2)}) copy-start(bf16[1,14,14,768]{3,2,1,0:T(8,128)(2,1)} %param.14) | copy-start | bytes 903172
  5.5 6.9 %copy-start.8 = (f32[768]{0:T(1024)S(1)}, f32[768]{0:T(1024)}, u32[]{:S(2)}) copy-start(f32[768]{0:T(1024)} %param.22) | copy-start | bytes 9220
  5.5 7.0 %copy-start.4 = (f32[768]{0:T(1024)S(1)}, f32[768]{0:T(1024)}, u32[]{:S(2)}) copy-start(f32[768]{0:T(1024)} %param.18) | copy-start | bytes 9220
  5.6 7.0 %copy-start.5 = (f32[768]{0:T(1024)S(1)}, f32[768]{0:T(1024)}, u32[]{:S(2)}) copy-start(f32[768]{0:T(1024)} %param.17) | copy-start | bytes 9220
  5.6 7.0 %copy-start.9 = (f32[3072]{0:T(1024)S(1)}, f32[3072]{0:T(1024)}, u32[]{:S(2)}) copy-start(f32[3072]{0:T(1024)} %param.20) | copy-start | bytes 36868
  12.2 10.4 %copy-start.6 = (f32[196]{0:T(256)}, f32[196]{0:T(256)S(1)}, u32[]{:S(2)}) copy-start(f32[196]{0:T(256)S(1)} %div.15) | copy-start | bytes 2356
  12.4 10.3 %copy-start.7 = (f32[196]{0:T(256)}, f32[196]{0:T(256)S(1)}, u32[]{:S(2)}) copy-start(f32[196]{0:T(256)S(1)} %rsqrt.12) | copy-start | bytes 2356
  12.5 8.1 %slice-start = ((s8[4718592]{0:T(1024)(128)(4,1)}), s8[4194304]{0:T(1024)(128)(4,1)S(1)}, s32[]{:S(2)}) async-start(s8[4718592]{0:T(1024)(128)(4,1)} %bitcast.36), calls=%async_computation | async-start | bytes 8388608
  12.6 8.1 %slice-start.1 = ((s8[4718592]{0:T(1024)(128)(4,1)}), s8[524288]{0:T(1024)(128)(4,1)S(1)}, s32[]{:S(2)}) async-start(s8[4718592]{0:T(1024)(128)(4,1)} %bitcast.36), calls=%async_computation.1 | async-start | bytes 1048576
  20.6 3.7 %copy-start.3 = (f32[768,32]{0,1:T(8,128)S(1)}, f32[768,32]{0,1:T(8,128)}, u32[]{:S(2)}) copy-start(f32[768,32]{0,1:T(8,128)} %param.24) | copy-start | bytes 294916
  27.4 1.7 %collective-permute-start = (bf16[16,3840]{1,0:T(8,128)(2,1)}, bf16[16,3840]{1,0:T(8,128)(2,1)S(1)}, u32[]{:S(2)}, u32[]{:S(2)}) collective-permute-start(bf16[16,3840]{1,0:T(8,128)(2,1)} %fusion.117), channel_id=1, source_target_pairs={{0,1},{1,0},{2,3},{3,2},{4,5},{5,4},{6,7},{7,6},{8,9},{9,8},{10,11... | collective-permute-start | bytes 368648 | tf_op jit(solution)/shard_map/ppermute | solution.py:130
  30.0 6.6 %collective-permute-start.1 = (bf16[16,3840]{1,0:T(8,128)(2,1)S(1)}, bf16[16,3840]{1,0:T(8,128)(2,1)S(1)}, u32[]{:S(2)}, u32[]{:S(2)}) collective-permute-start(bf16[16,3840]{1,0:T(8,128)(2,1)S(1)} %add_convert_fusion.10), channel_id=1, source_target_pairs={{0,2},{1,3},{2,0},{3,1},{4,6},{5,7},{6,4},{7,5},{8,10},{9,11},{10,... | collective-permute-start | bytes 368648 | tf_op jit(solution)/shard_map/ppermute | solution.py:107
  36.6 4.9 %collective-permute-start.2 = (bf16[16,3840]{1,0:T(8,128)(2,1)S(1)}, bf16[16,3840]{1,0:T(8,128)(2,1)S(1)}, u32[]{:S(2)}, u32[]{:S(2)}) collective-permute-start(bf16[16,3840]{1,0:T(8,128)(2,1)S(1)} %add_convert_fusion.9), channel_id=1, source_target_pairs={{0,4},{1,5},{2,6},{3,7},{4,0},{5,1},{6,2},{7,3},{8,12},{9,13},{10,... | collective-permute-start | bytes 368648 | tf_op jit(solution)/shard_map/ppermute | solution.py:107
  41.5 4.9 %collective-permute-start.3 = (bf16[16,3840]{1,0:T(8,128)(2,1)S(1)}, bf16[16,3840]{1,0:T(8,128)(2,1)S(1)}, u32[]{:S(2)}, u32[]{:S(2)}) collective-permute-start(bf16[16,3840]{1,0:T(8,128)(2,1)S(1)} %add_convert_fusion.8), channel_id=1, source_target_pairs={{0,8},{1,9},{2,10},{3,11},{4,12},{5,13},{6,14},{7,15},{8,0},{9,1},... | collective-permute-start | bytes 368648 | tf_op jit(solution)/shard_map/ppermute | solution.py:107
  46.5 6.8 %collective-permute-start.4 = (bf16[16,3840]{1,0:T(8,128)(2,1)S(1)}, bf16[16,3840]{1,0:T(8,128)(2,1)S(1)}, u32[]{:S(2)}, u32[]{:S(2)}) collective-permute-start(bf16[16,3840]{1,0:T(8,128)(2,1)S(1)} %add_convert_fusion.7), channel_id=1, source_target_pairs={{0,24},{1,25},{2,26},{3,27},{4,28},{5,29},{6,30},{7,31},{8,16},{9,... | collective-permute-start | bytes 368648 | tf_op jit(solution)/shard_map/ppermute | solution.py:107
  53.4 0.7 copy-start.1
  53.4 1.5 %collective-permute-start.5 = (bf16[16,3840]{1,0:T(8,128)(2,1)S(1)}, bf16[16,3840]{1,0:T(8,128)(2,1)}, u32[]{:S(2)}, u32[]{:S(2)}) collective-permute-start(bf16[16,3840]{1,0:T(8,128)(2,1)S(1)} %add_convert_fusion.6), channel_id=1, source_target_pairs={{0,1},{1,0},{2,3},{3,2},{4,5},{5,4},{6,7},{7,6},{8,9},{9,8},{10,11... | collective-permute-start | bytes 368648 | tf_op jit(solution)/shard_map/ppermute | solution.py:140
  55.9 0.8 copy-start
  83.3 1.4 %collective-permute-start.6 = (bf16[16,3840]{1,0:T(8,128)(2,1)S(1)}, bf16[16,3840]{1,0:T(8,128)(2,1)S(1)}, u32[]{:S(2)}, u32[]{:S(2)}) collective-permute-start(bf16[16,3840]{1,0:T(8,128)(2,1)S(1)} %fusion.115), channel_id=1, source_target_pairs={{0,1},{1,0},{2,3},{3,2},{4,5},{5,4},{6,7},{7,6},{8,9},{9,8},{10,11... | collective-permute-start | bytes 368648 | tf_op jit(solution)/shard_map/ppermute | solution.py:130
  84.7 5.4 %collective-permute-start.7 = (bf16[16,3840]{1,0:T(8,128)(2,1)S(1)}, bf16[16,3840]{1,0:T(8,128)(2,1)S(1)}, u32[]{:S(2)}, u32[]{:S(2)}) collective-permute-start(bf16[16,3840]{1,0:T(8,128)(2,1)S(1)} %add_convert_fusion.5), channel_id=1, source_target_pairs={{0,2},{1,3},{2,0},{3,1},{4,6},{5,7},{6,4},{7,5},{8,10},{9,11},{10,... | collective-permute-start | bytes 368648 | tf_op jit(solution)/shard_map/ppermute | solution.py:107
  90.2 4.9 %collective-permute-start.8 = (bf16[16,3840]{1,0:T(8,128)(2,1)S(1)}, bf16[16,3840]{1,0:T(8,128)(2,1)S(1)}, u32[]{:S(2)}, u32[]{:S(2)}) collective-permute-start(bf16[16,3840]{1,0:T(8,128)(2,1)S(1)} %add_convert_fusion.4), channel_id=1, source_target_pairs={{0,4},{1,5},{2,6},{3,7},{4,0},{5,1},{6,2},{7,3},{8,12},{9,13},{10,... | collective-permute-start | bytes 368648 | tf_op jit(solution)/shard_map/ppermute | solution.py:107
  95.2 4.9 %collective-permute-start.9 = (bf16[16,3840]{1,0:T(8,128)(2,1)S(1)}, bf16[16,3840]{1,0:T(8,128)(2,1)S(1)}, u32[]{:S(2)}, u32[]{:S(2)}) collective-permute-start(bf16[16,3840]{1,0:T(8,128)(2,1)S(1)} %add_convert_fusion.3), channel_id=1, source_target_pairs={{0,8},{1,9},{2,10},{3,11},{4,12},{5,13},{6,14},{7,15},{8,0},{9,1},... | collective-permute-start | bytes 368648 | tf_op jit(solution)/shard_map/ppermute | solution.py:107
  100.1 6.8 %collective-permute-start.10 = (bf16[16,3840]{1,0:T(8,128)(2,1)S(1)}, bf16[16,3840]{1,0:T(8,128)(2,1)S(1)}, u32[]{:S(2)}, u32[]{:S(2)}) collective-permute-start(bf16[16,3840]{1,0:T(8,128)(2,1)S(1)} %add_convert_fusion.2), channel_id=1, source_target_pairs={{0,24},{1,25},{2,26},{3,27},{4,28},{5,29},{6,30},{7,31},{8,16},{9,... | collective-permute-start | bytes 368648 | tf_op jit(solution)/shard_map/ppermute | solution.py:107
  107.0 1.4 %collective-permute-start.11 = (bf16[16,3840]{1,0:T(8,128)(2,1)S(1)}, bf16[16,3840]{1,0:T(8,128)(2,1)S(1)}, u32[]{:S(2)}, u32[]{:S(2)}) collective-permute-start(bf16[16,3840]{1,0:T(8,128)(2,1)S(1)} %add_convert_fusion.1), channel_id=1, source_target_pairs={{0,1},{1,0},{2,3},{3,2},{4,5},{5,4},{6,7},{7,6},{8,9},{9,8},{10,11... | collective-permute-start | bytes 368648 | tf_op jit(solution)/shard_map/ppermute | solution.py:140

commit v2 on v1

v2 whole, which is shorter than its diff:
```python
import functools

import jax
import jax.numpy as jnp
from jax import lax
from jax.experimental import pallas as pl
from jax.experimental.pallas import tpu as pltpu
from jax.sharding import PartitionSpec as P

LANES = 128
ROW = 16
LEFT = 8
BLOCK = 512


def phase_one(
    mine_ref,
    images_hbm,
    cotangent_hbm,
    taps_hbm,
    conv_bias_ref,
    gain_ref,
    norm_bias_ref,
    expand_hbm,
    expand_bias_ref,
    reduce_hbm,
    layer_scale_ref,
    first_hbm,
    second_hbm,
    keep_ref,
    give_ref,
    normed_ref,
    activated_ref,
    grad_ref,
    hid_ref,
    image,
    cot,
    taps,
    wide,
    conv,
    expand,
    reduce,
    first,
    second,
    low,
    high,
    sems,
):
    extent, channels = images_hbm.shape[1], images_hbm.shape[3]
    kernel = taps_hbm.shape[0]
    margin = kernel // 2
    hidden_units = expand_hbm.shape[1]
    blocks = hidden_units // BLOCK
    slabs = channels // LANES
    half = keep_ref.shape[0]

    def copies():
        yield pltpu.make_async_copy(images_hbm.at[0], image, sems.at[0])
        yield pltpu.make_async_copy(taps_hbm, taps, sems.at[1])
        yield pltpu.make_async_copy(cotangent_hbm.at[0], cot, sems.at[2])
        yield pltpu.make_async_copy(second_hbm, second, sems.at[3])
        for j in range(blocks):
            cut = pl.ds(j * BLOCK, BLOCK)
            yield pltpu.make_async_copy(expand_hbm.at[:, cut], expand.at[:, cut], sems.at[5 + 2 * j])
            yield pltpu.make_async_copy(reduce_hbm.at[cut, :], reduce.at[cut, :], sems.at[6 + 2 * j])
            if j == 0:
                yield pltpu.make_async_copy(first_hbm, first, sems.at[4])

    started = list(copies())
    for copy in started:
        copy.start()
    image_copy, taps_copy, cot_copy, second_copy = started[:4]
    rest = started[4:6] + started[7:]
    first_copy = started[6]

    wide[...] = jnp.zeros(wide.shape, jnp.float32)
    image_copy.wait()
    for row in range(extent):
        for slab in range(slabs):
            piece = image[row, :, slab * LANES : (slab + 1) * LANES].astype(jnp.float32)
            wide[slab, margin + row, LEFT : LEFT + extent, :] = piece
    taps_copy.wait()

    pieces = 2 if extent % 2 == 0 else 1
    tall = extent // pieces
    for slab in range(slabs):
        lanes = slice(slab * LANES, (slab + 1) * LANES)
        for piece in range(pieces):
            top = piece * tall
            total = jnp.broadcast_to(
                conv_bias_ref[:, lanes].reshape(1, 1, LANES), (tall, ROW, LANES)
            )
            for col in range(kernel):
                start = LEFT - margin + col
                seen = wide[slab, top : top + tall + kernel - 1, start : start + ROW, :]
                for row in range(kernel):
                    tap = taps[row, col : col + 1, lanes].reshape(1, 1, LANES)
                    total = total + seen[row : row + tall] * tap
            conv[slab, top * ROW : (top + tall) * ROW, :] = total.reshape(tall * ROW, LANES)

    rows = extent * ROW
    added = conv[0]
    for slab in range(1, slabs):
        added = added + conv[slab]
    center = jnp.sum(added, axis=-1, keepdims=True) * (1.0 / channels)
    added = jnp.zeros((rows, LANES), jnp.float32)
    for slab in range(slabs):
        away = conv[slab] - center
        added = added + away * away
    spread = jnp.sum(added, axis=-1, keepdims=True) * (1.0 / channels)
    inverse = lax.rsqrt(spread + 1e-06)
    place = lax.broadcasted_iota(jnp.int32, (rows, LANES), 0)
    real = lax.rem(place, ROW) < extent
    for slab in range(slabs):
        lanes = slice(slab * LANES, (slab + 1) * LANES)
        value = (conv[slab] - center) * inverse * gain_ref[:, lanes] + norm_bias_ref[:, lanes]
        normed_ref[:, lanes] = jnp.where(real, value, 0.0).astype(jnp.bfloat16)

    cot_copy.wait()
    grad_ref[...] = jnp.zeros(grad_ref.shape, jnp.bfloat16)
    for row in range(extent):
        piece = cot[row].astype(jnp.float32) * layer_scale_ref[...]
        grad_ref[row * ROW : row * ROW + extent, :] = piece.astype(jnp.bfloat16)

    second_copy.wait()
    normed = normed_ref[...]
    grad = grad_ref[...]
    thin = jnp.dot(grad, second[...].astype(jnp.bfloat16), preferred_element_type=jnp.float32)
    thin_second = thin.T.astype(jnp.bfloat16)
    first_copy.wait()
    thin = jnp.zeros((rows, first.shape[1]), jnp.float32)
    for j in range(blocks):
        cut = slice(j * BLOCK, (j + 1) * BLOCK)
        rest[2 * j].wait()
        hidden = jnp.dot(normed, expand[:, cut], preferred_element_type=jnp.float32)
        hidden = hidden + expand_bias_ref[:, cut]
        rest[2 * j + 1].wait()
        back = lax.dot_general(
            grad, reduce[cut, :], (((1,), (1,)), ((), ())), preferred_element_type=jnp.float32
        )
        cdf = 0.5 * (1.0 + lax.erf(hidden * 0.7071067811865476))
        slope = cdf + hidden * jnp.exp(-0.5 * hidden * hidden) * 0.3989422804014327
        activated = (hidden * cdf).astype(jnp.bfloat16)
        hid = (back * slope).astype(jnp.bfloat16)
        activated_ref[:, cut] = activated
        hid_ref[:, cut] = hid
        thin = thin + jnp.dot(
            hid, first[cut, :].astype(jnp.bfloat16), preferred_element_type=jnp.float32
        )
        sums = jnp.dot(thin_second, activated, preferred_element_type=jnp.float32)
        spot = slice(channels + j * BLOCK, channels + (j + 1) * BLOCK)
        low[:, spot] = sums[:half]
        high[:, spot] = sums[half:]
    sums = jnp.dot(thin.T.astype(jnp.bfloat16), normed, preferred_element_type=jnp.float32)
    low[:, :channels] = sums[:half]
    high[:, :channels] = sums[half:]
    mine = mine_ref[0]

    @pl.when(mine == 0)
    def _():
        keep_ref[...] = low[...]
        give_ref[...] = high[...].astype(jnp.bfloat16)

    @pl.when(mine != 0)
    def _():
        keep_ref[...] = high[...]
        give_ref[...] = low[...].astype(jnp.bfloat16)


def eliminate(gram_matrix, size):
    wide = 2 * size
    spot = lax.broadcasted_iota(jnp.int32, (size, size), 0)
    across = lax.broadcasted_iota(jnp.int32, (size, size), 1)
    eye = jnp.where(spot == across, 1.0, 0.0).astype(jnp.float32)
    work = jnp.concatenate([gram_matrix, eye], axis=1)
    down = lax.broadcasted_iota(jnp.int32, (size, wide), 0)
    group = 4
    for base in range(0, size, group):
        cols = [
            jnp.broadcast_to(work[:, base + b : base + b + 1], (size, wide)) for b in range(group)
        ]
        rows = [work[base + b : base + b + 1, :] for b in range(group)]
        for b in range(group):
            scale = lax.rsqrt(cols[b][base + b : base + b + 1, :])
            rows[b] = rows[b] * scale
            cols[b] = cols[b] * scale
            for c in range(b + 1, group):
                factor = cols[b][base + c : base + c + 1, :]
                rows[c] = rows[c] - factor * rows[b]
                cols[c] = cols[c] - cols[b] * factor
        change = jnp.zeros((size, wide), jnp.float32)
        for b in range(group):
            change = change + cols[b] * rows[b]
        work = jnp.where(down >= base + group, work - change, work)
        for b in range(group):
            work = jnp.where(down == base + b, rows[b], work)
    return work[:, size:]


def phase_two(
    mine_ref, value_ref, other_ref, normed_ref, activated_ref, grad_ref, hid_ref, keep_ref, give_ref
):
    channels = normed_ref.shape[1]
    half = value_ref.shape[0]
    mine = mine_ref[0]
    value = value_ref[...]
    other = other_ref[...]
    low = jnp.where(mine == 0, value, other)
    high = jnp.where(mine == 0, other, value)
    both = jnp.concatenate([low, high], axis=0)
    nt = (((1,), (1,)), ((), ()))
    bases = []
    for part in (both[:, :channels], both[:, channels:]):
        gram_matrix = lax.dot_general(part, part, nt, preferred_element_type=jnp.float32)
        inverse = eliminate(gram_matrix, 2 * half)
        coarse = inverse.astype(jnp.bfloat16)
        fine = (inverse - coarse.astype(jnp.float32)).astype(jnp.bfloat16)
        basis = jnp.dot(coarse, part, preferred_element_type=jnp.float32)
        basis = basis + jnp.dot(fine, part, preferred_element_type=jnp.float32)
        bases.append(basis.astype(jnp.bfloat16))
    thin = lax.dot_general(bases[0], normed_ref[...], nt, preferred_element_type=jnp.float32)
    first = jnp.dot(thin.astype(jnp.bfloat16), hid_ref[...], preferred_element_type=jnp.float32)
    thin = lax.dot_general(bases[1], activated_ref[...], nt, preferred_element_type=jnp.float32)
    second = jnp.dot(thin.astype(jnp.bfloat16), grad_ref[...], preferred_element_type=jnp.float32)
    for piece, spot in ((second, slice(0, channels)), (first, slice(channels, None))):
        keep_ref[:, spot] = jnp.where(mine == 0, piece[:half], piece[half:])
        give_ref[:, spot] = jnp.where(mine == 0, piece[half:], piece[:half]).astype(jnp.bfloat16)


def digits(size):
    found = []
    factor = 2
    while size > 1:
        while size % factor == 0:
            found.append(factor)
            size //= factor
        factor += 1
    return found


def plan(n_outer, n_inner):
    steps = []
    stride = 1
    for size in (n_inner, n_outer):
        for radix in digits(size):
            steps.append((stride, radix))
            stride *= radix
    return steps


def linear_index():
    return lax.axis_index("outer") * lax.axis_size("inner") + lax.axis_index("inner")


def shifted(value, count, stride, radix, amount):
    perm = []
    for source in range(count):
        digit = (source // stride) % radix
        target = source + ((digit + amount) % radix - digit) * stride
        perm.append((source, target))
    return lax.ppermute(value, ("outer", "inner"), perm)


def step_sum(value, count, stride, radix, mirror):
    sent = value.astype(jnp.bfloat16)
    if radix == 2:
        mask = stride | mirror
        perm = [(source, source ^ mask) for source in range(count)]
        got = lax.ppermute(sent, ("outer", "inner"), perm)
        return sent.astype(jnp.float32) + got.astype(jnp.float32)
    mine = (linear_index() // stride) % radix
    parts = jnp.stack([sent] + [shifted(sent, count, stride, radix, k) for k in range(1, radix)])
    total = jnp.zeros(value.shape, jnp.float32)
    for owner in range(radix):
        total = total + parts[(mine - owner) % radix].astype(jnp.float32)
    return total


def pair_perm(count):
    return [(source, source ^ 1) for source in range(count)]


def exchange(keep, give, mine):
    n_outer, n_inner = lax.axis_size("outer"), lax.axis_size("inner")
    count = n_outer * n_inner
    steps = plan(n_outer, n_inner)[1:]
    got = lax.ppermute(give, ("outer", "inner"), pair_perm(count))
    value = keep + got.astype(jnp.float32)
    for place, (stride, radix) in enumerate(steps):
        before = steps[place - 1] if place else None
        last = place == len(steps) - 1 and radix == 2 and before is not None
        mirror = before[0] if last and before[1] == 2 and stride > n_inner else 0
        value = step_sum(value, count, stride, radix, mirror)
    value = value.astype(jnp.bfloat16)
    other = lax.ppermute(value, ("outer", "inner"), pair_perm(count))
    return value, other


VMEM = pl.BlockSpec(memory_space=pltpu.VMEM)
ANY = pl.BlockSpec(memory_space=pl.ANY)
SMEM = pl.BlockSpec(memory_space=pltpu.SMEM)


def shards(
    images,
    cotangent,
    conv_weight,
    conv_bias,
    norm_gain,
    norm_bias,
    expand_weight,
    expand_bias,
    reduce_weight,
    layer_scale,
    right_first,
    right_second,
):
    count = lax.axis_size("outer") * lax.axis_size("inner")
    scale = jnp.float32(1.0) / count
    extent, width = images.shape[1], images.shape[3]
    kernel = conv_weight.shape[0]
    hidden_units = expand_weight.shape[1]
    rank = right_first.shape[1]
    rows, half, total = extent * ROW, rank // 2, width + hidden_units
    slabs = width // LANES
    bf16, f32 = jnp.bfloat16, jnp.float32
    mine = (linear_index() % 2).astype(jnp.int32).reshape(1)
    keep, give, normed, activated, grad, hid = pl.pallas_call(
        phase_one,
        out_shape=(
            jax.ShapeDtypeStruct((half, total), f32),
            jax.ShapeDtypeStruct((half, total), bf16),
            jax.ShapeDtypeStruct((rows, width), bf16),
            jax.ShapeDtypeStruct((rows, hidden_units), bf16),
            jax.ShapeDtypeStruct((rows, width), bf16),
            jax.ShapeDtypeStruct((rows, hidden_units), bf16),
        ),
        in_specs=[SMEM, ANY, ANY, ANY, VMEM, VMEM, VMEM, ANY, VMEM, ANY, VMEM, ANY, ANY],
        out_specs=(VMEM,) * 6,
        scratch_shapes=[
            pltpu.VMEM(images.shape[1:], bf16),
            pltpu.VMEM(images.shape[1:], bf16),
            pltpu.VMEM(conv_weight.shape, f32),
            pltpu.VMEM((slabs, extent + kernel - 1, 2 * ROW, LANES), f32),
            pltpu.VMEM((slabs, rows, LANES), f32),
            pltpu.VMEM(expand_weight.shape, bf16),
            pltpu.VMEM(reduce_weight.shape, bf16),
            pltpu.VMEM(right_first.shape, f32),
            pltpu.VMEM(right_second.shape, f32),
            pltpu.VMEM((half, total), f32),
            pltpu.VMEM((half, total), f32),
            pltpu.SemaphoreType.DMA((5 + 2 * (hidden_units // BLOCK),)),
        ],
        compiler_params=pltpu.CompilerParams(vmem_limit_bytes=40 * 1024 * 1024),
        name="phase_one",
    )(
        mine,
        images,
        cotangent,
        conv_weight,
        conv_bias.reshape(1, -1),
        norm_gain.reshape(1, -1),
        norm_bias.reshape(1, -1),
        expand_weight,
        expand_bias.reshape(1, -1),
        reduce_weight,
        layer_scale.reshape(1, -1),
        right_first,
        right_second,
    )
    value, other = exchange(keep, give, mine)
    keep, give = pl.pallas_call(
        phase_two,
        out_shape=(
            jax.ShapeDtypeStruct((half, total), f32),
            jax.ShapeDtypeStruct((half, total), bf16),
        ),
        in_specs=[SMEM] + [VMEM] * 6,
        out_specs=(VMEM, VMEM),
        compiler_params=pltpu.CompilerParams(vmem_limit_bytes=40 * 1024 * 1024),
        name="phase_two",
    )(mine, value, other, normed, activated, grad, hid)
    value, other = exchange(keep, give, mine)
    low = jnp.where(mine[0] == 0, value, other)
    high = jnp.where(mine[0] == 0, other, value)
    both = jnp.concatenate([low, high], axis=0).astype(f32) * scale
    return (both[:, width:].T, both[:, :width].T)


def solution(mesh):
    in_specs = (
        P(("outer", "inner"), None, None, None),
        P(("outer", "inner"), None, None, None),
        P(),
        P(),
        P(),
        P(),
        P(),
        P(),
        P(),
        P(),
        P(),
        P(),
    )
    out_specs = (P(), P())
    return jax.shard_map(shards, mesh=mesh, in_specs=in_specs, out_specs=out_specs, check_vma=False)
```

time: 111 us -> 74.6 us (0.67)
  other arithmetic: 32.2 us -> 0.38 us
  matrix products: 19.5 us -> 0 us
  Pallas kernels: 0 us -> 16.5 us
    another operation x11 -> x0, other arithmetic: 18.1 us -> none  [the longest x6 9.22 us: apply_factor(): factor = jnp.linalg.cholesky(gram_matrix)]
    dot_general x8 -> x0, matrix products: 17.1 us -> none  [the longest x1 8.02 us: shards(): jnp.dot(normed, expand_weight, preferred_element_type=jnp.float32)]
    pallas_call x0 -> x2, Pallas kernels: none -> 16.5 us  [the longest x1 13.8 us: shards(): pl.pallas_call(phase_one, out_shape=(jax.ShapeDtypeStruct((half, total),...]
    reduce_sum x2 -> x0, other arithmetic: 6.45 us -> none  [the longest x1 6.23 us: layer_norm(): center = jnp.mean(values, axis=-1, keepdims=True)]
    slice x3 -> x0, local copies, waits for them, and re-layouts: 3.83 us -> none  [depthwise(): conv_weight[tap_row, tap_col]]
    unnamed x24 -> x22, local copies, waits for them, and re-layouts: 0.62 us -> 4.08 us
    another operation x2 -> x0, matrix products: 2.34 us -> none  [apply_factor(): jax.scipy.linalg.solve_triangular(factor, partial_value.T, lower=True)]
    concatenate x2 -> x0, other arithmetic: 1.55 us -> none  [sum_layers(): total = exchange_sum(jnp.concatenate([first.T, second.T], axis=1))]
where the time goes in v2:
time: 74.6 us; the launch traced here: 74.5 us
  waiting for transfers between devices  31.1 us (42%)
  starting transfers between devices  20.1 us (27%)
  Pallas kernels  16.5 us (22%)
  local copies, waits for them, and re-layouts  5.51 us (7%)
  between operations  0.93 us (1%)
    ppermute x8, waiting for transfers between devices, step_sum(): got = lax.ppermute(sent, ('outer', 'inner'), perm)  26.3 us
    ppermute x8, starting transfers between devices, step_sum(): got = lax.ppermute(sent, ('outer', 'inner'), perm)  19.1 us
    pallas_call x1, Pallas kernels, shards(): pl.pallas_call(phase_one, out_shape=(jax.ShapeDtypeStruct((half, total),...  13.8 us
    unnamed x22, local copies, waits for them, and re-layouts  4.08 us
    ppermute x2, waiting for transfers between devices, exchange(): other = lax.ppermute(value, ('outer', 'inner'), pair_perm(count))  2.64 us
    pallas_call x1, Pallas kernels, shards(): pl.pallas_call(phase_two, out_shape=(jax.ShapeDtypeStruct((half, total),...  2.63 us
    ppermute x2, waiting for transfers between devices, exchange(): got = lax.ppermute(give, ('outer', 'inner'), pair_perm(count))  2.16 us
  transfers between devices with their start and end apart: 12, of which 12 were waited for; matrix products, arithmetic and copies ran while one was open for 0% of the time, Pallas kernels for 0%

profile of v2, /device:TPU:0, one launch (start us, length us, event | category | flops | bytes accessed | tf_op | source)
XLA Modules:
  0.0 74.5 jit_solution(11922705533742821359)
XLA Ops:
  0.7 1.5 %copy.14.first_hbm = f32[3072,32]{1,0:T(8,128)S(1)} copy(f32[3072,32]{0,1:T(8,128)} %param.22) | data formatting | bytes 786432 | tf_op args[10]
  2.3 0.2 copy.15.second_hbm
  2.6 0.0 copy-start
  2.6 2.3 %copy-done = bf16[768,3072]{1,0:T(8,128)(2,1)S(1)} copy-done((bf16[768,3072]{1,0:T(8,128)(2,1)S(1)}, bf16[768,3072]{1,0:T(8,128)(2,1)}, u32[]{:S(2)}) %copy-start) | copy-done | bytes 4718616
  4.9 13.8 %phase_one.1 = (f32[16,3840]{1,0:T(8,128)S(1)}, bf16[16,3840]{1,0:T(8,128)(2,1)S(1)}, bf16[224,768]{1,0:T(8,128)(2,1)S(1)}, bf16[224,3072]{1,0:T(8,128)(2,1)S(1)...) custom-call(s32[1]{0:T(128)} %bitcast.mine_ref, bf16[1,14,14,768]{3,2,1,0:T(8,128)(2,1)S(1)} %copy-done.1, ...), custom_call_target="tpu_custom_call" | custom-call | tf_op jit(solution)/shard_map/phase_one/pallas_call | solution.py:328
  18.8 0.6 collective-permute-start
  19.3 1.0 %collective-permute-done = bf16[16,3840]{1,0:T(8,128)(2,1)S(1)} collective-permute-done((bf16[16,3840]{1,0:T(8,128)(2,1)S(1)}, bf16[16,3840]{1,0:T(8,128)(2,1)S(1)}, u32[]{:S(2)}, u32[]{:S(2)}) %collective-permute-start) | collective-permute-done | bytes 122912 | tf_op jit(solution)/shard_map/ppermute | solution.py:287
  20.3 2.9 %collective-permute-start.1 = (bf16[16,3840]{1,0:T(8,128)(2,1)S(1)}, bf16[16,3840]{1,0:T(8,128)(2,1)S(1)}, u32[]{:S(2)}, u32[]{:S(2)}) collective-permute-start(bf16[16,3840]{1,0:T(8,128)(2,1)S(1)} %add_convert_fusion.9), channel_id=1, source_target_pairs={{0,2},{1,3},{2,0},{3,1},{4,6},{5,7},{6,4},{7,5},{8,10},{9,11},{10,... | collective-permute-start | bytes 368648 | tf_op jit(solution)/shard_map/ppermute | solution.py:269
  23.3 3.6 %collective-permute-done.1 = bf16[16,3840]{1,0:T(8,128)(2,1)S(1)} collective-permute-done((bf16[16,3840]{1,0:T(8,128)(2,1)S(1)}, bf16[16,3840]{1,0:T(8,128)(2,1)S(1)}, u32[]{:S(2)}, u32[]{:S(2)}) %collective-permute-start.1) | collective-permute-done | bytes 122912 | tf_op jit(solution)/shard_map/ppermute | solution.py:269
  26.9 1.8 %collective-permute-start.2 = (bf16[16,3840]{1,0:T(8,128)(2,1)S(1)}, bf16[16,3840]{1,0:T(8,128)(2,1)S(1)}, u32[]{:S(2)}, u32[]{:S(2)}) collective-permute-start(bf16[16,3840]{1,0:T(8,128)(2,1)S(1)} %add_convert_fusion.8), channel_id=1, source_target_pairs={{0,4},{1,5},{2,6},{3,7},{4,0},{5,1},{6,2},{7,3},{8,12},{9,13},{10,... | collective-permute-start | bytes 368648 | tf_op jit(solution)/shard_map/ppermute | solution.py:269
  28.7 3.2 %collective-permute-done.2 = bf16[16,3840]{1,0:T(8,128)(2,1)S(1)} collective-permute-done((bf16[16,3840]{1,0:T(8,128)(2,1)S(1)}, bf16[16,3840]{1,0:T(8,128)(2,1)S(1)}, u32[]{:S(2)}, u32[]{:S(2)}) %collective-permute-start.2) | collective-permute-done | bytes 122912 | tf_op jit(solution)/shard_map/ppermute | solution.py:269
  31.9 1.9 %collective-permute-start.3 = (bf16[16,3840]{1,0:T(8,128)(2,1)S(1)}, bf16[16,3840]{1,0:T(8,128)(2,1)S(1)}, u32[]{:S(2)}, u32[]{:S(2)}) collective-permute-start(bf16[16,3840]{1,0:T(8,128)(2,1)S(1)} %add_convert_fusion.7), channel_id=1, source_target_pairs={{0,8},{1,9},{2,10},{3,11},{4,12},{5,13},{6,14},{7,15},{8,0},{9,1},... | collective-permute-start | bytes 368648 | tf_op jit(solution)/shard_map/ppermute | solution.py:269
  33.8 3.1 %collective-permute-done.3 = bf16[16,3840]{1,0:T(8,128)(2,1)S(1)} collective-permute-done((bf16[16,3840]{1,0:T(8,128)(2,1)S(1)}, bf16[16,3840]{1,0:T(8,128)(2,1)S(1)}, u32[]{:S(2)}, u32[]{:S(2)}) %collective-permute-start.3) | collective-permute-done | bytes 122912 | tf_op jit(solution)/shard_map/ppermute | solution.py:269
  36.9 3.9 %collective-permute-start.4 = (bf16[16,3840]{1,0:T(8,128)(2,1)S(1)}, bf16[16,3840]{1,0:T(8,128)(2,1)S(1)}, u32[]{:S(2)}, u32[]{:S(2)}) collective-permute-start(bf16[16,3840]{1,0:T(8,128)(2,1)S(1)} %add_convert_fusion.6), channel_id=1, source_target_pairs={{0,24},{1,25},{2,26},{3,27},{4,28},{5,29},{6,30},{7,31},{8,16},{9,... | collective-permute-start | bytes 368648 | tf_op jit(solution)/shard_map/ppermute | solution.py:269
  40.8 3.0 %collective-permute-done.4 = bf16[16,3840]{1,0:T(8,128)(2,1)S(1)} collective-permute-done((bf16[16,3840]{1,0:T(8,128)(2,1)S(1)}, bf16[16,3840]{1,0:T(8,128)(2,1)S(1)}, u32[]{:S(2)}, u32[]{:S(2)}) %collective-permute-start.4) | collective-permute-done | bytes 122912 | tf_op jit(solution)/shard_map/ppermute | solution.py:269
  43.8 0.1 collective-permute-start.5
  43.9 1.3 %collective-permute-done.5.other_ref = bf16[16,3840]{1,0:T(8,128)(2,1)S(1)} collective-permute-done((bf16[16,3840]{1,0:T(8,128)(2,1)S(1)}, bf16[16,3840]{1,0:T(8,128)(2,1)S(1)}, u32[]{:S(2)}, u32[]{:S(2)}) %collective-permute-start.5) | collective-permute-done | bytes 122912 | tf_op jit(solution)/shard_map/ppermute | solution.py:295
  45.2 2.6 %phase_two.1 = (f32[16,3840]{1,0:T(8,128)S(1)}, bf16[16,3840]{1,0:T(8,128)(2,1)S(1)}) custom-call(s32[1]{0:T(128)} %bitcast.mine_ref, bf16[16,3840]{1,0:T(8,128)(2,1)S(1)} %add_convert_fusion.5.value_ref, bf16[16,3840]{1,0:T(8,128)(2,1)S(1)} %collective-permute-done.5.other_ref, bf16[224,768]{1,0:T(8,128)(2,1)S(1)} %get-tuple-element.12.normed_ref, ...), custom_call_target="tpu_custom_call" | custom-call | tf_op jit(solution)/shard_map/phase_two/pallas_call | solution.py:372
  47.8 0.2 collective-permute-start.6
  48.0 1.2 %collective-permute-done.6 = bf16[16,3840]{1,0:T(8,128)(2,1)S(1)} collective-permute-done((bf16[16,3840]{1,0:T(8,128)(2,1)S(1)}, bf16[16,3840]{1,0:T(8,128)(2,1)S(1)}, u32[]{:S(2)}, u32[]{:S(2)}) %collective-permute-start.6) | collective-permute-done | bytes 122912 | tf_op jit(solution)/shard_map/ppermute | solution.py:287
  49.2 1.8 %collective-permute-start.7 = (bf16[16,3840]{1,0:T(8,128)(2,1)S(1)}, bf16[16,3840]{1,0:T(8,128)(2,1)S(1)}, u32[]{:S(2)}, u32[]{:S(2)}) collective-permute-start(bf16[16,3840]{1,0:T(8,128)(2,1)S(1)} %add_convert_fusion.4), channel_id=1, source_target_pairs={{0,2},{1,3},{2,0},{3,1},{4,6},{5,7},{6,4},{7,5},{8,10},{9,11},{10,... | collective-permute-start | bytes 368648 | tf_op jit(solution)/shard_map/ppermute | solution.py:269
  51.1 3.6 %collective-permute-done.7 = bf16[16,3840]{1,0:T(8,128)(2,1)S(1)} collective-permute-done((bf16[16,3840]{1,0:T(8,128)(2,1)S(1)}, bf16[16,3840]{1,0:T(8,128)(2,1)S(1)}, u32[]{:S(2)}, u32[]{:S(2)}) %collective-permute-start.7) | collective-permute-done | bytes 122912 | tf_op jit(solution)/shard_map/ppermute | solution.py:269
  54.7 1.8 %collective-permute-start.8 = (bf16[16,3840]{1,0:T(8,128)(2,1)S(1)}, bf16[16,3840]{1,0:T(8,128)(2,1)S(1)}, u32[]{:S(2)}, u32[]{:S(2)}) collective-permute-start(bf16[16,3840]{1,0:T(8,128)(2,1)S(1)} %add_convert_fusion.3), channel_id=1, source_target_pairs={{0,4},{1,5},{2,6},{3,7},{4,0},{5,1},{6,2},{7,3},{8,12},{9,13},{10,... | collective-permute-start | bytes 368648 | tf_op jit(solution)/shard_map/ppermute | solution.py:269
  56.5 3.2 %collective-permute-done.8 = bf16[16,3840]{1,0:T(8,128)(2,1)S(1)} collective-permute-done((bf16[16,3840]{1,0:T(8,128)(2,1)S(1)}, bf16[16,3840]{1,0:T(8,128)(2,1)S(1)}, u32[]{:S(2)}, u32[]{:S(2)}) %collective-permute-start.8) | collective-permute-done | bytes 122912 | tf_op jit(solution)/shard_map/ppermute | solution.py:269
  59.7 1.3 %collective-permute-start.9 = (bf16[16,3840]{1,0:T(8,128)(2,1)S(1)}, bf16[16,3840]{1,0:T(8,128)(2,1)S(1)}, u32[]{:S(2)}, u32[]{:S(2)}) collective-permute-start(bf16[16,3840]{1,0:T(8,128)(2,1)S(1)} %add_convert_fusion.2), channel_id=1, source_target_pairs={{0,8},{1,9},{2,10},{3,11},{4,12},{5,13},{6,14},{7,15},{8,0},{9,1},... | collective-permute-start | bytes 368648 | tf_op jit(solution)/shard_map/ppermute | solution.py:269
  61.0 3.6 %collective-permute-done.9 = bf16[16,3840]{1,0:T(8,128)(2,1)S(1)} collective-permute-done((bf16[16,3840]{1,0:T(8,128)(2,1)S(1)}, bf16[16,3840]{1,0:T(8,128)(2,1)S(1)}, u32[]{:S(2)}, u32[]{:S(2)}) %collective-permute-start.9) | collective-permute-done | bytes 122912 | tf_op jit(solution)/shard_map/ppermute | solution.py:269
  64.7 3.8 %collective-permute-start.10 = (bf16[16,3840]{1,0:T(8,128)(2,1)S(1)}, bf16[16,3840]{1,0:T(8,128)(2,1)S(1)}, u32[]{:S(2)}, u32[]{:S(2)}) collective-permute-start(bf16[16,3840]{1,0:T(8,128)(2,1)S(1)} %add_convert_fusion.1), channel_id=1, source_target_pairs={{0,24},{1,25},{2,26},{3,27},{4,28},{5,29},{6,30},{7,31},{8,16},{9,... | collective-permute-start | bytes 368648 | tf_op jit(solution)/shard_map/ppermute | solution.py:269
  68.5 3.1 %collective-permute-done.10 = bf16[16,3840]{1,0:T(8,128)(2,1)S(1)} collective-permute-done((bf16[16,3840]{1,0:T(8,128)(2,1)S(1)}, bf16[16,3840]{1,0:T(8,128)(2,1)S(1)}, u32[]{:S(2)}, u32[]{:S(2)}) %collective-permute-start.10) | collective-permute-done | bytes 122912 | tf_op jit(solution)/shard_map/ppermute | solution.py:269
  71.6 0.1 collective-permute-start.11
  71.7 1.3 %collective-permute-done.11 = bf16[16,3840]{1,0:T(8,128)(2,1)S(1)} collective-permute-done((bf16[16,3840]{1,0:T(8,128)(2,1)S(1)}, bf16[16,3840]{1,0:T(8,128)(2,1)S(1)}, u32[]{:S(2)}, u32[]{:S(2)}) %collective-permute-start.11) | collective-permute-done | bytes 122912 | tf_op jit(solution)/shard_map/ppermute | solution.py:295
  73.0 0.8 %slice_bitcast_fusion = f32[3072,32]{0,1:T(8,128)} fusion(f32[32,3840]{1,0:T(8,128)S(1)} %convert_multiply_fusion), kind=kLoop, calls=%fused_computation.1 | loop fusion | bytes 786432 | tf_op jit(solution)/shard_map/transpose | solution.py:387
  73.8 0.6 slice_bitcast_fusion.1
  (34 shorter events, 0.4 us)
Async XLA Ops:
  0.6 1.7 %copy-start.5 = (f32[768,32]{0,1:T(8,128)S(1)}, f32[768,32]{0,1:T(8,128)}, u32[]{:S(2)}) copy-start(f32[768,32]{0,1:T(8,128)} %param.23) | copy-start | bytes 294916
  0.6 1.8 %copy-start.6 = (f32[768]{0:T(1024)S(1)}, f32[768]{0:T(1024)}, u32[]{:S(2)}) copy-start(f32[768]{0:T(1024)} %param.15) | copy-start | bytes 9220
  0.7 1.8 %copy-start.7 = (f32[768]{0:T(1024)S(1)}, f32[768]{0:T(1024)}, u32[]{:S(2)}) copy-start(f32[768]{0:T(1024)} %param.16) | copy-start | bytes 9220
  0.7 1.8 %copy-start.8 = (f32[768]{0:T(1024)S(1)}, f32[768]{0:T(1024)}, u32[]{:S(2)}) copy-start(f32[768]{0:T(1024)} %param.17) | copy-start | bytes 9220
  0.7 1.9 %copy-start.9 = (f32[768]{0:T(1024)S(1)}, f32[768]{0:T(1024)}, u32[]{:S(2)}) copy-start(f32[768]{0:T(1024)} %param.21) | copy-start | bytes 9220
  0.7 1.9 %copy-start.4 = (f32[3072]{0:T(1024)S(1)}, f32[3072]{0:T(1024)}, u32[]{:S(2)}) copy-start(f32[3072]{0:T(1024)} %param.19) | copy-start | bytes 36868
  0.7 1.9 %copy-start.1 = (bf16[1,14,14,768]{3,2,1,0:T(8,128)(2,1)S(1)}, bf16[1,14,14,768]{3,2,1,0:T(8,128)(2,1)}, u32[]{:S(2)}) copy-start(bf16[1,14,14,768]{3,2,1,0:T(8,128)(2,1)} %images_hbm.1) | copy-start | bytes 903172
  0.7 1.9 %copy-start.2 = (bf16[1,14,14,768]{3,2,1,0:T(8,128)(2,1)S(1)}, bf16[1,14,14,768]{3,2,1,0:T(8,128)(2,1)}, u32[]{:S(2)}) copy-start(bf16[1,14,14,768]{3,2,1,0:T(8,128)(2,1)} %cotangent_hbm.1) | copy-start | bytes 903172
  0.7 1.9 %copy-start.3 = (f32[7,7,768]{2,1,0:T(8,128)S(1)}, f32[7,7,768]{2,1,0:T(8,128)}, u32[]{:S(2)}) copy-start(f32[7,7,768]{2,1,0:T(8,128)} %taps_hbm.1) | copy-start | bytes 451588
  2.6 2.3 %copy-start = (bf16[768,3072]{1,0:T(8,128)(2,1)S(1)}, bf16[768,3072]{1,0:T(8,128)(2,1)}, u32[]{:S(2)}) copy-start(bf16[768,3072]{1,0:T(8,128)(2,1)} %expand_hbm.1) | copy-start | bytes 14155780
  18.8 1.5 %collective-permute-start = (bf16[16,3840]{1,0:T(8,128)(2,1)S(1)}, bf16[16,3840]{1,0:T(8,128)(2,1)S(1)}, u32[]{:S(2)}, u32[]{:S(2)}) collective-permute-start(bf16[16,3840]{1,0:T(8,128)(2,1)S(1)} %get-tuple-element.11), channel_id=1, source_target_pairs={{0,1},{1,0},{2,3},{3,2},{4,5},{5,4},{6,7},{7,6},{8,9},{9,8},{10,11... | collective-permute-start | bytes 368648 | tf_op jit(solution)/shard_map/ppermute | solution.py:287
  20.3 6.5 %collective-permute-start.1 = (bf16[16,3840]{1,0:T(8,128)(2,1)S(1)}, bf16[16,3840]{1,0:T(8,128)(2,1)S(1)}, u32[]{:S(2)}, u32[]{:S(2)}) collective-permute-start(bf16[16,3840]{1,0:T(8,128)(2,1)S(1)} %add_convert_fusion.9), channel_id=1, source_target_pairs={{0,2},{1,3},{2,0},{3,1},{4,6},{5,7},{6,4},{7,5},{8,10},{9,11},{10,... | collective-permute-start | bytes 368648 | tf_op jit(solution)/shard_map/ppermute | solution.py:269
  26.9 4.9 %collective-permute-start.2 = (bf16[16,3840]{1,0:T(8,128)(2,1)S(1)}, bf16[16,3840]{1,0:T(8,128)(2,1)S(1)}, u32[]{:S(2)}, u32[]{:S(2)}) collective-permute-start(bf16[16,3840]{1,0:T(8,128)(2,1)S(1)} %add_convert_fusion.8), channel_id=1, source_target_pairs={{0,4},{1,5},{2,6},{3,7},{4,0},{5,1},{6,2},{7,3},{8,12},{9,13},{10,... | collective-permute-start | bytes 368648 | tf_op jit(solution)/shard_map/ppermute | solution.py:269
  31.9 4.9 %collective-permute-start.3 = (bf16[16,3840]{1,0:T(8,128)(2,1)S(1)}, bf16[16,3840]{1,0:T(8,128)(2,1)S(1)}, u32[]{:S(2)}, u32[]{:S(2)}) collective-permute-start(bf16[16,3840]{1,0:T(8,128)(2,1)S(1)} %add_convert_fusion.7), channel_id=1, source_target_pairs={{0,8},{1,9},{2,10},{3,11},{4,12},{5,13},{6,14},{7,15},{8,0},{9,1},... | collective-permute-start | bytes 368648 | tf_op jit(solution)/shard_map/ppermute | solution.py:269
  36.9 6.8 %collective-permute-start.4 = (bf16[16,3840]{1,0:T(8,128)(2,1)S(1)}, bf16[16,3840]{1,0:T(8,128)(2,1)S(1)}, u32[]{:S(2)}, u32[]{:S(2)}) collective-permute-start(bf16[16,3840]{1,0:T(8,128)(2,1)S(1)} %add_convert_fusion.6), channel_id=1, source_target_pairs={{0,24},{1,25},{2,26},{3,27},{4,28},{5,29},{6,30},{7,31},{8,16},{9,... | collective-permute-start | bytes 368648 | tf_op jit(solution)/shard_map/ppermute | solution.py:269
  43.8 1.4 %collective-permute-start.5 = (bf16[16,3840]{1,0:T(8,128)(2,1)S(1)}, bf16[16,3840]{1,0:T(8,128)(2,1)S(1)}, u32[]{:S(2)}, u32[]{:S(2)}) collective-permute-start(bf16[16,3840]{1,0:T(8,128)(2,1)S(1)} %add_convert_fusion.5.value_ref), channel_id=1, source_target_pairs={{0,1},{1,0},{2,3},{3,2},{4,5},{5,4},{6,7},{7,6},{8,9},{9,8},{10,11... | collective-permute-start | bytes 368648 | tf_op jit(solution)/shard_map/ppermute | solution.py:295
  47.8 1.4 %collective-permute-start.6 = (bf16[16,3840]{1,0:T(8,128)(2,1)S(1)}, bf16[16,3840]{1,0:T(8,128)(2,1)S(1)}, u32[]{:S(2)}, u32[]{:S(2)}) collective-permute-start(bf16[16,3840]{1,0:T(8,128)(2,1)S(1)} %get-tuple-element.17), channel_id=1, source_target_pairs={{0,1},{1,0},{2,3},{3,2},{4,5},{5,4},{6,7},{7,6},{8,9},{9,8},{10,11... | collective-permute-start | bytes 368648 | tf_op jit(solution)/shard_map/ppermute | solution.py:287
  49.2 5.4 %collective-permute-start.7 = (bf16[16,3840]{1,0:T(8,128)(2,1)S(1)}, bf16[16,3840]{1,0:T(8,128)(2,1)S(1)}, u32[]{:S(2)}, u32[]{:S(2)}) collective-permute-start(bf16[16,3840]{1,0:T(8,128)(2,1)S(1)} %add_convert_fusion.4), channel_id=1, source_target_pairs={{0,2},{1,3},{2,0},{3,1},{4,6},{5,7},{6,4},{7,5},{8,10},{9,11},{10,... | collective-permute-start | bytes 368648 | tf_op jit(solution)/shard_map/ppermute | solution.py:269
  54.7 4.9 %collective-permute-start.8 = (bf16[16,3840]{1,0:T(8,128)(2,1)S(1)}, bf16[16,3840]{1,0:T(8,128)(2,1)S(1)}, u32[]{:S(2)}, u32[]{:S(2)}) collective-permute-start(bf16[16,3840]{1,0:T(8,128)(2,1)S(1)} %add_convert_fusion.3), channel_id=1, source_target_pairs={{0,4},{1,5},{2,6},{3,7},{4,0},{5,1},{6,2},{7,3},{8,12},{9,13},{10,... | collective-permute-start | bytes 368648 | tf_op jit(solution)/shard_map/ppermute | solution.py:269
  59.7 4.9 %collective-permute-start.9 = (bf16[16,3840]{1,0:T(8,128)(2,1)S(1)}, bf16[16,3840]{1,0:T(8,128)(2,1)S(1)}, u32[]{:S(2)}, u32[]{:S(2)}) collective-permute-start(bf16[16,3840]{1,0:T(8,128)(2,1)S(1)} %add_convert_fusion.2), channel_id=1, source_target_pairs={{0,8},{1,9},{2,10},{3,11},{4,12},{5,13},{6,14},{7,15},{8,0},{9,1},... | collective-permute-start | bytes 368648 | tf_op jit(solution)/shard_map/ppermute | solution.py:269
  64.7 6.8 %collective-permute-start.10 = (bf16[16,3840]{1,0:T(8,128)(2,1)S(1)}, bf16[16,3840]{1,0:T(8,128)(2,1)S(1)}, u32[]{:S(2)}, u32[]{:S(2)}) collective-permute-start(bf16[16,3840]{1,0:T(8,128)(2,1)S(1)} %add_convert_fusion.1), channel_id=1, source_target_pairs={{0,24},{1,25},{2,26},{3,27},{4,28},{5,29},{6,30},{7,31},{8,16},{9,... | collective-permute-start | bytes 368648 | tf_op jit(solution)/shard_map/ppermute | solution.py:269
  71.6 1.4 %collective-permute-start.11 = (bf16[16,3840]{1,0:T(8,128)(2,1)S(1)}, bf16[16,3840]{1,0:T(8,128)(2,1)S(1)}, u32[]{:S(2)}, u32[]{:S(2)}) collective-permute-start(bf16[16,3840]{1,0:T(8,128)(2,1)S(1)} %add_convert_fusion), channel_id=1, source_target_pairs={{0,1},{1,0},{2,3},{3,2},{4,5},{5,4},{6,7},{7,6},{8,9},{9,8},{10,11... | collective-permute-start | bytes 368648 | tf_op jit(solution)/shard_map/ppermute | solution.py:295

commit v3 on v2

--- a/solution.py
+++ b/solution.py
@@ -261,13 +261,8 @@
     return lax.ppermute(value, ("outer", "inner"), perm)
 
 
-def step_sum(value, count, stride, radix, mirror):
+def turn(value, count, stride, radix):
     sent = value.astype(jnp.bfloat16)
-    if radix == 2:
-        mask = stride | mirror
-        perm = [(source, source ^ mask) for source in range(count)]
-        got = lax.ppermute(sent, ("outer", "inner"), perm)
-        return sent.astype(jnp.float32) + got.astype(jnp.float32)
     mine = (linear_index() // stride) % radix
     parts = jnp.stack([sent] + [shifted(sent, count, stride, radix, k) for k in range(1, radix)])
     total = jnp.zeros(value.shape, jnp.float32)
@@ -276,6 +271,31 @@
     return total
 
 
+def swap_stages(steps):
+    masks = [stride for stride, radix in steps if radix == 2]
+    even = len(masks) // 2 * 2
+    return [masks[k : k + 2] for k in range(0, even, 2)], [[mask] for mask in masks[even:]]
+
+
+def swap_sum(value, count, orders):
+    sent = value.astype(jnp.bfloat16)
+
+    def partner(pick):
+        masks = []
+        for stage in orders:
+            mask = 0
+            for k in pick:
+                mask ^= stage[k]
+            masks.append(mask)
+        perm = [(source, source ^ masks[source % 2]) for source in range(count)]
+        return lax.ppermute(sent, ("outer", "inner"), perm).astype(jnp.float32)
+
+    if len(orders[0]) == 1:
+        return sent.astype(jnp.float32) + partner((0,))
+    near, far, both = partner((0,)), partner((1,)), partner((0, 1))
+    return (sent.astype(jnp.float32) + near) + (far + both)
+
+
 def pair_perm(count):
     return [(source, source ^ 1) for source in range(count)]
 
@@ -286,11 +306,13 @@
     steps = plan(n_outer, n_inner)[1:]
     got = lax.ppermute(give, ("outer", "inner"), pair_perm(count))
     value = keep + got.astype(jnp.float32)
-    for place, (stride, radix) in enumerate(steps):
-        before = steps[place - 1] if place else None
-        last = place == len(steps) - 1 and radix == 2 and before is not None
-        mirror = before[0] if last and before[1] == 2 and stride > n_inner else 0
-        value = step_sum(value, count, stride, radix, mirror)
+    quads, singles = swap_stages(steps)
+    cut = len(quads) // 2
+    for even, odd in zip(quads + singles, quads[cut:] + quads[:cut] + singles):
+        value = swap_sum(value, count, (even, odd))
+    for stride, radix in steps:
+        if radix != 2:
+            value = turn(value, count, stride, radix)
     value = value.astype(jnp.bfloat16)
     other = lax.ppermute(value, ("outer", "inner"), pair_perm(count))
     return value, other

time: 74.6 us -> 67.4 us (0.903)
  waiting for transfers between devices: 31.1 us -> 26.2 us
  starting transfers between devices: 20.1 us -> 17.8 us
    ppermute x8 -> x12, waiting for transfers between devices: 26.3 us -> 21.4 us  [partner(): return lax.ppermute(sent, ('outer', 'inner'), perm).astype(jnp.float32)]
    ppermute x8 -> x12, starting transfers between devices: 19.1 us -> 16.9 us  [partner(): return lax.ppermute(sent, ('outer', 'inner'), perm).astype(jnp.float32)]
  transfers between devices with their start and end apart: 12 -> 16, of which waited for: 12 -> 15; matrix products, arithmetic and copies ran while one was open for 0% -> 0% of each run, Pallas kernels for 0% -> 0%
where the time goes in v3:
time: 67.4 us; the launch traced here: 67.3 us
  waiting for transfers between devices  26.2 us (39%)
  starting transfers between devices  17.8 us (26%)
  Pallas kernels  16.5 us (24%)
  local copies, waits for them, and re-layouts  5.51 us (8%)
  between operations  0.92 us (1%)
    ppermute x12, waiting for transfers between devices, partner(): return lax.ppermute(sent, ('outer', 'inner'), perm).astype(jnp.float32)  21.4 us
    ppermute x12, starting transfers between devices, partner(): return lax.ppermute(sent, ('outer', 'inner'), perm).astype(jnp.float32)  16.9 us
    pallas_call x1, Pallas kernels, shards(): pl.pallas_call(phase_one, out_shape=(jax.ShapeDtypeStruct((half, total),...  13.8 us
    unnamed x22, local copies, waits for them, and re-layouts  4.08 us
    ppermute x2, waiting for transfers between devices, exchange(): other = lax.ppermute(value, ('outer', 'inner'), pair_perm(count))  2.64 us
    pallas_call x1, Pallas kernels, shards(): pl.pallas_call(phase_two, out_shape=(jax.ShapeDtypeStruct((half, total),...  2.63 us
    ppermute x2, waiting for transfers between devices, exchange(): got = lax.ppermute(give, ('outer', 'inner'), pair_perm(count))  2.16 us
    transpose x2, local copies, waits for them, and re-layouts, shards(): return (both[:, width:].T, both[:, :width].T)  1.42 us
  transfers between devices with their start and end apart: 16, of which 15 were waited for; matrix products, arithmetic and copies ran while one was open for 0% of the time, Pallas kernels for 0%

profile of v3, /device:TPU:0, one launch (start us, length us, event | category | flops | bytes accessed | tf_op | source)
XLA Modules:
  0.0 67.3 jit_solution(309438083865384639)
XLA Ops:
  0.7 1.5 %copy.14.first_hbm = f32[3072,32]{1,0:T(8,128)S(1)} copy(f32[3072,32]{0,1:T(8,128)} %param.22) | data formatting | bytes 786432 | tf_op args[10]
  2.6 2.3 %copy-done = bf16[768,3072]{1,0:T(8,128)(2,1)S(1)} copy-done((bf16[768,3072]{1,0:T(8,128)(2,1)S(1)}, bf16[768,3072]{1,0:T(8,128)(2,1)}, u32[]{:S(2)}) %copy-start) | copy-done | bytes 4718616
  4.9 13.8 %phase_one.1 = (f32[16,3840]{1,0:T(8,128)S(1)}, bf16[16,3840]{1,0:T(8,128)(2,1)S(1)}, bf16[224,768]{1,0:T(8,128)(2,1)S(1)}, bf16[224,3072]{1,0:T(8,128)(2,1)S(1)...) custom-call(s32[1]{0:T(128)} %bitcast.mine_ref, bf16[1,14,14,768]{3,2,1,0:T(8,128)(2,1)S(1)} %copy-done.1, ...), custom_call_target="tpu_custom_call" | custom-call | tf_op jit(solution)/shard_map/phase_one/pallas_call | solution.py:350
  18.8 0.6 collective-permute-start
  19.3 1.0 %collective-permute-done = bf16[16,3840]{1,0:T(8,128)(2,1)S(1)} collective-permute-done((bf16[16,3840]{1,0:T(8,128)(2,1)S(1)}, bf16[16,3840]{1,0:T(8,128)(2,1)S(1)}, u32[]{:S(2)}, u32[]{:S(2)}) %collective-permute-start) | collective-permute-done | bytes 122912 | tf_op jit(solution)/shard_map/ppermute | solution.py:307
  20.3 2.9 %collective-permute-start.1 = (bf16[16,3840]{1,0:T(8,128)(2,1)S(1)}, bf16[16,3840]{1,0:T(8,128)(2,1)S(1)}, u32[]{:S(2)}, u32[]{:S(2)}) collective-permute-start(bf16[16,3840]{1,0:T(8,128)(2,1)S(1)} %add_convert_fusion.5), channel_id=1, source_target_pairs={{0,2},{1,9},{2,0},{3,11},{4,6},{5,13},{6,4},{7,15},{8,10},{9,1},{1... | collective-permute-start | bytes 368648 | tf_op jit(solution)/shard_map/ppermute | solution.py:291
  23.3 1.5 %collective-permute-start.2 = (bf16[16,3840]{1,0:T(8,128)(2,1)S(1)}, bf16[16,3840]{1,0:T(8,128)(2,1)S(1)}, u32[]{:S(2)}, u32[]{:S(2)}) collective-permute-start(bf16[16,3840]{1,0:T(8,128)(2,1)S(1)} %add_convert_fusion.5), channel_id=1, source_target_pairs={{0,4},{1,17},{2,6},{3,19},{4,0},{5,21},{6,2},{7,23},{8,12},{9,25},... | collective-permute-start | bytes 368648 | tf_op jit(solution)/shard_map/ppermute | solution.py:291
  24.8 1.3 %collective-permute-done.1 = bf16[16,3840]{1,0:T(8,128)(2,1)S(1)} collective-permute-done((bf16[16,3840]{1,0:T(8,128)(2,1)S(1)}, bf16[16,3840]{1,0:T(8,128)(2,1)S(1)}, u32[]{:S(2)}, u32[]{:S(2)}) %collective-permute-start.1) | collective-permute-done | bytes 122912 | tf_op jit(solution)/shard_map/ppermute | solution.py:291
  26.1 2.0 %collective-permute-done.2 = bf16[16,3840]{1,0:T(8,128)(2,1)S(1)} collective-permute-done((bf16[16,3840]{1,0:T(8,128)(2,1)S(1)}, bf16[16,3840]{1,0:T(8,128)(2,1)S(1)}, u32[]{:S(2)}, u32[]{:S(2)}) %collective-permute-start.2) | collective-permute-done | bytes 122912 | tf_op jit(solution)/shard_map/ppermute | solution.py:291
  28.1 2.4 %collective-permute-done.3 = bf16[16,3840]{1,0:T(8,128)(2,1)S(1)} collective-permute-done((bf16[16,3840]{1,0:T(8,128)(2,1)S(1)}, bf16[16,3840]{1,0:T(8,128)(2,1)S(1)}, u32[]{:S(2)}, u32[]{:S(2)}) %collective-permute-start.3) | collective-permute-done | bytes 122912 | tf_op jit(solution)/shard_map/ppermute | solution.py:291
  30.6 1.7 %collective-permute-start.4 = (bf16[16,3840]{1,0:T(8,128)(2,1)S(1)}, bf16[16,3840]{1,0:T(8,128)(2,1)S(1)}, u32[]{:S(2)}, u32[]{:S(2)}) collective-permute-start(bf16[16,3840]{1,0:T(8,128)(2,1)S(1)} %add_convert_fusion.4), channel_id=1, source_target_pairs={{0,8},{1,3},{2,10},{3,1},{4,12},{5,7},{6,14},{7,5},{8,0},{9,11},{1... | collective-permute-start | bytes 368648 | tf_op jit(solution)/shard_map/ppermute | solution.py:291
  32.2 2.6 %collective-permute-start.5 = (bf16[16,3840]{1,0:T(8,128)(2,1)S(1)}, bf16[16,3840]{1,0:T(8,128)(2,1)S(1)}, u32[]{:S(2)}, u32[]{:S(2)}) collective-permute-start(bf16[16,3840]{1,0:T(8,128)(2,1)S(1)} %add_convert_fusion.4), channel_id=1, source_target_pairs={{0,16},{1,5},{2,18},{3,7},{4,20},{5,1},{6,22},{7,3},{8,24},{9,13},... | collective-permute-start | bytes 368648 | tf_op jit(solution)/shard_map/ppermute | solution.py:291
  35.0 0.5 collective-permute-done.4
  35.5 3.8 %collective-permute-done.5 = bf16[16,3840]{1,0:T(8,128)(2,1)S(1)} collective-permute-done((bf16[16,3840]{1,0:T(8,128)(2,1)S(1)}, bf16[16,3840]{1,0:T(8,128)(2,1)S(1)}, u32[]{:S(2)}, u32[]{:S(2)}) %collective-permute-start.5) | collective-permute-done | bytes 122912 | tf_op jit(solution)/shard_map/ppermute | solution.py:291
  39.3 2.3 %collective-permute-done.6 = bf16[16,3840]{1,0:T(8,128)(2,1)S(1)} collective-permute-done((bf16[16,3840]{1,0:T(8,128)(2,1)S(1)}, bf16[16,3840]{1,0:T(8,128)(2,1)S(1)}, u32[]{:S(2)}, u32[]{:S(2)}) %collective-permute-start.6) | collective-permute-done | bytes 122912 | tf_op jit(solution)/shard_map/ppermute | solution.py:291
  41.8 1.3 %collective-permute-done.7.other_ref = bf16[16,3840]{1,0:T(8,128)(2,1)S(1)} collective-permute-done((bf16[16,3840]{1,0:T(8,128)(2,1)S(1)}, bf16[16,3840]{1,0:T(8,128)(2,1)S(1)}, u32[]{:S(2)}, u32[]{:S(2)}) %collective-permute-start.7) | collective-permute-done | bytes 122912 | tf_op jit(solution)/shard_map/ppermute | solution.py:317
  43.1 2.6 %phase_two.1 = (f32[16,3840]{1,0:T(8,128)S(1)}, bf16[16,3840]{1,0:T(8,128)(2,1)S(1)}) custom-call(s32[1]{0:T(128)} %bitcast.mine_ref, bf16[16,3840]{1,0:T(8,128)(2,1)S(1)} %add_convert_fusion.3.value_ref, bf16[16,3840]{1,0:T(8,128)(2,1)S(1)} %collective-permute-done.7.other_ref, bf16[224,768]{1,0:T(8,128)(2,1)S(1)} %get-tuple-element.12.normed_ref, ...), custom_call_target="tpu_custom_call" | custom-call | tf_op jit(solution)/shard_map/phase_two/pallas_call | solution.py:394
  45.9 1.2 %collective-permute-done.8 = bf16[16,3840]{1,0:T(8,128)(2,1)S(1)} collective-permute-done((bf16[16,3840]{1,0:T(8,128)(2,1)S(1)}, bf16[16,3840]{1,0:T(8,128)(2,1)S(1)}, u32[]{:S(2)}, u32[]{:S(2)}) %collective-permute-start.8) | collective-permute-done | bytes 122912 | tf_op jit(solution)/shard_map/ppermute | solution.py:307
  47.1 0.6 collective-permute-start.10
  47.7 1.4 %collective-permute-start.11 = (bf16[16,3840]{1,0:T(8,128)(2,1)S(1)}, bf16[16,3840]{1,0:T(8,128)(2,1)S(1)}, u32[]{:S(2)}, u32[]{:S(2)}) collective-permute-start(bf16[16,3840]{1,0:T(8,128)(2,1)S(1)} %add_convert_fusion.2), channel_id=1, source_target_pairs={{0,6},{1,25},{2,4},{3,27},{4,2},{5,29},{6,0},{7,31},{8,14},{9,17},... | collective-permute-start | bytes 368648 | tf_op jit(solution)/shard_map/ppermute | solution.py:291
  49.2 1.5 %collective-permute-start.9 = (bf16[16,3840]{1,0:T(8,128)(2,1)S(1)}, bf16[16,3840]{1,0:T(8,128)(2,1)S(1)}, u32[]{:S(2)}, u32[]{:S(2)}) collective-permute-start(bf16[16,3840]{1,0:T(8,128)(2,1)S(1)} %add_convert_fusion.2), channel_id=1, source_target_pairs={{0,2},{1,9},{2,0},{3,11},{4,6},{5,13},{6,4},{7,15},{8,10},{9,1},{1... | collective-permute-start | bytes 368648 | tf_op jit(solution)/shard_map/ppermute | solution.py:291
  50.7 1.4 %collective-permute-done.10 = bf16[16,3840]{1,0:T(8,128)(2,1)S(1)} collective-permute-done((bf16[16,3840]{1,0:T(8,128)(2,1)S(1)}, bf16[16,3840]{1,0:T(8,128)(2,1)S(1)}, u32[]{:S(2)}, u32[]{:S(2)}) %collective-permute-start.10) | collective-permute-done | bytes 122912 | tf_op jit(solution)/shard_map/ppermute | solution.py:291
  52.1 1.5 %collective-permute-done.11 = bf16[16,3840]{1,0:T(8,128)(2,1)S(1)} collective-permute-done((bf16[16,3840]{1,0:T(8,128)(2,1)S(1)}, bf16[16,3840]{1,0:T(8,128)(2,1)S(1)}, u32[]{:S(2)}, u32[]{:S(2)}) %collective-permute-start.11) | collective-permute-done | bytes 122912 | tf_op jit(solution)/shard_map/ppermute | solution.py:291
  53.6 1.2 %collective-permute-done.9 = bf16[16,3840]{1,0:T(8,128)(2,1)S(1)} collective-permute-done((bf16[16,3840]{1,0:T(8,128)(2,1)S(1)}, bf16[16,3840]{1,0:T(8,128)(2,1)S(1)}, u32[]{:S(2)}, u32[]{:S(2)}) %collective-permute-start.9) | collective-permute-done | bytes 122912 | tf_op jit(solution)/shard_map/ppermute | solution.py:291
  54.9 1.0 %collective-permute-start.12 = (bf16[16,3840]{1,0:T(8,128)(2,1)S(1)}, bf16[16,3840]{1,0:T(8,128)(2,1)S(1)}, u32[]{:S(2)}, u32[]{:S(2)}) collective-permute-start(bf16[16,3840]{1,0:T(8,128)(2,1)S(1)} %add_convert_fusion.1), channel_id=1, source_target_pairs={{0,8},{1,3},{2,10},{3,1},{4,12},{5,7},{6,14},{7,5},{8,0},{9,11},{1... | collective-permute-start | bytes 368648 | tf_op jit(solution)/shard_map/ppermute | solution.py:291
  55.9 1.2 %collective-permute-start.13 = (bf16[16,3840]{1,0:T(8,128)(2,1)S(1)}, bf16[16,3840]{1,0:T(8,128)(2,1)S(1)}, u32[]{:S(2)}, u32[]{:S(2)}) collective-permute-start(bf16[16,3840]{1,0:T(8,128)(2,1)S(1)} %add_convert_fusion.1), channel_id=1, source_target_pairs={{0,16},{1,5},{2,18},{3,7},{4,20},{5,1},{6,22},{7,3},{8,24},{9,13},... | collective-permute-start | bytes 368648 | tf_op jit(solution)/shard_map/ppermute | solution.py:291
  57.1 2.3 %collective-permute-start.14 = (bf16[16,3840]{1,0:T(8,128)(2,1)S(1)}, bf16[16,3840]{1,0:T(8,128)(2,1)S(1)}, u32[]{:S(2)}, u32[]{:S(2)}) collective-permute-start(bf16[16,3840]{1,0:T(8,128)(2,1)S(1)} %add_convert_fusion.1), channel_id=1, source_target_pairs={{0,24},{1,7},{2,26},{3,5},{4,28},{5,3},{6,30},{7,1},{8,16},{9,15},... | collective-permute-start | bytes 368648 | tf_op jit(solution)/shard_map/ppermute | solution.py:291
  59.4 0.5 collective-permute-done.12
  59.9 4.5 %collective-permute-done.13 = bf16[16,3840]{1,0:T(8,128)(2,1)S(1)} collective-permute-done((bf16[16,3840]{1,0:T(8,128)(2,1)S(1)}, bf16[16,3840]{1,0:T(8,128)(2,1)S(1)}, u32[]{:S(2)}, u32[]{:S(2)}) %collective-permute-start.13) | collective-permute-done | bytes 122912 | tf_op jit(solution)/shard_map/ppermute | solution.py:291
  64.5 1.3 %collective-permute-done.15 = bf16[16,3840]{1,0:T(8,128)(2,1)S(1)} collective-permute-done((bf16[16,3840]{1,0:T(8,128)(2,1)S(1)}, bf16[16,3840]{1,0:T(8,128)(2,1)S(1)}, u32[]{:S(2)}, u32[]{:S(2)}) %collective-permute-start.15) | collective-permute-done | bytes 122912 | tf_op jit(solution)/shard_map/ppermute | solution.py:317
  65.9 0.8 %slice_bitcast_fusion = f32[3072,32]{0,1:T(8,128)} fusion(f32[32,3840]{1,0:T(8,128)S(1)} %convert_multiply_fusion), kind=kLoop, calls=%fused_computation.1 | loop fusion | bytes 786432 | tf_op jit(solution)/shard_map/transpose | solution.py:409
  66.6 0.6 slice_bitcast_fusion.1
  (38 shorter events, 1.2 us)
Async XLA Ops:
  0.6 1.7 %copy-start.5 = (f32[768,32]{0,1:T(8,128)S(1)}, f32[768,32]{0,1:T(8,128)}, u32[]{:S(2)}) copy-start(f32[768,32]{0,1:T(8,128)} %param.23) | copy-start | bytes 294916
  0.6 1.8 %copy-start.6 = (f32[768]{0:T(1024)S(1)}, f32[768]{0:T(1024)}, u32[]{:S(2)}) copy-start(f32[768]{0:T(1024)} %param.15) | copy-start | bytes 9220
  0.7 1.8 %copy-start.7 = (f32[768]{0:T(1024)S(1)}, f32[768]{0:T(1024)}, u32[]{:S(2)}) copy-start(f32[768]{0:T(1024)} %param.16) | copy-start | bytes 9220
  0.7 1.8 %copy-start.8 = (f32[768]{0:T(1024)S(1)}, f32[768]{0:T(1024)}, u32[]{:S(2)}) copy-start(f32[768]{0:T(1024)} %param.17) | copy-start | bytes 9220
  0.7 1.9 %copy-start.9 = (f32[768]{0:T(1024)S(1)}, f32[768]{0:T(1024)}, u32[]{:S(2)}) copy-start(f32[768]{0:T(1024)} %param.21) | copy-start | bytes 9220
  0.7 1.9 %copy-start.4 = (f32[3072]{0:T(1024)S(1)}, f32[3072]{0:T(1024)}, u32[]{:S(2)}) copy-start(f32[3072]{0:T(1024)} %param.19) | copy-start | bytes 36868
  0.7 1.9 %copy-start.1 = (bf16[1,14,14,768]{3,2,1,0:T(8,128)(2,1)S(1)}, bf16[1,14,14,768]{3,2,1,0:T(8,128)(2,1)}, u32[]{:S(2)}) copy-start(bf16[1,14,14,768]{3,2,1,0:T(8,128)(2,1)} %images_hbm.1) | copy-start | bytes 903172
  0.7 1.9 %copy-start.2 = (bf16[1,14,14,768]{3,2,1,0:T(8,128)(2,1)S(1)}, bf16[1,14,14,768]{3,2,1,0:T(8,128)(2,1)}, u32[]{:S(2)}) copy-start(bf16[1,14,14,768]{3,2,1,0:T(8,128)(2,1)} %cotangent_hbm.1) | copy-start | bytes 903172
  0.7 1.9 %copy-start.3 = (f32[7,7,768]{2,1,0:T(8,128)S(1)}, f32[7,7,768]{2,1,0:T(8,128)}, u32[]{:S(2)}) copy-start(f32[7,7,768]{2,1,0:T(8,128)} %taps_hbm.1) | copy-start | bytes 451588
  2.6 2.3 %copy-start = (bf16[768,3072]{1,0:T(8,128)(2,1)S(1)}, bf16[768,3072]{1,0:T(8,128)(2,1)}, u32[]{:S(2)}) copy-start(bf16[768,3072]{1,0:T(8,128)(2,1)} %expand_hbm.1) | copy-start | bytes 14155780
  18.8 1.5 %collective-permute-start = (bf16[16,3840]{1,0:T(8,128)(2,1)S(1)}, bf16[16,3840]{1,0:T(8,128)(2,1)S(1)}, u32[]{:S(2)}, u32[]{:S(2)}) collective-permute-start(bf16[16,3840]{1,0:T(8,128)(2,1)S(1)} %get-tuple-element.11), channel_id=1, source_target_pairs={{0,1},{1,0},{2,3},{3,2},{4,5},{5,4},{6,7},{7,6},{8,9},{9,8},{10,11... | collective-permute-start | bytes 368648 | tf_op jit(solution)/shard_map/ppermute | solution.py:307
  20.3 5.8 %collective-permute-start.1 = (bf16[16,3840]{1,0:T(8,128)(2,1)S(1)}, bf16[16,3840]{1,0:T(8,128)(2,1)S(1)}, u32[]{:S(2)}, u32[]{:S(2)}) collective-permute-start(bf16[16,3840]{1,0:T(8,128)(2,1)S(1)} %add_convert_fusion.5), channel_id=1, source_target_pairs={{0,2},{1,9},{2,0},{3,11},{4,6},{5,13},{6,4},{7,15},{8,10},{9,1},{1... | collective-permute-start | bytes 368648 | tf_op jit(solution)/shard_map/ppermute | solution.py:291
  23.3 4.9 %collective-permute-start.2 = (bf16[16,3840]{1,0:T(8,128)(2,1)S(1)}, bf16[16,3840]{1,0:T(8,128)(2,1)S(1)}, u32[]{:S(2)}, u32[]{:S(2)}) collective-permute-start(bf16[16,3840]{1,0:T(8,128)(2,1)S(1)} %add_convert_fusion.5), channel_id=1, source_target_pairs={{0,4},{1,17},{2,6},{3,19},{4,0},{5,21},{6,2},{7,23},{8,12},{9,25},... | collective-permute-start | bytes 368648 | tf_op jit(solution)/shard_map/ppermute | solution.py:291
  24.7 5.8 %collective-permute-start.3 = (bf16[16,3840]{1,0:T(8,128)(2,1)S(1)}, bf16[16,3840]{1,0:T(8,128)(2,1)S(1)}, u32[]{:S(2)}, u32[]{:S(2)}) collective-permute-start(bf16[16,3840]{1,0:T(8,128)(2,1)S(1)} %add_convert_fusion.5), channel_id=1, source_target_pairs={{0,6},{1,25},{2,4},{3,27},{4,2},{5,29},{6,0},{7,31},{8,14},{9,17},... | collective-permute-start | bytes 368648 | tf_op jit(solution)/shard_map/ppermute | solution.py:291
  30.6 4.9 %collective-permute-start.4 = (bf16[16,3840]{1,0:T(8,128)(2,1)S(1)}, bf16[16,3840]{1,0:T(8,128)(2,1)S(1)}, u32[]{:S(2)}, u32[]{:S(2)}) collective-permute-start(bf16[16,3840]{1,0:T(8,128)(2,1)S(1)} %add_convert_fusion.4), channel_id=1, source_target_pairs={{0,8},{1,3},{2,10},{3,1},{4,12},{5,7},{6,14},{7,5},{8,0},{9,11},{1... | collective-permute-start | bytes 368648 | tf_op jit(solution)/shard_map/ppermute | solution.py:291
  32.2 7.1 %collective-permute-start.5 = (bf16[16,3840]{1,0:T(8,128)(2,1)S(1)}, bf16[16,3840]{1,0:T(8,128)(2,1)S(1)}, u32[]{:S(2)}, u32[]{:S(2)}) collective-permute-start(bf16[16,3840]{1,0:T(8,128)(2,1)S(1)} %add_convert_fusion.4), channel_id=1, source_target_pairs={{0,16},{1,5},{2,18},{3,7},{4,20},{5,1},{6,22},{7,3},{8,24},{9,13},... | collective-permute-start | bytes 368648 | tf_op jit(solution)/shard_map/ppermute | solution.py:291
  34.8 6.8 %collective-permute-start.6 = (bf16[16,3840]{1,0:T(8,128)(2,1)S(1)}, bf16[16,3840]{1,0:T(8,128)(2,1)S(1)}, u32[]{:S(2)}, u32[]{:S(2)}) collective-permute-start(bf16[16,3840]{1,0:T(8,128)(2,1)S(1)} %add_convert_fusion.4), channel_id=1, source_target_pairs={{0,24},{1,7},{2,26},{3,5},{4,28},{5,3},{6,30},{7,1},{8,16},{9,15},... | collective-permute-start | bytes 368648 | tf_op jit(solution)/shard_map/ppermute | solution.py:291
  41.7 1.4 %collective-permute-start.7 = (bf16[16,3840]{1,0:T(8,128)(2,1)S(1)}, bf16[16,3840]{1,0:T(8,128)(2,1)S(1)}, u32[]{:S(2)}, u32[]{:S(2)}) collective-permute-start(bf16[16,3840]{1,0:T(8,128)(2,1)S(1)} %add_convert_fusion.3.value_ref), channel_id=1, source_target_pairs={{0,1},{1,0},{2,3},{3,2},{4,5},{5,4},{6,7},{7,6},{8,9},{9,8},{10,11... | collective-permute-start | bytes 368648 | tf_op jit(solution)/shard_map/ppermute | solution.py:317
  45.7 1.4 %collective-permute-start.8 = (bf16[16,3840]{1,0:T(8,128)(2,1)S(1)}, bf16[16,3840]{1,0:T(8,128)(2,1)S(1)}, u32[]{:S(2)}, u32[]{:S(2)}) collective-permute-start(bf16[16,3840]{1,0:T(8,128)(2,1)S(1)} %get-tuple-element.17), channel_id=1, source_target_pairs={{0,1},{1,0},{2,3},{3,2},{4,5},{5,4},{6,7},{7,6},{8,9},{9,8},{10,11... | collective-permute-start | bytes 368648 | tf_op jit(solution)/shard_map/ppermute | solution.py:307
  47.1 4.9 %collective-permute-start.10 = (bf16[16,3840]{1,0:T(8,128)(2,1)S(1)}, bf16[16,3840]{1,0:T(8,128)(2,1)S(1)}, u32[]{:S(2)}, u32[]{:S(2)}) collective-permute-start(bf16[16,3840]{1,0:T(8,128)(2,1)S(1)} %add_convert_fusion.2), channel_id=1, source_target_pairs={{0,4},{1,17},{2,6},{3,19},{4,0},{5,21},{6,2},{7,23},{8,12},{9,25},... | collective-permute-start | bytes 368648 | tf_op jit(solution)/shard_map/ppermute | solution.py:291
  47.7 5.9 %collective-permute-start.11 = (bf16[16,3840]{1,0:T(8,128)(2,1)S(1)}, bf16[16,3840]{1,0:T(8,128)(2,1)S(1)}, u32[]{:S(2)}, u32[]{:S(2)}) collective-permute-start(bf16[16,3840]{1,0:T(8,128)(2,1)S(1)} %add_convert_fusion.2), channel_id=1, source_target_pairs={{0,6},{1,25},{2,4},{3,27},{4,2},{5,29},{6,0},{7,31},{8,14},{9,17},... | collective-permute-start | bytes 368648 | tf_op jit(solution)/shard_map/ppermute | solution.py:291
  49.2 5.7 %collective-permute-start.9 = (bf16[16,3840]{1,0:T(8,128)(2,1)S(1)}, bf16[16,3840]{1,0:T(8,128)(2,1)S(1)}, u32[]{:S(2)}, u32[]{:S(2)}) collective-permute-start(bf16[16,3840]{1,0:T(8,128)(2,1)S(1)} %add_convert_fusion.2), channel_id=1, source_target_pairs={{0,2},{1,9},{2,0},{3,11},{4,6},{5,13},{6,4},{7,15},{8,10},{9,1},{1... | collective-permute-start | bytes 368648 | tf_op jit(solution)/shard_map/ppermute | solution.py:291
  54.9 4.9 %collective-permute-start.12 = (bf16[16,3840]{1,0:T(8,128)(2,1)S(1)}, bf16[16,3840]{1,0:T(8,128)(2,1)S(1)}, u32[]{:S(2)}, u32[]{:S(2)}) collective-permute-start(bf16[16,3840]{1,0:T(8,128)(2,1)S(1)} %add_convert_fusion.1), channel_id=1, source_target_pairs={{0,8},{1,3},{2,10},{3,1},{4,12},{5,7},{6,14},{7,5},{8,0},{9,11},{1... | collective-permute-start | bytes 368648 | tf_op jit(solution)/shard_map/ppermute | solution.py:291
  55.9 8.4 %collective-permute-start.13 = (bf16[16,3840]{1,0:T(8,128)(2,1)S(1)}, bf16[16,3840]{1,0:T(8,128)(2,1)S(1)}, u32[]{:S(2)}, u32[]{:S(2)}) collective-permute-start(bf16[16,3840]{1,0:T(8,128)(2,1)S(1)} %add_convert_fusion.1), channel_id=1, source_target_pairs={{0,16},{1,5},{2,18},{3,7},{4,20},{5,1},{6,22},{7,3},{8,24},{9,13},... | collective-permute-start | bytes 368648 | tf_op jit(solution)/shard_map/ppermute | solution.py:291
  57.1 7.3 %collective-permute-start.14 = (bf16[16,3840]{1,0:T(8,128)(2,1)S(1)}, bf16[16,3840]{1,0:T(8,128)(2,1)S(1)}, u32[]{:S(2)}, u32[]{:S(2)}) collective-permute-start(bf16[16,3840]{1,0:T(8,128)(2,1)S(1)} %add_convert_fusion.1), channel_id=1, source_target_pairs={{0,24},{1,7},{2,26},{3,5},{4,28},{5,3},{6,30},{7,1},{8,16},{9,15},... | collective-permute-start | bytes 368648 | tf_op jit(solution)/shard_map/ppermute | solution.py:291
  64.4 1.4 %collective-permute-start.15 = (bf16[16,3840]{1,0:T(8,128)(2,1)S(1)}, bf16[16,3840]{1,0:T(8,128)(2,1)S(1)}, u32[]{:S(2)}, u32[]{:S(2)}) collective-permute-start(bf16[16,3840]{1,0:T(8,128)(2,1)S(1)} %add_convert_fusion), channel_id=1, source_target_pairs={{0,1},{1,0},{2,3},{3,2},{4,5},{5,4},{6,7},{7,6},{8,9},{9,8},{10,11... | collective-permute-start | bytes 368648 | tf_op jit(solution)/shard_map/ppermute | solution.py:317

commit v4 on v3

--- a/solution.py
+++ b/solution.py
@@ -18,13 +18,13 @@
     images_hbm,
     cotangent_hbm,
     taps_hbm,
-    conv_bias_ref,
-    gain_ref,
-    norm_bias_ref,
+    conv_bias_hbm,
+    gain_hbm,
+    norm_bias_hbm,
     expand_hbm,
-    expand_bias_ref,
+    expand_bias_hbm,
     reduce_hbm,
-    layer_scale_ref,
+    layer_scale_hbm,
     first_hbm,
     second_hbm,
     keep_ref,
@@ -36,15 +36,22 @@
     image,
     cot,
     taps,
+    conv_bias,
+    gain,
+    norm_bias,
+    layer_scale,
+    expand_bias,
     wide,
     conv,
     expand,
     reduce,
+    back,
     first,
     second,
     low,
     high,
     sems,
+    block_sems,
 ):
     extent, channels = images_hbm.shape[1], images_hbm.shape[3]
     kernel = taps_hbm.shape[0]
@@ -53,52 +60,90 @@
     blocks = hidden_units // BLOCK
     slabs = channels // LANES
     half = keep_ref.shape[0]
-
-    def copies():
-        yield pltpu.make_async_copy(images_hbm.at[0], image, sems.at[0])
-        yield pltpu.make_async_copy(taps_hbm, taps, sems.at[1])
-        yield pltpu.make_async_copy(cotangent_hbm.at[0], cot, sems.at[2])
-        yield pltpu.make_async_copy(second_hbm, second, sems.at[3])
-        for j in range(blocks):
-            cut = pl.ds(j * BLOCK, BLOCK)
-            yield pltpu.make_async_copy(expand_hbm.at[:, cut], expand.at[:, cut], sems.at[5 + 2 * j])
-            yield pltpu.make_async_copy(reduce_hbm.at[cut, :], reduce.at[cut, :], sems.at[6 + 2 * j])
-            if j == 0:
-                yield pltpu.make_async_copy(first_hbm, first, sems.at[4])
-
-    started = list(copies())
-    for copy in started:
+    rows = extent * ROW
+    nt = (((1,), (1,)), ((), ()))
+
+    pairs = [
+        (images_hbm.at[0], image),
+        (taps_hbm, taps),
+        (cotangent_hbm.at[0], cot),
+        (layer_scale_hbm, layer_scale),
+        (conv_bias_hbm, conv_bias),
+        (gain_hbm, gain),
+        (norm_bias_hbm, norm_bias),
+        (expand_bias_hbm, expand_bias),
+        (second_hbm, second),
+        (first_hbm, first),
+        (expand_hbm, expand),
+    ]
+    copies = [pltpu.make_async_copy(src, dst, sems.at[k]) for k, (src, dst) in enumerate(pairs)]
+
+    def reduce_copy(j):
+        cut = pl.ds(pl.multiple_of(j * BLOCK, BLOCK), BLOCK)
+        return pltpu.make_async_copy(reduce_hbm.at[cut, :], reduce.at[cut, :], block_sems.at[j])
+
+    for copy in copies[:5]:
         copy.start()
-    image_copy, taps_copy, cot_copy, second_copy = started[:4]
-    rest = started[4:6] + started[7:]
-    first_copy = started[6]
+    for j in range(blocks):
+        reduce_copy(j).start()
+    for copy in copies[5:]:
+        copy.start()
 
     wide[...] = jnp.zeros(wide.shape, jnp.float32)
-    image_copy.wait()
+    grad_ref[...] = jnp.zeros(grad_ref.shape, jnp.bfloat16)
+    copies[0].wait()
     for row in range(extent):
         for slab in range(slabs):
             piece = image[row, :, slab * LANES : (slab + 1) * LANES].astype(jnp.float32)
             wide[slab, margin + row, LEFT : LEFT + extent, :] = piece
-    taps_copy.wait()
-
-    pieces = 2 if extent % 2 == 0 else 1
-    tall = extent // pieces
-    for slab in range(slabs):
-        lanes = slice(slab * LANES, (slab + 1) * LANES)
-        for piece in range(pieces):
-            top = piece * tall
-            total = jnp.broadcast_to(
-                conv_bias_ref[:, lanes].reshape(1, 1, LANES), (tall, ROW, LANES)
-            )
-            for col in range(kernel):
-                start = LEFT - margin + col
-                seen = wide[slab, top : top + tall + kernel - 1, start : start + ROW, :]
-                for row in range(kernel):
-                    tap = taps[row, col : col + 1, lanes].reshape(1, 1, LANES)
-                    total = total + seen[row : row + tall] * tap
-            conv[slab, top * ROW : (top + tall) * ROW, :] = total.reshape(tall * ROW, LANES)
-
-    rows = extent * ROW
+    copies[2].wait()
+    copies[3].wait()
+    for row in range(extent):
+        piece = cot[row].astype(jnp.float32) * layer_scale[...].reshape(1, channels)
+        grad_ref[row * ROW : row * ROW + extent, :] = piece.astype(jnp.bfloat16)
+    copies[1].wait()
+    copies[4].wait()
+
+    def conv_tile(slab, top, tall):
+        lanes = pl.ds(pl.multiple_of(slab * LANES, LANES), LANES)
+        total = jnp.broadcast_to(conv_bias[lanes].reshape(1, 1, LANES), (tall, ROW, LANES))
+        for col in range(kernel):
+            start = LEFT - margin + col
+            seen = wide[slab, pl.ds(top, tall + kernel - 1), start : start + ROW, :]
+            for row in range(kernel):
+                tap = taps[row, col : col + 1, lanes].reshape(1, 1, LANES)
+                total = total + seen[row : row + tall] * tap
+        spot = pl.ds(pl.multiple_of(top * ROW, ROW), tall * ROW)
+        conv[slab, spot, :] = total.reshape(tall * ROW, LANES)
+
+    TALL = 7
+    tiles = extent // TALL
+
+    def conv_step(step, _):
+        conv_tile(step // tiles, (step % tiles) * TALL, TALL)
+        return 0
+
+    def back_block(j):
+        reduce_copy(j).wait()
+        cut = pl.ds(pl.multiple_of(j * BLOCK, BLOCK), BLOCK)
+        back[:, cut] = lax.dot_general(
+            grad_ref[...], reduce[cut, :], nt, preferred_element_type=jnp.float32
+        )
+
+    if True:
+        per = slabs * tiles // blocks
+
+        def both_step(j, _):
+            back_block(j)
+            for k in range(per):
+                step = j * per + k
+                conv_tile(step // tiles, (step % tiles) * TALL, TALL)
+            return 0
+
+        lax.fori_loop(0, blocks, both_step, 0)
+    else:
+        lax.fori_loop(0, slabs * tiles, conv_step, 0)
+
     added = conv[0]
     for slab in range(1, slabs):
         added = added + conv[slab]
@@ -111,47 +156,45 @@
     inverse = lax.rsqrt(spread + 1e-06)
     place = lax.broadcasted_iota(jnp.int32, (rows, LANES), 0)
     real = lax.rem(place, ROW) < extent
+    for copy in copies[5:]:
+        copy.wait()
     for slab in range(slabs):
         lanes = slice(slab * LANES, (slab + 1) * LANES)
-        value = (conv[slab] - center) * inverse * gain_ref[:, lanes] + norm_bias_ref[:, lanes]
+        value = (conv[slab] - center) * inverse * gain[lanes].reshape(1, LANES) + norm_bias[lanes].reshape(1, LANES)
         normed_ref[:, lanes] = jnp.where(real, value, 0.0).astype(jnp.bfloat16)
 
-    cot_copy.wait()
-    grad_ref[...] = jnp.zeros(grad_ref.shape, jnp.bfloat16)
-    for row in range(extent):
-        piece = cot[row].astype(jnp.float32) * layer_scale_ref[...]
-        grad_ref[row * ROW : row * ROW + extent, :] = piece.astype(jnp.bfloat16)
-
-    second_copy.wait()
     normed = normed_ref[...]
-    grad = grad_ref[...]
-    thin = jnp.dot(grad, second[...].astype(jnp.bfloat16), preferred_element_type=jnp.float32)
-    thin_second = thin.T.astype(jnp.bfloat16)
-    first_copy.wait()
-    thin = jnp.zeros((rows, first.shape[1]), jnp.float32)
+    thin_second = lax.dot_general(
+        second[...].astype(jnp.bfloat16), grad_ref[...], nt, preferred_element_type=jnp.float32
+    ).astype(jnp.bfloat16)
+    thin = jnp.zeros((first.shape[0], rows), jnp.float32)
+    if False:
+        for j in range(blocks):
+            reduce_copy(j).wait()
     for j in range(blocks):
         cut = slice(j * BLOCK, (j + 1) * BLOCK)
-        rest[2 * j].wait()
         hidden = jnp.dot(normed, expand[:, cut], preferred_element_type=jnp.float32)
-        hidden = hidden + expand_bias_ref[:, cut]
-        rest[2 * j + 1].wait()
-        back = lax.dot_general(
-            grad, reduce[cut, :], (((1,), (1,)), ((), ())), preferred_element_type=jnp.float32
-        )
+        hidden = hidden + expand_bias[cut].reshape(1, BLOCK)
+        if True:
+            pulled = back[:, cut]
+        else:
+            pulled = lax.dot_general(
+                grad_ref[...], reduce[cut, :], nt, preferred_element_type=jnp.float32
+            )
         cdf = 0.5 * (1.0 + lax.erf(hidden * 0.7071067811865476))
         slope = cdf + hidden * jnp.exp(-0.5 * hidden * hidden) * 0.3989422804014327
         activated = (hidden * cdf).astype(jnp.bfloat16)
-        hid = (back * slope).astype(jnp.bfloat16)
+        hid = (pulled * slope).astype(jnp.bfloat16)
         activated_ref[:, cut] = activated
         hid_ref[:, cut] = hid
-        thin = thin + jnp.dot(
-            hid, first[cut, :].astype(jnp.bfloat16), preferred_element_type=jnp.float32
+        thin = thin + lax.dot_general(
+            first[:, cut].astype(jnp.bfloat16), hid, nt, preferred_element_type=jnp.float32
         )
         sums = jnp.dot(thin_second, activated, preferred_element_type=jnp.float32)
         spot = slice(channels + j * BLOCK, channels + (j + 1) * BLOCK)
         low[:, spot] = sums[:half]
         high[:, spot] = sums[half:]
-    sums = jnp.dot(thin.T.astype(jnp.bfloat16), normed, preferred_element_type=jnp.float32)
+    sums = jnp.dot(thin.astype(jnp.bfloat16), normed, preferred_element_type=jnp.float32)
     low[:, :channels] = sums[:half]
     high[:, :channels] = sums[half:]
     mine = mine_ref[0]
@@ -319,8 +362,12 @@
 
 
 VMEM = pl.BlockSpec(memory_space=pltpu.VMEM)
-ANY = pl.BlockSpec(memory_space=pl.ANY)
+HBM = pl.BlockSpec(memory_space=pltpu.HBM)
 SMEM = pl.BlockSpec(memory_space=pltpu.SMEM)
+
+
+def stay(value):
+    return pltpu.with_memory_space_constraint(value, pltpu.HBM)
 
 
 def shards(
@@ -357,38 +404,45 @@
             jax.ShapeDtypeStruct((rows, width), bf16),
             jax.ShapeDtypeStruct((rows, hidden_units), bf16),
         ),
-        in_specs=[SMEM, ANY, ANY, ANY, VMEM, VMEM, VMEM, ANY, VMEM, ANY, VMEM, ANY, ANY],
+        in_specs=[SMEM] + [HBM] * 12,
         out_specs=(VMEM,) * 6,
         scratch_shapes=[
             pltpu.VMEM(images.shape[1:], bf16),
             pltpu.VMEM(images.shape[1:], bf16),
             pltpu.VMEM(conv_weight.shape, f32),
+            pltpu.VMEM((width,), f32),
+            pltpu.VMEM((width,), f32),
+            pltpu.VMEM((width,), f32),
+            pltpu.VMEM((width,), f32),
+            pltpu.VMEM((hidden_units,), f32),
             pltpu.VMEM((slabs, extent + kernel - 1, 2 * ROW, LANES), f32),
             pltpu.VMEM((slabs, rows, LANES), f32),
             pltpu.VMEM(expand_weight.shape, bf16),
             pltpu.VMEM(reduce_weight.shape, bf16),
-            pltpu.VMEM(right_first.shape, f32),
-            pltpu.VMEM(right_second.shape, f32),
+            pltpu.VMEM((rows, hidden_units), f32),
+            pltpu.VMEM((rank, hidden_units), f32),
+            pltpu.VMEM((rank, width), f32),
             pltpu.VMEM((half, total), f32),
             pltpu.VMEM((half, total), f32),
-            pltpu.SemaphoreType.DMA((5 + 2 * (hidden_units // BLOCK),)),
+            pltpu.SemaphoreType.DMA((11,)),
+            pltpu.SemaphoreType.DMA((hidden_units // BLOCK,)),
         ],
         compiler_params=pltpu.CompilerParams(vmem_limit_bytes=40 * 1024 * 1024),
         name="phase_one",
     )(
         mine,
-        images,
-        cotangent,
-        conv_weight,
-        conv_bias.reshape(1, -1),
-        norm_gain.reshape(1, -1),
-        norm_bias.reshape(1, -1),
-        expand_weight,
-        expand_bias.reshape(1, -1),
-        reduce_weight,
-        layer_scale.reshape(1, -1),
-        right_first,
-        right_second,
+        stay(images),
+        stay(cotangent),
+        stay(conv_weight),
+        stay(conv_bias),
+        stay(norm_gain),
+        stay(norm_bias),
+        stay(expand_weight),
+        stay(expand_bias),
+        stay(reduce_weight),
+        stay(layer_scale),
+        stay(right_first.T),
+        stay(right_second.T),
     )
     value, other = exchange(keep, give, mine)
     keep, give = pl.pallas_call(

time: 67.4 us -> 57.2 us (0.85)
  Pallas kernels: 16.5 us -> 10.6 us
  local copies, waits for them, and re-layouts: 5.51 us -> 1.42 us
    pallas_call x1, Pallas kernels: 13.8 us -> 7.94 us  [shards(): pl.pallas_call(phase_one, out_shape=(jax.ShapeDtypeStruct((half, total),...]
    unnamed x22 -> x0, local copies, waits for them, and re-layouts: 4.08 us -> none
where the time goes in v4:
time: 57.2 us; the launch traced here: 57.1 us
  waiting for transfers between devices  26.2 us (46%)
  starting transfers between devices  17.9 us (31%)
  Pallas kernels  10.6 us (19%)
  local copies, waits for them, and re-layouts  1.42 us (2%)
  between operations  0.72 us (1%)
    ppermute x12, waiting for transfers between devices, partner(): return lax.ppermute(sent, ('outer', 'inner'), perm).astype(jnp.float32)  21.4 us
    ppermute x12, starting transfers between devices, partner(): return lax.ppermute(sent, ('outer', 'inner'), perm).astype(jnp.float32)  16.9 us
    pallas_call x1, Pallas kernels, shards(): pl.pallas_call(phase_one, out_shape=(jax.ShapeDtypeStruct((half, total),...  7.94 us
    ppermute x2, waiting for transfers between devices, exchange(): other = lax.ppermute(value, ('outer', 'inner'), pair_perm(count))  2.64 us
    pallas_call x1, Pallas kernels, shards(): pl.pallas_call(phase_two, out_shape=(jax.ShapeDtypeStruct((half, total),...  2.62 us
    ppermute x2, waiting for transfers between devices, exchange(): got = lax.ppermute(give, ('outer', 'inner'), pair_perm(count))  2.16 us
    transpose x2, local copies, waits for them, and re-layouts, shards(): return (both[:, width:].T, both[:, :width].T)  1.42 us
  transfers between devices with their start and end apart: 16, of which 15 were waited for; matrix products, arithmetic and copies ran while one was open for 0% of the time, Pallas kernels for 0%

profile of v4, /device:TPU:0, one launch (start us, length us, event | category | flops | bytes accessed | tf_op | source)
XLA Modules:
  0.0 57.1 jit_solution(4995196599643343104)
XLA Ops:
  0.6 7.9 %phase_one.1 = (f32[16,3840]{1,0:T(8,128)S(1)}, bf16[16,3840]{1,0:T(8,128)(2,1)S(1)}, bf16[224,768]{1,0:T(8,128)(2,1)S(1)}, bf16[224,3072]{1,0:T(8,128)(2,1)S(1)...) custom-call(s32[1]{0:T(128)} %bitcast.mine_ref, bf16[1,14,14,768]{3,2,1,0:T(8,128)(2,1)} %images_hbm.1, ...), custom_call_target="tpu_custom_call" | custom-call | tf_op jit(solution)/shard_map/phase_one/pallas_call | solution.py:397
  8.6 0.6 %collective-permute-start = (bf16[16,3840]{1,0:T(8,128)(2,1)S(1)}, bf16[16,3840]{1,0:T(8,128)(2,1)S(1)}, u32[]{:S(2)}, u32[]{:S(2)}) collective-permute-start(bf16[16,3840]{1,0:T(8,128)(2,1)S(1)} %get-tuple-element.11), channel_id=1, source_target_pairs={{0,1},{1,0},{2,3},{3,2},{4,5},{5,4},{6,7},{7,6},{8,9},{9,8},{10,11... | collective-permute-start | bytes 368648 | tf_op jit(solution)/shard_map/ppermute | solution.py:350
  9.2 1.0 %collective-permute-done = bf16[16,3840]{1,0:T(8,128)(2,1)S(1)} collective-permute-done((bf16[16,3840]{1,0:T(8,128)(2,1)S(1)}, bf16[16,3840]{1,0:T(8,128)(2,1)S(1)}, u32[]{:S(2)}, u32[]{:S(2)}) %collective-permute-start) | collective-permute-done | bytes 122912 | tf_op jit(solution)/shard_map/ppermute | solution.py:350
  10.2 2.9 %collective-permute-start.1 = (bf16[16,3840]{1,0:T(8,128)(2,1)S(1)}, bf16[16,3840]{1,0:T(8,128)(2,1)S(1)}, u32[]{:S(2)}, u32[]{:S(2)}) collective-permute-start(bf16[16,3840]{1,0:T(8,128)(2,1)S(1)} %add_convert_fusion.5), channel_id=1, source_target_pairs={{0,2},{1,9},{2,0},{3,11},{4,6},{5,13},{6,4},{7,15},{8,10},{9,1},{1... | collective-permute-start | bytes 368648 | tf_op jit(solution)/shard_map/ppermute | solution.py:334
  13.1 1.4 %collective-permute-start.2 = (bf16[16,3840]{1,0:T(8,128)(2,1)S(1)}, bf16[16,3840]{1,0:T(8,128)(2,1)S(1)}, u32[]{:S(2)}, u32[]{:S(2)}) collective-permute-start(bf16[16,3840]{1,0:T(8,128)(2,1)S(1)} %add_convert_fusion.5), channel_id=1, source_target_pairs={{0,4},{1,17},{2,6},{3,19},{4,0},{5,21},{6,2},{7,23},{8,12},{9,25},... | collective-permute-start | bytes 368648 | tf_op jit(solution)/shard_map/ppermute | solution.py:334
  14.6 1.3 %collective-permute-done.1 = bf16[16,3840]{1,0:T(8,128)(2,1)S(1)} collective-permute-done((bf16[16,3840]{1,0:T(8,128)(2,1)S(1)}, bf16[16,3840]{1,0:T(8,128)(2,1)S(1)}, u32[]{:S(2)}, u32[]{:S(2)}) %collective-permute-start.1) | collective-permute-done | bytes 122912 | tf_op jit(solution)/shard_map/ppermute | solution.py:334
  16.0 2.0 %collective-permute-done.2 = bf16[16,3840]{1,0:T(8,128)(2,1)S(1)} collective-permute-done((bf16[16,3840]{1,0:T(8,128)(2,1)S(1)}, bf16[16,3840]{1,0:T(8,128)(2,1)S(1)}, u32[]{:S(2)}, u32[]{:S(2)}) %collective-permute-start.2) | collective-permute-done | bytes 122912 | tf_op jit(solution)/shard_map/ppermute | solution.py:334
  18.0 2.3 %collective-permute-done.3 = bf16[16,3840]{1,0:T(8,128)(2,1)S(1)} collective-permute-done((bf16[16,3840]{1,0:T(8,128)(2,1)S(1)}, bf16[16,3840]{1,0:T(8,128)(2,1)S(1)}, u32[]{:S(2)}, u32[]{:S(2)}) %collective-permute-start.3) | collective-permute-done | bytes 122912 | tf_op jit(solution)/shard_map/ppermute | solution.py:334
  20.4 1.7 %collective-permute-start.4 = (bf16[16,3840]{1,0:T(8,128)(2,1)S(1)}, bf16[16,3840]{1,0:T(8,128)(2,1)S(1)}, u32[]{:S(2)}, u32[]{:S(2)}) collective-permute-start(bf16[16,3840]{1,0:T(8,128)(2,1)S(1)} %add_convert_fusion.4), channel_id=1, source_target_pairs={{0,8},{1,3},{2,10},{3,1},{4,12},{5,7},{6,14},{7,5},{8,0},{9,11},{1... | collective-permute-start | bytes 368648 | tf_op jit(solution)/shard_map/ppermute | solution.py:334
  22.1 2.6 %collective-permute-start.5 = (bf16[16,3840]{1,0:T(8,128)(2,1)S(1)}, bf16[16,3840]{1,0:T(8,128)(2,1)S(1)}, u32[]{:S(2)}, u32[]{:S(2)}) collective-permute-start(bf16[16,3840]{1,0:T(8,128)(2,1)S(1)} %add_convert_fusion.4), channel_id=1, source_target_pairs={{0,16},{1,5},{2,18},{3,7},{4,20},{5,1},{6,22},{7,3},{8,24},{9,13},... | collective-permute-start | bytes 368648 | tf_op jit(solution)/shard_map/ppermute | solution.py:334
  24.7 0.2 collective-permute-start.6
  24.8 0.5 collective-permute-done.4
  25.3 3.8 %collective-permute-done.5 = bf16[16,3840]{1,0:T(8,128)(2,1)S(1)} collective-permute-done((bf16[16,3840]{1,0:T(8,128)(2,1)S(1)}, bf16[16,3840]{1,0:T(8,128)(2,1)S(1)}, u32[]{:S(2)}, u32[]{:S(2)}) %collective-permute-start.5) | collective-permute-done | bytes 122912 | tf_op jit(solution)/shard_map/ppermute | solution.py:334
  29.2 2.3 %collective-permute-done.6 = bf16[16,3840]{1,0:T(8,128)(2,1)S(1)} collective-permute-done((bf16[16,3840]{1,0:T(8,128)(2,1)S(1)}, bf16[16,3840]{1,0:T(8,128)(2,1)S(1)}, u32[]{:S(2)}, u32[]{:S(2)}) %collective-permute-start.6) | collective-permute-done | bytes 122912 | tf_op jit(solution)/shard_map/ppermute | solution.py:334
  31.6 1.3 %collective-permute-done.7.other_ref = bf16[16,3840]{1,0:T(8,128)(2,1)S(1)} collective-permute-done((bf16[16,3840]{1,0:T(8,128)(2,1)S(1)}, bf16[16,3840]{1,0:T(8,128)(2,1)S(1)}, u32[]{:S(2)}, u32[]{:S(2)}) %collective-permute-start.7) | collective-permute-done | bytes 122912 | tf_op jit(solution)/shard_map/ppermute | solution.py:360
  32.9 2.6 %phase_two.1 = (f32[16,3840]{1,0:T(8,128)S(1)}, bf16[16,3840]{1,0:T(8,128)(2,1)S(1)}) custom-call(s32[1]{0:T(128)} %bitcast.mine_ref, bf16[16,3840]{1,0:T(8,128)(2,1)S(1)} %add_convert_fusion.3.value_ref, bf16[16,3840]{1,0:T(8,128)(2,1)S(1)} %collective-permute-done.7.other_ref, bf16[224,768]{1,0:T(8,128)(2,1)S(1)} %get-tuple-element.12.normed_ref, ...), custom_call_target="tpu_custom_call" | custom-call | tf_op jit(solution)/shard_map/phase_two/pallas_call | solution.py:448
  35.5 0.2 collective-permute-start.8
  35.8 1.2 %collective-permute-done.8 = bf16[16,3840]{1,0:T(8,128)(2,1)S(1)} collective-permute-done((bf16[16,3840]{1,0:T(8,128)(2,1)S(1)}, bf16[16,3840]{1,0:T(8,128)(2,1)S(1)}, u32[]{:S(2)}, u32[]{:S(2)}) %collective-permute-start.8) | collective-permute-done | bytes 122912 | tf_op jit(solution)/shard_map/ppermute | solution.py:350
  37.0 0.6 %collective-permute-start.10 = (bf16[16,3840]{1,0:T(8,128)(2,1)S(1)}, bf16[16,3840]{1,0:T(8,128)(2,1)S(1)}, u32[]{:S(2)}, u32[]{:S(2)}) collective-permute-start(bf16[16,3840]{1,0:T(8,128)(2,1)S(1)} %add_convert_fusion.2), channel_id=1, source_target_pairs={{0,4},{1,17},{2,6},{3,19},{4,0},{5,21},{6,2},{7,23},{8,12},{9,25},... | collective-permute-start | bytes 368648 | tf_op jit(solution)/shard_map/ppermute | solution.py:334
  37.6 1.4 %collective-permute-start.11 = (bf16[16,3840]{1,0:T(8,128)(2,1)S(1)}, bf16[16,3840]{1,0:T(8,128)(2,1)S(1)}, u32[]{:S(2)}, u32[]{:S(2)}) collective-permute-start(bf16[16,3840]{1,0:T(8,128)(2,1)S(1)} %add_convert_fusion.2), channel_id=1, source_target_pairs={{0,6},{1,25},{2,4},{3,27},{4,2},{5,29},{6,0},{7,31},{8,14},{9,17},... | collective-permute-start | bytes 368648 | tf_op jit(solution)/shard_map/ppermute | solution.py:334
  39.0 1.5 %collective-permute-start.9 = (bf16[16,3840]{1,0:T(8,128)(2,1)S(1)}, bf16[16,3840]{1,0:T(8,128)(2,1)S(1)}, u32[]{:S(2)}, u32[]{:S(2)}) collective-permute-start(bf16[16,3840]{1,0:T(8,128)(2,1)S(1)} %add_convert_fusion.2), channel_id=1, source_target_pairs={{0,2},{1,9},{2,0},{3,11},{4,6},{5,13},{6,4},{7,15},{8,10},{9,1},{1... | collective-permute-start | bytes 368648 | tf_op jit(solution)/shard_map/ppermute | solution.py:334
  40.5 1.4 %collective-permute-done.10 = bf16[16,3840]{1,0:T(8,128)(2,1)S(1)} collective-permute-done((bf16[16,3840]{1,0:T(8,128)(2,1)S(1)}, bf16[16,3840]{1,0:T(8,128)(2,1)S(1)}, u32[]{:S(2)}, u32[]{:S(2)}) %collective-permute-start.10) | collective-permute-done | bytes 122912 | tf_op jit(solution)/shard_map/ppermute | solution.py:334
  41.9 1.5 %collective-permute-done.11 = bf16[16,3840]{1,0:T(8,128)(2,1)S(1)} collective-permute-done((bf16[16,3840]{1,0:T(8,128)(2,1)S(1)}, bf16[16,3840]{1,0:T(8,128)(2,1)S(1)}, u32[]{:S(2)}, u32[]{:S(2)}) %collective-permute-start.11) | collective-permute-done | bytes 122912 | tf_op jit(solution)/shard_map/ppermute | solution.py:334
  43.4 1.2 %collective-permute-done.9 = bf16[16,3840]{1,0:T(8,128)(2,1)S(1)} collective-permute-done((bf16[16,3840]{1,0:T(8,128)(2,1)S(1)}, bf16[16,3840]{1,0:T(8,128)(2,1)S(1)}, u32[]{:S(2)}, u32[]{:S(2)}) %collective-permute-start.9) | collective-permute-done | bytes 122912 | tf_op jit(solution)/shard_map/ppermute | solution.py:334
  44.7 1.0 %collective-permute-start.12 = (bf16[16,3840]{1,0:T(8,128)(2,1)S(1)}, bf16[16,3840]{1,0:T(8,128)(2,1)S(1)}, u32[]{:S(2)}, u32[]{:S(2)}) collective-permute-start(bf16[16,3840]{1,0:T(8,128)(2,1)S(1)} %add_convert_fusion.1), channel_id=1, source_target_pairs={{0,8},{1,3},{2,10},{3,1},{4,12},{5,7},{6,14},{7,5},{8,0},{9,11},{1... | collective-permute-start | bytes 368648 | tf_op jit(solution)/shard_map/ppermute | solution.py:334
  45.7 1.2 %collective-permute-start.13 = (bf16[16,3840]{1,0:T(8,128)(2,1)S(1)}, bf16[16,3840]{1,0:T(8,128)(2,1)S(1)}, u32[]{:S(2)}, u32[]{:S(2)}) collective-permute-start(bf16[16,3840]{1,0:T(8,128)(2,1)S(1)} %add_convert_fusion.1), channel_id=1, source_target_pairs={{0,16},{1,5},{2,18},{3,7},{4,20},{5,1},{6,22},{7,3},{8,24},{9,13},... | collective-permute-start | bytes 368648 | tf_op jit(solution)/shard_map/ppermute | solution.py:334
  46.9 2.3 %collective-permute-start.14 = (bf16[16,3840]{1,0:T(8,128)(2,1)S(1)}, bf16[16,3840]{1,0:T(8,128)(2,1)S(1)}, u32[]{:S(2)}, u32[]{:S(2)}) collective-permute-start(bf16[16,3840]{1,0:T(8,128)(2,1)S(1)} %add_convert_fusion.1), channel_id=1, source_target_pairs={{0,24},{1,7},{2,26},{3,5},{4,28},{5,3},{6,30},{7,1},{8,16},{9,15},... | collective-permute-start | bytes 368648 | tf_op jit(solution)/shard_map/ppermute | solution.py:334
  49.2 0.5 collective-permute-done.12
  49.7 4.5 %collective-permute-done.13 = bf16[16,3840]{1,0:T(8,128)(2,1)S(1)} collective-permute-done((bf16[16,3840]{1,0:T(8,128)(2,1)S(1)}, bf16[16,3840]{1,0:T(8,128)(2,1)S(1)}, u32[]{:S(2)}, u32[]{:S(2)}) %collective-permute-start.13) | collective-permute-done | bytes 122912 | tf_op jit(solution)/shard_map/ppermute | solution.py:334
  54.3 1.3 %collective-permute-done.15 = bf16[16,3840]{1,0:T(8,128)(2,1)S(1)} collective-permute-done((bf16[16,3840]{1,0:T(8,128)(2,1)S(1)}, bf16[16,3840]{1,0:T(8,128)(2,1)S(1)}, u32[]{:S(2)}, u32[]{:S(2)}) %collective-permute-start.15) | collective-permute-done | bytes 122912 | tf_op jit(solution)/shard_map/ppermute | solution.py:360
  55.7 0.8 %slice_bitcast_fusion = f32[3072,32]{0,1:T(8,128)} fusion(f32[32,3840]{1,0:T(8,128)S(1)} %convert_multiply_fusion), kind=kLoop, calls=%fused_computation.1 | loop fusion | bytes 786432 | tf_op jit(solution)/shard_map/transpose | solution.py:463
  56.4 0.6 %slice_bitcast_fusion.1 = f32[768,32]{0,1:T(8,128)} fusion(f32[32,3840]{1,0:T(8,128)S(1)} %convert_multiply_fusion), kind=kLoop, calls=%fused_computation.10 | loop fusion | bytes 196608 | tf_op jit(solution)/shard_map/transpose | solution.py:463
  (12 shorter events, 0.6 us)
Async XLA Ops:
  8.6 1.6 %collective-permute-start = (bf16[16,3840]{1,0:T(8,128)(2,1)S(1)}, bf16[16,3840]{1,0:T(8,128)(2,1)S(1)}, u32[]{:S(2)}, u32[]{:S(2)}) collective-permute-start(bf16[16,3840]{1,0:T(8,128)(2,1)S(1)} %get-tuple-element.11), channel_id=1, source_target_pairs={{0,1},{1,0},{2,3},{3,2},{4,5},{5,4},{6,7},{7,6},{8,9},{9,8},{10,11... | collective-permute-start | bytes 368648 | tf_op jit(solution)/shard_map/ppermute | solution.py:350
  10.2 5.8 %collective-permute-start.1 = (bf16[16,3840]{1,0:T(8,128)(2,1)S(1)}, bf16[16,3840]{1,0:T(8,128)(2,1)S(1)}, u32[]{:S(2)}, u32[]{:S(2)}) collective-permute-start(bf16[16,3840]{1,0:T(8,128)(2,1)S(1)} %add_convert_fusion.5), channel_id=1, source_target_pairs={{0,2},{1,9},{2,0},{3,11},{4,6},{5,13},{6,4},{7,15},{8,10},{9,1},{1... | collective-permute-start | bytes 368648 | tf_op jit(solution)/shard_map/ppermute | solution.py:334
  13.1 4.9 %collective-permute-start.2 = (bf16[16,3840]{1,0:T(8,128)(2,1)S(1)}, bf16[16,3840]{1,0:T(8,128)(2,1)S(1)}, u32[]{:S(2)}, u32[]{:S(2)}) collective-permute-start(bf16[16,3840]{1,0:T(8,128)(2,1)S(1)} %add_convert_fusion.5), channel_id=1, source_target_pairs={{0,4},{1,17},{2,6},{3,19},{4,0},{5,21},{6,2},{7,23},{8,12},{9,25},... | collective-permute-start | bytes 368648 | tf_op jit(solution)/shard_map/ppermute | solution.py:334
  14.5 5.8 %collective-permute-start.3 = (bf16[16,3840]{1,0:T(8,128)(2,1)S(1)}, bf16[16,3840]{1,0:T(8,128)(2,1)S(1)}, u32[]{:S(2)}, u32[]{:S(2)}) collective-permute-start(bf16[16,3840]{1,0:T(8,128)(2,1)S(1)} %add_convert_fusion.5), channel_id=1, source_target_pairs={{0,6},{1,25},{2,4},{3,27},{4,2},{5,29},{6,0},{7,31},{8,14},{9,17},... | collective-permute-start | bytes 368648 | tf_op jit(solution)/shard_map/ppermute | solution.py:334
  20.4 4.9 %collective-permute-start.4 = (bf16[16,3840]{1,0:T(8,128)(2,1)S(1)}, bf16[16,3840]{1,0:T(8,128)(2,1)S(1)}, u32[]{:S(2)}, u32[]{:S(2)}) collective-permute-start(bf16[16,3840]{1,0:T(8,128)(2,1)S(1)} %add_convert_fusion.4), channel_id=1, source_target_pairs={{0,8},{1,3},{2,10},{3,1},{4,12},{5,7},{6,14},{7,5},{8,0},{9,11},{1... | collective-permute-start | bytes 368648 | tf_op jit(solution)/shard_map/ppermute | solution.py:334
  22.1 7.1 %collective-permute-start.5 = (bf16[16,3840]{1,0:T(8,128)(2,1)S(1)}, bf16[16,3840]{1,0:T(8,128)(2,1)S(1)}, u32[]{:S(2)}, u32[]{:S(2)}) collective-permute-start(bf16[16,3840]{1,0:T(8,128)(2,1)S(1)} %add_convert_fusion.4), channel_id=1, source_target_pairs={{0,16},{1,5},{2,18},{3,7},{4,20},{5,1},{6,22},{7,3},{8,24},{9,13},... | collective-permute-start | bytes 368648 | tf_op jit(solution)/shard_map/ppermute | solution.py:334
  24.7 6.8 %collective-permute-start.6 = (bf16[16,3840]{1,0:T(8,128)(2,1)S(1)}, bf16[16,3840]{1,0:T(8,128)(2,1)S(1)}, u32[]{:S(2)}, u32[]{:S(2)}) collective-permute-start(bf16[16,3840]{1,0:T(8,128)(2,1)S(1)} %add_convert_fusion.4), channel_id=1, source_target_pairs={{0,24},{1,7},{2,26},{3,5},{4,28},{5,3},{6,30},{7,1},{8,16},{9,15},... | collective-permute-start | bytes 368648 | tf_op jit(solution)/shard_map/ppermute | solution.py:334
  31.5 1.4 %collective-permute-start.7 = (bf16[16,3840]{1,0:T(8,128)(2,1)S(1)}, bf16[16,3840]{1,0:T(8,128)(2,1)S(1)}, u32[]{:S(2)}, u32[]{:S(2)}) collective-permute-start(bf16[16,3840]{1,0:T(8,128)(2,1)S(1)} %add_convert_fusion.3.value_ref), channel_id=1, source_target_pairs={{0,1},{1,0},{2,3},{3,2},{4,5},{5,4},{6,7},{7,6},{8,9},{9,8},{10,11... | collective-permute-start | bytes 368648 | tf_op jit(solution)/shard_map/ppermute | solution.py:360
  35.5 1.4 %collective-permute-start.8 = (bf16[16,3840]{1,0:T(8,128)(2,1)S(1)}, bf16[16,3840]{1,0:T(8,128)(2,1)S(1)}, u32[]{:S(2)}, u32[]{:S(2)}) collective-permute-start(bf16[16,3840]{1,0:T(8,128)(2,1)S(1)} %get-tuple-element.17), channel_id=1, source_target_pairs={{0,1},{1,0},{2,3},{3,2},{4,5},{5,4},{6,7},{7,6},{8,9},{9,8},{10,11... | collective-permute-start | bytes 368648 | tf_op jit(solution)/shard_map/ppermute | solution.py:350
  37.0 4.9 %collective-permute-start.10 = (bf16[16,3840]{1,0:T(8,128)(2,1)S(1)}, bf16[16,3840]{1,0:T(8,128)(2,1)S(1)}, u32[]{:S(2)}, u32[]{:S(2)}) collective-permute-start(bf16[16,3840]{1,0:T(8,128)(2,1)S(1)} %add_convert_fusion.2), channel_id=1, source_target_pairs={{0,4},{1,17},{2,6},{3,19},{4,0},{5,21},{6,2},{7,23},{8,12},{9,25},... | collective-permute-start | bytes 368648 | tf_op jit(solution)/shard_map/ppermute | solution.py:334
  37.6 5.9 %collective-permute-start.11 = (bf16[16,3840]{1,0:T(8,128)(2,1)S(1)}, bf16[16,3840]{1,0:T(8,128)(2,1)S(1)}, u32[]{:S(2)}, u32[]{:S(2)}) collective-permute-start(bf16[16,3840]{1,0:T(8,128)(2,1)S(1)} %add_convert_fusion.2), channel_id=1, source_target_pairs={{0,6},{1,25},{2,4},{3,27},{4,2},{5,29},{6,0},{7,31},{8,14},{9,17},... | collective-permute-start | bytes 368648 | tf_op jit(solution)/shard_map/ppermute | solution.py:334
  39.0 5.7 %collective-permute-start.9 = (bf16[16,3840]{1,0:T(8,128)(2,1)S(1)}, bf16[16,3840]{1,0:T(8,128)(2,1)S(1)}, u32[]{:S(2)}, u32[]{:S(2)}) collective-permute-start(bf16[16,3840]{1,0:T(8,128)(2,1)S(1)} %add_convert_fusion.2), channel_id=1, source_target_pairs={{0,2},{1,9},{2,0},{3,11},{4,6},{5,13},{6,4},{7,15},{8,10},{9,1},{1... | collective-permute-start | bytes 368648 | tf_op jit(solution)/shard_map/ppermute | solution.py:334
  44.7 4.9 %collective-permute-start.12 = (bf16[16,3840]{1,0:T(8,128)(2,1)S(1)}, bf16[16,3840]{1,0:T(8,128)(2,1)S(1)}, u32[]{:S(2)}, u32[]{:S(2)}) collective-permute-start(bf16[16,3840]{1,0:T(8,128)(2,1)S(1)} %add_convert_fusion.1), channel_id=1, source_target_pairs={{0,8},{1,3},{2,10},{3,1},{4,12},{5,7},{6,14},{7,5},{8,0},{9,11},{1... | collective-permute-start | bytes 368648 | tf_op jit(solution)/shard_map/ppermute | solution.py:334
  45.7 8.4 %collective-permute-start.13 = (bf16[16,3840]{1,0:T(8,128)(2,1)S(1)}, bf16[16,3840]{1,0:T(8,128)(2,1)S(1)}, u32[]{:S(2)}, u32[]{:S(2)}) collective-permute-start(bf16[16,3840]{1,0:T(8,128)(2,1)S(1)} %add_convert_fusion.1), channel_id=1, source_target_pairs={{0,16},{1,5},{2,18},{3,7},{4,20},{5,1},{6,22},{7,3},{8,24},{9,13},... | collective-permute-start | bytes 368648 | tf_op jit(solution)/shard_map/ppermute | solution.py:334
  46.9 7.3 %collective-permute-start.14 = (bf16[16,3840]{1,0:T(8,128)(2,1)S(1)}, bf16[16,3840]{1,0:T(8,128)(2,1)S(1)}, u32[]{:S(2)}, u32[]{:S(2)}) collective-permute-start(bf16[16,3840]{1,0:T(8,128)(2,1)S(1)} %add_convert_fusion.1), channel_id=1, source_target_pairs={{0,24},{1,7},{2,26},{3,5},{4,28},{5,3},{6,30},{7,1},{8,16},{9,15},... | collective-permute-start | bytes 368648 | tf_op jit(solution)/shard_map/ppermute | solution.py:334
  54.2 1.4 %collective-permute-start.15 = (bf16[16,3840]{1,0:T(8,128)(2,1)S(1)}, bf16[16,3840]{1,0:T(8,128)(2,1)S(1)}, u32[]{:S(2)}, u32[]{:S(2)}) collective-permute-start(bf16[16,3840]{1,0:T(8,128)(2,1)S(1)} %add_convert_fusion), channel_id=1, source_target_pairs={{0,1},{1,0},{2,3},{3,2},{4,5},{5,4},{6,7},{7,6},{8,9},{9,8},{10,11... | collective-permute-start | bytes 368648 | tf_op jit(solution)/shard_map/ppermute | solution.py:360

commit v5 on v4

--- a/solution.py
+++ b/solution.py
@@ -11,6 +11,8 @@
 ROW = 16
 LEFT = 8
 BLOCK = 512
+TALL = 7
+PIECE = 1024
 
 
 def phase_one(
@@ -116,33 +118,22 @@
         spot = pl.ds(pl.multiple_of(top * ROW, ROW), tall * ROW)
         conv[slab, spot, :] = total.reshape(tall * ROW, LANES)
 
-    TALL = 7
     tiles = extent // TALL
-
-    def conv_step(step, _):
-        conv_tile(step // tiles, (step % tiles) * TALL, TALL)
-        return 0
-
-    def back_block(j):
+    per = slabs * tiles // blocks
+    assert tiles * TALL == extent and per * blocks == slabs * tiles
+
+    def both_step(j, _):
         reduce_copy(j).wait()
         cut = pl.ds(pl.multiple_of(j * BLOCK, BLOCK), BLOCK)
         back[:, cut] = lax.dot_general(
             grad_ref[...], reduce[cut, :], nt, preferred_element_type=jnp.float32
         )
-
-    if True:
-        per = slabs * tiles // blocks
-
-        def both_step(j, _):
-            back_block(j)
-            for k in range(per):
-                step = j * per + k
-                conv_tile(step // tiles, (step % tiles) * TALL, TALL)
-            return 0
-
-        lax.fori_loop(0, blocks, both_step, 0)
-    else:
-        lax.fori_loop(0, slabs * tiles, conv_step, 0)
+        for k in range(per):
+            step = j * per + k
+            conv_tile(step // tiles, (step % tiles) * TALL, TALL)
+        return 0
+
+    lax.fori_loop(0, blocks, both_step, 0)
 
     added = conv[0]
     for slab in range(1, slabs):
@@ -168,30 +159,21 @@
         second[...].astype(jnp.bfloat16), grad_ref[...], nt, preferred_element_type=jnp.float32
     ).astype(jnp.bfloat16)
     thin = jnp.zeros((first.shape[0], rows), jnp.float32)
-    if False:
-        for j in range(blocks):
-            reduce_copy(j).wait()
-    for j in range(blocks):
-        cut = slice(j * BLOCK, (j + 1) * BLOCK)
+    for start in range(0, hidden_units, PIECE):
+        cut = slice(start, start + PIECE)
         hidden = jnp.dot(normed, expand[:, cut], preferred_element_type=jnp.float32)
-        hidden = hidden + expand_bias[cut].reshape(1, BLOCK)
-        if True:
-            pulled = back[:, cut]
-        else:
-            pulled = lax.dot_general(
-                grad_ref[...], reduce[cut, :], nt, preferred_element_type=jnp.float32
-            )
+        hidden = hidden + expand_bias[cut].reshape(1, PIECE)
         cdf = 0.5 * (1.0 + lax.erf(hidden * 0.7071067811865476))
         slope = cdf + hidden * jnp.exp(-0.5 * hidden * hidden) * 0.3989422804014327
         activated = (hidden * cdf).astype(jnp.bfloat16)
-        hid = (pulled * slope).astype(jnp.bfloat16)
+        hid = (back[:, cut] * slope).astype(jnp.bfloat16)
         activated_ref[:, cut] = activated
         hid_ref[:, cut] = hid
         thin = thin + lax.dot_general(
             first[:, cut].astype(jnp.bfloat16), hid, nt, preferred_element_type=jnp.float32
         )
         sums = jnp.dot(thin_second, activated, preferred_element_type=jnp.float32)
-        spot = slice(channels + j * BLOCK, channels + (j + 1) * BLOCK)
+        spot = slice(channels + start, channels + start + PIECE)
         low[:, spot] = sums[:half]
         high[:, spot] = sums[half:]
     sums = jnp.dot(thin.astype(jnp.bfloat16), normed, preferred_element_type=jnp.float32)
@@ -270,6 +252,28 @@
         give_ref[:, spot] = jnp.where(mine == 0, piece[half:], piece[:half]).astype(jnp.bfloat16)
 
 
+def phase_three(
+    factor, mine_ref, value_ref, other_ref, second_hbm, first_hbm, second, first, sems
+):
+    half, channels = value_ref.shape[0], second.shape[1]
+    mine = mine_ref[0]
+    copies = (
+        pltpu.make_async_copy(first, first_hbm, sems.at[0]),
+        pltpu.make_async_copy(second, second_hbm, sems.at[1]),
+    )
+    for spot, target, copy in (
+        (slice(channels, None), first, copies[0]),
+        (slice(0, channels), second, copies[1]),
+    ):
+        value = value_ref[:, spot].astype(jnp.float32) * factor
+        other = other_ref[:, spot].astype(jnp.float32) * factor
+        target[:half, :] = jnp.where(mine == 0, value, other)
+        target[half:, :] = jnp.where(mine == 0, other, value)
+        copy.start()
+    for copy in copies:
+        copy.wait()
+
+
 def digits(size):
     found = []
     factor = 2
@@ -385,7 +389,7 @@
     right_second,
 ):
     count = lax.axis_size("outer") * lax.axis_size("inner")
-    scale = jnp.float32(1.0) / count
+    scale = 1.0 / count
     extent, width = images.shape[1], images.shape[3]
     kernel = conv_weight.shape[0]
     hidden_units = expand_weight.shape[1]
@@ -457,10 +461,23 @@
         name="phase_two",
     )(mine, value, other, normed, activated, grad, hid)
     value, other = exchange(keep, give, mine)
-    low = jnp.where(mine[0] == 0, value, other)
-    high = jnp.where(mine[0] == 0, other, value)
-    both = jnp.concatenate([low, high], axis=0).astype(f32) * scale
-    return (both[:, width:].T, both[:, :width].T)
+    second, first = pl.pallas_call(
+        functools.partial(phase_three, scale),
+        out_shape=(
+            jax.ShapeDtypeStruct((rank, width), f32),
+            jax.ShapeDtypeStruct((rank, hidden_units), f32),
+        ),
+        in_specs=[SMEM, VMEM, VMEM],
+        out_specs=(HBM, HBM),
+        scratch_shapes=[
+            pltpu.VMEM((rank, width), f32),
+            pltpu.VMEM((rank, hidden_units), f32),
+            pltpu.SemaphoreType.DMA((2,)),
+        ],
+        compiler_params=pltpu.CompilerParams(vmem_limit_bytes=8 * 1024 * 1024),
+        name="phase_three",
+    )(mine, value, other)
+    return (first.T, second.T)
 
 
 def solution(mesh):

time: 57.2 us -> 53.7 us (0.939)
  waiting for transfers between devices: 26.2 us -> 23.9 us
  local copies, waits for them, and re-layouts: 1.42 us -> 0 us
    ppermute x12, waiting for transfers between devices: 21.4 us -> 19.1 us  [partner(): return lax.ppermute(sent, ('outer', 'inner'), perm).astype(jnp.float32)]
    transpose x2 -> x0, local copies, waits for them, and re-layouts: 1.42 us -> none  [shards(): return (both[:, width:].T, both[:, :width].T)]
    pallas_call x0 -> x1, Pallas kernels: none -> 0.83 us  [shards(): pl.pallas_call(functools.partial(phase_three, scale), out_shape=(jax.Shap...]
    pallas_call x1, Pallas kernels: 7.94 us -> 7.35 us  [shards(): pl.pallas_call(phase_one, out_shape=(jax.ShapeDtypeStruct((half, total),...]
  transfers between devices with their start and end apart: 16 -> 16, of which waited for: 15 -> 14; matrix products, arithmetic and copies ran while one was open for 0% -> 0% of each run, Pallas kernels for 0% -> 0%
where the time goes in v5:
time: 53.7 us; the launch traced here: 53.5 us
  waiting for transfers between devices  23.9 us (45%)
  starting transfers between devices  17.8 us (33%)
  Pallas kernels  10.8 us (20%)
  between operations  0.71 us (1%)
    ppermute x12, waiting for transfers between devices, partner(): return lax.ppermute(sent, ('outer', 'inner'), perm).astype(jnp.float32)  19.1 us
    ppermute x12, starting transfers between devices, partner(): return lax.ppermute(sent, ('outer', 'inner'), perm).astype(jnp.float32)  16.9 us
    pallas_call x1, Pallas kernels, shards(): pl.pallas_call(phase_one, out_shape=(jax.ShapeDtypeStruct((half, total),...  7.35 us
    ppermute x2, waiting for transfers between devices, exchange(): other = lax.ppermute(value, ('outer', 'inner'), pair_perm(count))  2.65 us
    pallas_call x1, Pallas kernels, shards(): pl.pallas_call(phase_two, out_shape=(jax.ShapeDtypeStruct((half, total),...  2.62 us
    ppermute x2, waiting for transfers between devices, exchange(): got = lax.ppermute(give, ('outer', 'inner'), pair_perm(count))  2.16 us
  transfers between devices with their start and end apart: 16, of which 14 were waited for; matrix products, arithmetic and copies ran while one was open for 0% of the time, Pallas kernels for 0%

profile of v5, /device:TPU:0, one launch (start us, length us, event | category | flops | bytes accessed | tf_op | source)
XLA Modules:
  0.0 53.5 jit_solution(10909634144241441658)
XLA Ops:
  0.6 7.3 %phase_one.1 = (f32[16,3840]{1,0:T(8,128)S(1)}, bf16[16,3840]{1,0:T(8,128)(2,1)S(1)}, bf16[224,768]{1,0:T(8,128)(2,1)S(1)}, bf16[224,3072]{1,0:T(8,128)(2,1)S(1)...) custom-call(s32[1]{0:T(128)} %bitcast.mine_ref, bf16[1,14,14,768]{3,2,1,0:T(8,128)(2,1)} %images_hbm.1, ...), custom_call_target="tpu_custom_call" | custom-call | tf_op jit(solution)/shard_map/phase_one/pallas_call | solution.py:401
  8.0 0.6 %collective-permute-start = (bf16[16,3840]{1,0:T(8,128)(2,1)S(1)}, bf16[16,3840]{1,0:T(8,128)(2,1)S(1)}, u32[]{:S(2)}, u32[]{:S(2)}) collective-permute-start(bf16[16,3840]{1,0:T(8,128)(2,1)S(1)} %get-tuple-element.13), channel_id=1, source_target_pairs={{0,1},{1,0},{2,3},{3,2},{4,5},{5,4},{6,7},{7,6},{8,9},{9,8},{10,11... | collective-permute-start | bytes 368648 | tf_op jit(solution)/shard_map/ppermute | solution.py:354
  8.6 1.0 %collective-permute-done = bf16[16,3840]{1,0:T(8,128)(2,1)S(1)} collective-permute-done((bf16[16,3840]{1,0:T(8,128)(2,1)S(1)}, bf16[16,3840]{1,0:T(8,128)(2,1)S(1)}, u32[]{:S(2)}, u32[]{:S(2)}) %collective-permute-start) | collective-permute-done | bytes 122912 | tf_op jit(solution)/shard_map/ppermute | solution.py:354
  9.6 3.8 %collective-permute-start.3 = (bf16[16,3840]{1,0:T(8,128)(2,1)S(1)}, bf16[16,3840]{1,0:T(8,128)(2,1)S(1)}, u32[]{:S(2)}, u32[]{:S(2)}) collective-permute-start(bf16[16,3840]{1,0:T(8,128)(2,1)S(1)} %add_convert_fusion.5), channel_id=1, source_target_pairs={{0,6},{1,25},{2,4},{3,27},{4,2},{5,29},{6,0},{7,31},{8,14},{9,17},... | collective-permute-start | bytes 368648 | tf_op jit(solution)/shard_map/ppermute | solution.py:338
  13.4 0.6 %collective-permute-start.2 = (bf16[16,3840]{1,0:T(8,128)(2,1)S(1)}, bf16[16,3840]{1,0:T(8,128)(2,1)S(1)}, u32[]{:S(2)}, u32[]{:S(2)}) collective-permute-start(bf16[16,3840]{1,0:T(8,128)(2,1)S(1)} %add_convert_fusion.5), channel_id=1, source_target_pairs={{0,4},{1,17},{2,6},{3,19},{4,0},{5,21},{6,2},{7,23},{8,12},{9,25},... | collective-permute-start | bytes 368648 | tf_op jit(solution)/shard_map/ppermute | solution.py:338
  14.0 2.2 %collective-permute-done.3 = bf16[16,3840]{1,0:T(8,128)(2,1)S(1)} collective-permute-done((bf16[16,3840]{1,0:T(8,128)(2,1)S(1)}, bf16[16,3840]{1,0:T(8,128)(2,1)S(1)}, u32[]{:S(2)}, u32[]{:S(2)}) %collective-permute-start.3) | collective-permute-done | bytes 122912 | tf_op jit(solution)/shard_map/ppermute | solution.py:338
  16.2 2.0 %collective-permute-done.2 = bf16[16,3840]{1,0:T(8,128)(2,1)S(1)} collective-permute-done((bf16[16,3840]{1,0:T(8,128)(2,1)S(1)}, bf16[16,3840]{1,0:T(8,128)(2,1)S(1)}, u32[]{:S(2)}, u32[]{:S(2)}) %collective-permute-start.2) | collective-permute-done | bytes 122912 | tf_op jit(solution)/shard_map/ppermute | solution.py:338
  18.2 0.6 %collective-permute-done.1 = bf16[16,3840]{1,0:T(8,128)(2,1)S(1)} collective-permute-done((bf16[16,3840]{1,0:T(8,128)(2,1)S(1)}, bf16[16,3840]{1,0:T(8,128)(2,1)S(1)}, u32[]{:S(2)}, u32[]{:S(2)}) %collective-permute-start.1) | collective-permute-done | bytes 122912 | tf_op jit(solution)/shard_map/ppermute | solution.py:338
  18.9 3.7 %collective-permute-start.6 = (bf16[16,3840]{1,0:T(8,128)(2,1)S(1)}, bf16[16,3840]{1,0:T(8,128)(2,1)S(1)}, u32[]{:S(2)}, u32[]{:S(2)}) collective-permute-start(bf16[16,3840]{1,0:T(8,128)(2,1)S(1)} %add_convert_fusion.4), channel_id=1, source_target_pairs={{0,24},{1,7},{2,26},{3,5},{4,28},{5,3},{6,30},{7,1},{8,16},{9,15},... | collective-permute-start | bytes 368648 | tf_op jit(solution)/shard_map/ppermute | solution.py:338
  22.6 0.8 %collective-permute-start.4 = (bf16[16,3840]{1,0:T(8,128)(2,1)S(1)}, bf16[16,3840]{1,0:T(8,128)(2,1)S(1)}, u32[]{:S(2)}, u32[]{:S(2)}) collective-permute-start(bf16[16,3840]{1,0:T(8,128)(2,1)S(1)} %add_convert_fusion.4), channel_id=1, source_target_pairs={{0,8},{1,3},{2,10},{3,1},{4,12},{5,7},{6,14},{7,5},{8,0},{9,11},{1... | collective-permute-start | bytes 368648 | tf_op jit(solution)/shard_map/ppermute | solution.py:338
  23.4 2.4 %collective-permute-done.6 = bf16[16,3840]{1,0:T(8,128)(2,1)S(1)} collective-permute-done((bf16[16,3840]{1,0:T(8,128)(2,1)S(1)}, bf16[16,3840]{1,0:T(8,128)(2,1)S(1)}, u32[]{:S(2)}, u32[]{:S(2)}) %collective-permute-start.6) | collective-permute-done | bytes 122912 | tf_op jit(solution)/shard_map/ppermute | solution.py:338
  25.7 3.1 %collective-permute-done.5 = bf16[16,3840]{1,0:T(8,128)(2,1)S(1)} collective-permute-done((bf16[16,3840]{1,0:T(8,128)(2,1)S(1)}, bf16[16,3840]{1,0:T(8,128)(2,1)S(1)}, u32[]{:S(2)}, u32[]{:S(2)}) %collective-permute-start.5) | collective-permute-done | bytes 122912 | tf_op jit(solution)/shard_map/ppermute | solution.py:338
  28.9 0.1 collective-permute-start.7
  29.0 1.3 %collective-permute-done.7.other_ref = bf16[16,3840]{1,0:T(8,128)(2,1)S(1)} collective-permute-done((bf16[16,3840]{1,0:T(8,128)(2,1)S(1)}, bf16[16,3840]{1,0:T(8,128)(2,1)S(1)}, u32[]{:S(2)}, u32[]{:S(2)}) %collective-permute-start.7) | collective-permute-done | bytes 122912 | tf_op jit(solution)/shard_map/ppermute | solution.py:364
  30.3 2.6 %phase_two.1 = (f32[16,3840]{1,0:T(8,128)S(1)}, bf16[16,3840]{1,0:T(8,128)(2,1)S(1)}) custom-call(s32[1]{0:T(128)} %bitcast.mine_ref, bf16[16,3840]{1,0:T(8,128)(2,1)S(1)} %add_convert_fusion.3.value_ref, bf16[16,3840]{1,0:T(8,128)(2,1)S(1)} %collective-permute-done.7.other_ref, bf16[224,768]{1,0:T(8,128)(2,1)S(1)} %get-tuple-element.14.normed_ref, ...), custom_call_target="tpu_custom_call" | custom-call | tf_op jit(solution)/shard_map/phase_two/pallas_call | solution.py:452
  32.9 0.2 collective-permute-start.8
  33.1 1.2 %collective-permute-done.8 = bf16[16,3840]{1,0:T(8,128)(2,1)S(1)} collective-permute-done((bf16[16,3840]{1,0:T(8,128)(2,1)S(1)}, bf16[16,3840]{1,0:T(8,128)(2,1)S(1)}, u32[]{:S(2)}, u32[]{:S(2)}) %collective-permute-start.8) | collective-permute-done | bytes 122912 | tf_op jit(solution)/shard_map/ppermute | solution.py:354
  34.3 1.7 %collective-permute-start.11 = (bf16[16,3840]{1,0:T(8,128)(2,1)S(1)}, bf16[16,3840]{1,0:T(8,128)(2,1)S(1)}, u32[]{:S(2)}, u32[]{:S(2)}) collective-permute-start(bf16[16,3840]{1,0:T(8,128)(2,1)S(1)} %add_convert_fusion.2), channel_id=1, source_target_pairs={{0,6},{1,25},{2,4},{3,27},{4,2},{5,29},{6,0},{7,31},{8,14},{9,17},... | collective-permute-start | bytes 368648 | tf_op jit(solution)/shard_map/ppermute | solution.py:338
  36.1 0.5 %collective-permute-start.10 = (bf16[16,3840]{1,0:T(8,128)(2,1)S(1)}, bf16[16,3840]{1,0:T(8,128)(2,1)S(1)}, u32[]{:S(2)}, u32[]{:S(2)}) collective-permute-start(bf16[16,3840]{1,0:T(8,128)(2,1)S(1)} %add_convert_fusion.2), channel_id=1, source_target_pairs={{0,4},{1,17},{2,6},{3,19},{4,0},{5,21},{6,2},{7,23},{8,12},{9,25},... | collective-permute-start | bytes 368648 | tf_op jit(solution)/shard_map/ppermute | solution.py:338
  36.6 1.3 %collective-permute-start.9 = (bf16[16,3840]{1,0:T(8,128)(2,1)S(1)}, bf16[16,3840]{1,0:T(8,128)(2,1)S(1)}, u32[]{:S(2)}, u32[]{:S(2)}) collective-permute-start(bf16[16,3840]{1,0:T(8,128)(2,1)S(1)} %add_convert_fusion.2), channel_id=1, source_target_pairs={{0,2},{1,9},{2,0},{3,11},{4,6},{5,13},{6,4},{7,15},{8,10},{9,1},{1... | collective-permute-start | bytes 368648 | tf_op jit(solution)/shard_map/ppermute | solution.py:338
  37.9 2.3 %collective-permute-done.11 = bf16[16,3840]{1,0:T(8,128)(2,1)S(1)} collective-permute-done((bf16[16,3840]{1,0:T(8,128)(2,1)S(1)}, bf16[16,3840]{1,0:T(8,128)(2,1)S(1)}, u32[]{:S(2)}, u32[]{:S(2)}) %collective-permute-start.11) | collective-permute-done | bytes 122912 | tf_op jit(solution)/shard_map/ppermute | solution.py:338
  40.2 0.8 %collective-permute-done.10 = bf16[16,3840]{1,0:T(8,128)(2,1)S(1)} collective-permute-done((bf16[16,3840]{1,0:T(8,128)(2,1)S(1)}, bf16[16,3840]{1,0:T(8,128)(2,1)S(1)}, u32[]{:S(2)}, u32[]{:S(2)}) %collective-permute-start.10) | collective-permute-done | bytes 122912 | tf_op jit(solution)/shard_map/ppermute | solution.py:338
  41.0 0.5 %collective-permute-done.9 = bf16[16,3840]{1,0:T(8,128)(2,1)S(1)} collective-permute-done((bf16[16,3840]{1,0:T(8,128)(2,1)S(1)}, bf16[16,3840]{1,0:T(8,128)(2,1)S(1)}, u32[]{:S(2)}, u32[]{:S(2)}) %collective-permute-start.9) | collective-permute-done | bytes 122912 | tf_op jit(solution)/shard_map/ppermute | solution.py:338
  41.6 2.5 %collective-permute-start.14 = (bf16[16,3840]{1,0:T(8,128)(2,1)S(1)}, bf16[16,3840]{1,0:T(8,128)(2,1)S(1)}, u32[]{:S(2)}, u32[]{:S(2)}) collective-permute-start(bf16[16,3840]{1,0:T(8,128)(2,1)S(1)} %add_convert_fusion.1), channel_id=1, source_target_pairs={{0,24},{1,7},{2,26},{3,5},{4,28},{5,3},{6,30},{7,1},{8,16},{9,15},... | collective-permute-start | bytes 368648 | tf_op jit(solution)/shard_map/ppermute | solution.py:338
  44.1 0.3 collective-permute-start.13
  44.4 1.6 %collective-permute-start.12 = (bf16[16,3840]{1,0:T(8,128)(2,1)S(1)}, bf16[16,3840]{1,0:T(8,128)(2,1)S(1)}, u32[]{:S(2)}, u32[]{:S(2)}) collective-permute-start(bf16[16,3840]{1,0:T(8,128)(2,1)S(1)} %add_convert_fusion.1), channel_id=1, source_target_pairs={{0,8},{1,3},{2,10},{3,1},{4,12},{5,7},{6,14},{7,5},{8,0},{9,11},{1... | collective-permute-start | bytes 368648 | tf_op jit(solution)/shard_map/ppermute | solution.py:338
  46.0 2.4 %collective-permute-done.14 = bf16[16,3840]{1,0:T(8,128)(2,1)S(1)} collective-permute-done((bf16[16,3840]{1,0:T(8,128)(2,1)S(1)}, bf16[16,3840]{1,0:T(8,128)(2,1)S(1)}, u32[]{:S(2)}, u32[]{:S(2)}) %collective-permute-start.14) | collective-permute-done | bytes 122912 | tf_op jit(solution)/shard_map/ppermute | solution.py:338
  48.5 2.8 %collective-permute-done.13 = bf16[16,3840]{1,0:T(8,128)(2,1)S(1)} collective-permute-done((bf16[16,3840]{1,0:T(8,128)(2,1)S(1)}, bf16[16,3840]{1,0:T(8,128)(2,1)S(1)}, u32[]{:S(2)}, u32[]{:S(2)}) %collective-permute-start.13) | collective-permute-done | bytes 122912 | tf_op jit(solution)/shard_map/ppermute | solution.py:338
  51.2 0.1 add_convert_fusion.value_ref
  51.3 0.1 collective-permute-start.15
  51.4 1.3 %collective-permute-done.15.other_ref = bf16[16,3840]{1,0:T(8,128)(2,1)S(1)} collective-permute-done((bf16[16,3840]{1,0:T(8,128)(2,1)S(1)}, bf16[16,3840]{1,0:T(8,128)(2,1)S(1)}, u32[]{:S(2)}, u32[]{:S(2)}) %collective-permute-start.15) | collective-permute-done | bytes 122912 | tf_op jit(solution)/shard_map/ppermute | solution.py:364
  52.7 0.8 %phase_three.1 = (f32[32,768]{1,0:T(8,128)}, f32[32,3072]{1,0:T(8,128)}) custom-call(s32[1]{0:T(128)} %bitcast.mine_ref, bf16[16,3840]{1,0:T(8,128)(2,1)S(1)} %add_convert_fusion.value_ref, bf16[16,3840]{1,0:T(8,128)(2,1)S(1)} %collective-permute-done.15.other_ref), custom_call_target="tpu_custom_call" | custom-call | tf_op jit(solution)/shard_map/phase_three/pallas_call | solution.py:464
  (9 shorter events, 0.3 us)
Async XLA Ops:
  8.0 1.6 %collective-permute-start = (bf16[16,3840]{1,0:T(8,128)(2,1)S(1)}, bf16[16,3840]{1,0:T(8,128)(2,1)S(1)}, u32[]{:S(2)}, u32[]{:S(2)}) collective-permute-start(bf16[16,3840]{1,0:T(8,128)(2,1)S(1)} %get-tuple-element.13), channel_id=1, source_target_pairs={{0,1},{1,0},{2,3},{3,2},{4,5},{5,4},{6,7},{7,6},{8,9},{9,8},{10,11... | collective-permute-start | bytes 368648 | tf_op jit(solution)/shard_map/ppermute | solution.py:354
  9.6 6.6 %collective-permute-start.3 = (bf16[16,3840]{1,0:T(8,128)(2,1)S(1)}, bf16[16,3840]{1,0:T(8,128)(2,1)S(1)}, u32[]{:S(2)}, u32[]{:S(2)}) collective-permute-start(bf16[16,3840]{1,0:T(8,128)(2,1)S(1)} %add_convert_fusion.5), channel_id=1, source_target_pairs={{0,6},{1,25},{2,4},{3,27},{4,2},{5,29},{6,0},{7,31},{8,14},{9,17},... | collective-permute-start | bytes 368648 | tf_op jit(solution)/shard_map/ppermute | solution.py:338
  13.4 4.9 %collective-permute-start.2 = (bf16[16,3840]{1,0:T(8,128)(2,1)S(1)}, bf16[16,3840]{1,0:T(8,128)(2,1)S(1)}, u32[]{:S(2)}, u32[]{:S(2)}) collective-permute-start(bf16[16,3840]{1,0:T(8,128)(2,1)S(1)} %add_convert_fusion.5), channel_id=1, source_target_pairs={{0,4},{1,17},{2,6},{3,19},{4,0},{5,21},{6,2},{7,23},{8,12},{9,25},... | collective-permute-start | bytes 368648 | tf_op jit(solution)/shard_map/ppermute | solution.py:338
  14.0 4.9 %collective-permute-start.1 = (bf16[16,3840]{1,0:T(8,128)(2,1)S(1)}, bf16[16,3840]{1,0:T(8,128)(2,1)S(1)}, u32[]{:S(2)}, u32[]{:S(2)}) collective-permute-start(bf16[16,3840]{1,0:T(8,128)(2,1)S(1)} %add_convert_fusion.5), channel_id=1, source_target_pairs={{0,2},{1,9},{2,0},{3,11},{4,6},{5,13},{6,4},{7,15},{8,10},{9,1},{1... | collective-permute-start | bytes 368648 | tf_op jit(solution)/shard_map/ppermute | solution.py:338
  18.9 6.8 %collective-permute-start.6 = (bf16[16,3840]{1,0:T(8,128)(2,1)S(1)}, bf16[16,3840]{1,0:T(8,128)(2,1)S(1)}, u32[]{:S(2)}, u32[]{:S(2)}) collective-permute-start(bf16[16,3840]{1,0:T(8,128)(2,1)S(1)} %add_convert_fusion.4), channel_id=1, source_target_pairs={{0,24},{1,7},{2,26},{3,5},{4,28},{5,3},{6,30},{7,1},{8,16},{9,15},... | collective-permute-start | bytes 368648 | tf_op jit(solution)/shard_map/ppermute | solution.py:338
  22.6 6.2 %collective-permute-start.5 = (bf16[16,3840]{1,0:T(8,128)(2,1)S(1)}, bf16[16,3840]{1,0:T(8,128)(2,1)S(1)}, u32[]{:S(2)}, u32[]{:S(2)}) collective-permute-start(bf16[16,3840]{1,0:T(8,128)(2,1)S(1)} %add_convert_fusion.4), channel_id=1, source_target_pairs={{0,16},{1,5},{2,18},{3,7},{4,20},{5,1},{6,22},{7,3},{8,24},{9,13},... | collective-permute-start | bytes 368648 | tf_op jit(solution)/shard_map/ppermute | solution.py:338
  22.6 6.2 %collective-permute-start.4 = (bf16[16,3840]{1,0:T(8,128)(2,1)S(1)}, bf16[16,3840]{1,0:T(8,128)(2,1)S(1)}, u32[]{:S(2)}, u32[]{:S(2)}) collective-permute-start(bf16[16,3840]{1,0:T(8,128)(2,1)S(1)} %add_convert_fusion.4), channel_id=1, source_target_pairs={{0,8},{1,3},{2,10},{3,1},{4,12},{5,7},{6,14},{7,5},{8,0},{9,11},{1... | collective-permute-start | bytes 368648 | tf_op jit(solution)/shard_map/ppermute | solution.py:338
  28.9 1.4 %collective-permute-start.7 = (bf16[16,3840]{1,0:T(8,128)(2,1)S(1)}, bf16[16,3840]{1,0:T(8,128)(2,1)S(1)}, u32[]{:S(2)}, u32[]{:S(2)}) collective-permute-start(bf16[16,3840]{1,0:T(8,128)(2,1)S(1)} %add_convert_fusion.3.value_ref), channel_id=1, source_target_pairs={{0,1},{1,0},{2,3},{3,2},{4,5},{5,4},{6,7},{7,6},{8,9},{9,8},{10,11... | collective-permute-start | bytes 368648 | tf_op jit(solution)/shard_map/ppermute | solution.py:364
  32.9 1.4 %collective-permute-start.8 = (bf16[16,3840]{1,0:T(8,128)(2,1)S(1)}, bf16[16,3840]{1,0:T(8,128)(2,1)S(1)}, u32[]{:S(2)}, u32[]{:S(2)}) collective-permute-start(bf16[16,3840]{1,0:T(8,128)(2,1)S(1)} %get-tuple-element.19), channel_id=1, source_target_pairs={{0,1},{1,0},{2,3},{3,2},{4,5},{5,4},{6,7},{7,6},{8,9},{9,8},{10,11... | collective-permute-start | bytes 368648 | tf_op jit(solution)/shard_map/ppermute | solution.py:354
  34.3 5.8 %collective-permute-start.11 = (bf16[16,3840]{1,0:T(8,128)(2,1)S(1)}, bf16[16,3840]{1,0:T(8,128)(2,1)S(1)}, u32[]{:S(2)}, u32[]{:S(2)}) collective-permute-start(bf16[16,3840]{1,0:T(8,128)(2,1)S(1)} %add_convert_fusion.2), channel_id=1, source_target_pairs={{0,6},{1,25},{2,4},{3,27},{4,2},{5,29},{6,0},{7,31},{8,14},{9,17},... | collective-permute-start | bytes 368648 | tf_op jit(solution)/shard_map/ppermute | solution.py:338
  36.1 4.9 %collective-permute-start.10 = (bf16[16,3840]{1,0:T(8,128)(2,1)S(1)}, bf16[16,3840]{1,0:T(8,128)(2,1)S(1)}, u32[]{:S(2)}, u32[]{:S(2)}) collective-permute-start(bf16[16,3840]{1,0:T(8,128)(2,1)S(1)} %add_convert_fusion.2), channel_id=1, source_target_pairs={{0,4},{1,17},{2,6},{3,19},{4,0},{5,21},{6,2},{7,23},{8,12},{9,25},... | collective-permute-start | bytes 368648 | tf_op jit(solution)/shard_map/ppermute | solution.py:338
  36.6 4.9 %collective-permute-start.9 = (bf16[16,3840]{1,0:T(8,128)(2,1)S(1)}, bf16[16,3840]{1,0:T(8,128)(2,1)S(1)}, u32[]{:S(2)}, u32[]{:S(2)}) collective-permute-start(bf16[16,3840]{1,0:T(8,128)(2,1)S(1)} %add_convert_fusion.2), channel_id=1, source_target_pairs={{0,2},{1,9},{2,0},{3,11},{4,6},{5,13},{6,4},{7,15},{8,10},{9,1},{1... | collective-permute-start | bytes 368648 | tf_op jit(solution)/shard_map/ppermute | solution.py:338
  41.6 6.9 %collective-permute-start.14 = (bf16[16,3840]{1,0:T(8,128)(2,1)S(1)}, bf16[16,3840]{1,0:T(8,128)(2,1)S(1)}, u32[]{:S(2)}, u32[]{:S(2)}) collective-permute-start(bf16[16,3840]{1,0:T(8,128)(2,1)S(1)} %add_convert_fusion.1), channel_id=1, source_target_pairs={{0,24},{1,7},{2,26},{3,5},{4,28},{5,3},{6,30},{7,1},{8,16},{9,15},... | collective-permute-start | bytes 368648 | tf_op jit(solution)/shard_map/ppermute | solution.py:338
  44.1 7.1 %collective-permute-start.13 = (bf16[16,3840]{1,0:T(8,128)(2,1)S(1)}, bf16[16,3840]{1,0:T(8,128)(2,1)S(1)}, u32[]{:S(2)}, u32[]{:S(2)}) collective-permute-start(bf16[16,3840]{1,0:T(8,128)(2,1)S(1)} %add_convert_fusion.1), channel_id=1, source_target_pairs={{0,16},{1,5},{2,18},{3,7},{4,20},{5,1},{6,22},{7,3},{8,24},{9,13},... | collective-permute-start | bytes 368648 | tf_op jit(solution)/shard_map/ppermute | solution.py:338
  44.4 6.8 %collective-permute-start.12 = (bf16[16,3840]{1,0:T(8,128)(2,1)S(1)}, bf16[16,3840]{1,0:T(8,128)(2,1)S(1)}, u32[]{:S(2)}, u32[]{:S(2)}) collective-permute-start(bf16[16,3840]{1,0:T(8,128)(2,1)S(1)} %add_convert_fusion.1), channel_id=1, source_target_pairs={{0,8},{1,3},{2,10},{3,1},{4,12},{5,7},{6,14},{7,5},{8,0},{9,11},{1... | collective-permute-start | bytes 368648 | tf_op jit(solution)/shard_map/ppermute | solution.py:338
  51.3 1.4 %collective-permute-start.15 = (bf16[16,3840]{1,0:T(8,128)(2,1)S(1)}, bf16[16,3840]{1,0:T(8,128)(2,1)S(1)}, u32[]{:S(2)}, u32[]{:S(2)}) collective-permute-start(bf16[16,3840]{1,0:T(8,128)(2,1)S(1)} %add_convert_fusion.value_ref), channel_id=1, source_target_pairs={{0,1},{1,0},{2,3},{3,2},{4,5},{5,4},{6,7},{7,6},{8,9},{9,8},{10,11... | collective-permute-start | bytes 368648 | tf_op jit(solution)/shard_map/ppermute | solution.py:364

commit v6 on v5

--- a/solution.py
+++ b/solution.py
@@ -12,7 +12,9 @@
 LEFT = 8
 BLOCK = 512
 TALL = 7
-PIECE = 1024
+SUBLANES = 8
+GROUP = 8
+PIECE = 512
 
 
 def phase_one(
@@ -135,6 +137,11 @@
 
     lax.fori_loop(0, blocks, both_step, 0)
 
+    for copy in copies[5:]:
+        copy.wait()
+    thin_second = lax.dot_general(
+        second[...].astype(jnp.bfloat16), grad_ref[...], nt, preferred_element_type=jnp.float32
+    ).astype(jnp.bfloat16)
     added = conv[0]
     for slab in range(1, slabs):
         added = added + conv[slab]
@@ -147,24 +154,29 @@
     inverse = lax.rsqrt(spread + 1e-06)
     place = lax.broadcasted_iota(jnp.int32, (rows, LANES), 0)
     real = lax.rem(place, ROW) < extent
-    for copy in copies[5:]:
-        copy.wait()
     for slab in range(slabs):
         lanes = slice(slab * LANES, (slab + 1) * LANES)
         value = (conv[slab] - center) * inverse * gain[lanes].reshape(1, LANES) + norm_bias[lanes].reshape(1, LANES)
         normed_ref[:, lanes] = jnp.where(real, value, 0.0).astype(jnp.bfloat16)
 
     normed = normed_ref[...]
-    thin_second = lax.dot_general(
-        second[...].astype(jnp.bfloat16), grad_ref[...], nt, preferred_element_type=jnp.float32
-    ).astype(jnp.bfloat16)
     thin = jnp.zeros((first.shape[0], rows), jnp.float32)
-    for start in range(0, hidden_units, PIECE):
+
+    def expanded(start):
         cut = slice(start, start + PIECE)
         hidden = jnp.dot(normed, expand[:, cut], preferred_element_type=jnp.float32)
-        hidden = hidden + expand_bias[cut].reshape(1, PIECE)
-        cdf = 0.5 * (1.0 + lax.erf(hidden * 0.7071067811865476))
-        slope = cdf + hidden * jnp.exp(-0.5 * hidden * hidden) * 0.3989422804014327
+        return hidden + expand_bias[cut].reshape(1, PIECE)
+
+    starts = range(0, hidden_units, PIECE)
+    ahead = expanded(0)
+    for start in starts:
+        cut = slice(start, start + PIECE)
+        hidden = ahead
+        if start + PIECE < hidden_units:
+            ahead = expanded(start + PIECE)
+        cdf = 1.0 + lax.erf(hidden * 0.7071067811865476)
+        bell = lax.exp2(hidden * hidden * -0.7213475204444817)
+        slope = cdf + (hidden * 0.7978845608028654) * bell
         activated = (hidden * cdf).astype(jnp.bfloat16)
         hid = (back[:, cut] * slope).astype(jnp.bfloat16)
         activated_ref[:, cut] = activated
@@ -198,28 +210,41 @@
     across = lax.broadcasted_iota(jnp.int32, (size, size), 1)
     eye = jnp.where(spot == across, 1.0, 0.0).astype(jnp.float32)
     work = jnp.concatenate([gram_matrix, eye], axis=1)
-    down = lax.broadcasted_iota(jnp.int32, (size, wide), 0)
-    group = 4
-    for base in range(0, size, group):
+    down = lax.broadcasted_iota(jnp.int32, (SUBLANES, wide), 0)
+    tiles = [work[k : k + SUBLANES, :] for k in range(0, size, SUBLANES)]
+    for base in range(0, size, GROUP):
+        top, spot = base // SUBLANES, base % SUBLANES
+        count = len(tiles) - top
         cols = [
-            jnp.broadcast_to(work[:, base + b : base + b + 1], (size, wide)) for b in range(group)
+            [
+                jnp.broadcast_to(tile[:, base + b : base + b + 1], (SUBLANES, wide))
+                for tile in tiles[top:]
+            ]
+            for b in range(GROUP)
         ]
-        rows = [work[base + b : base + b + 1, :] for b in range(group)]
-        for b in range(group):
-            scale = lax.rsqrt(cols[b][base + b : base + b + 1, :])
+        rows = [tiles[top][spot + b : spot + b + 1, :] for b in range(GROUP)]
+        for b in range(GROUP):
+            scale = lax.rsqrt(cols[b][0][spot + b : spot + b + 1, :])
             rows[b] = rows[b] * scale
-            cols[b] = cols[b] * scale
-            for c in range(b + 1, group):
-                factor = cols[b][base + c : base + c + 1, :]
+            cols[b] = [col * scale for col in cols[b]]
+            for c in range(b + 1, GROUP):
+                factor = cols[b][0][spot + c : spot + c + 1, :]
                 rows[c] = rows[c] - factor * rows[b]
-                cols[c] = cols[c] - cols[b] * factor
-        change = jnp.zeros((size, wide), jnp.float32)
-        for b in range(group):
-            change = change + cols[b] * rows[b]
-        work = jnp.where(down >= base + group, work - change, work)
-        for b in range(group):
-            work = jnp.where(down == base + b, rows[b], work)
-    return work[:, size:]
+                cols[c] = [cols[c][k] - cols[b][k] * factor for k in range(count)]
+        for k in range(count):
+            change = cols[0][k] * rows[0]
+            for b in range(1, GROUP):
+                change = change + cols[b][k] * rows[b]
+            tile = tiles[top + k]
+            if k:
+                tile = tile - change
+            else:
+                if spot + GROUP < SUBLANES:
+                    tile = jnp.where(down >= spot + GROUP, tile - change, tile)
+                for b in range(GROUP):
+                    tile = jnp.where(down == spot + b, rows[b], tile)
+            tiles[top + k] = tile
+    return jnp.concatenate(tiles, axis=0)[:, size:]
 
 
 def phase_two(
@@ -462,7 +487,7 @@
     )(mine, value, other, normed, activated, grad, hid)
     value, other = exchange(keep, give, mine)
     second, first = pl.pallas_call(
-        functools.partial(phase_three, scale),
+        functools.partial(phase_three, 0.5 * scale),
         out_shape=(
             jax.ShapeDtypeStruct((rank, width), f32),
             jax.ShapeDtypeStruct((rank, hidden_units), f32),

time: 53.7 us -> 53.3 us (level)
  no operation moved by 1% of the time
where the time goes in v6:
time: 53.3 us; the launch traced here: 53.2 us
  waiting for transfers between devices  23.8 us (45%)
  starting transfers between devices  17.9 us (34%)
  Pallas kernels  10.4 us (20%)
  between operations  0.71 us (1%)
    ppermute x12, waiting for transfers between devices, partner(): return lax.ppermute(sent, ('outer', 'inner'), perm).astype(jnp.float32)  19 us
    ppermute x12, starting transfers between devices, partner(): return lax.ppermute(sent, ('outer', 'inner'), perm).astype(jnp.float32)  16.9 us
    pallas_call x1, Pallas kernels, shards(): pl.pallas_call(phase_one, out_shape=(jax.ShapeDtypeStruct((half, total),...  7.21 us
    ppermute x2, waiting for transfers between devices, exchange(): other = lax.ppermute(value, ('outer', 'inner'), pair_perm(count))  2.65 us
    pallas_call x1, Pallas kernels, shards(): pl.pallas_call(phase_two, out_shape=(jax.ShapeDtypeStruct((half, total),...  2.38 us
    ppermute x2, waiting for transfers between devices, exchange(): got = lax.ppermute(give, ('outer', 'inner'), pair_perm(count))  2.16 us
  transfers between devices with their start and end apart: 16, of which 14 were waited for; matrix products, arithmetic and copies ran while one was open for 0% of the time, Pallas kernels for 0%

profile of v6, /device:TPU:0, one launch (start us, length us, event | category | flops | bytes accessed | tf_op | source)
XLA Modules:
  0.0 53.2 jit_solution(14560863327262954279)
XLA Ops:
  0.6 7.2 %phase_one.1 = (f32[16,3840]{1,0:T(8,128)S(1)}, bf16[16,3840]{1,0:T(8,128)(2,1)S(1)}, bf16[224,768]{1,0:T(8,128)(2,1)S(1)}, bf16[224,3072]{1,0:T(8,128)(2,1)S(1)...) custom-call(s32[1]{0:T(128)} %bitcast.mine_ref, bf16[1,14,14,768]{3,2,1,0:T(8,128)(2,1)} %images_hbm.1, ...), custom_call_target="tpu_custom_call" | custom-call | tf_op jit(solution)/shard_map/phase_one/pallas_call | solution.py:426
  7.9 0.6 %collective-permute-start = (bf16[16,3840]{1,0:T(8,128)(2,1)S(1)}, bf16[16,3840]{1,0:T(8,128)(2,1)S(1)}, u32[]{:S(2)}, u32[]{:S(2)}) collective-permute-start(bf16[16,3840]{1,0:T(8,128)(2,1)S(1)} %get-tuple-element.13), channel_id=1, source_target_pairs={{0,1},{1,0},{2,3},{3,2},{4,5},{5,4},{6,7},{7,6},{8,9},{9,8},{10,11... | collective-permute-start | bytes 368648 | tf_op jit(solution)/shard_map/ppermute | solution.py:379
  8.4 1.0 %collective-permute-done = bf16[16,3840]{1,0:T(8,128)(2,1)S(1)} collective-permute-done((bf16[16,3840]{1,0:T(8,128)(2,1)S(1)}, bf16[16,3840]{1,0:T(8,128)(2,1)S(1)}, u32[]{:S(2)}, u32[]{:S(2)}) %collective-permute-start) | collective-permute-done | bytes 122912 | tf_op jit(solution)/shard_map/ppermute | solution.py:379
  9.4 3.8 %collective-permute-start.3 = (bf16[16,3840]{1,0:T(8,128)(2,1)S(1)}, bf16[16,3840]{1,0:T(8,128)(2,1)S(1)}, u32[]{:S(2)}, u32[]{:S(2)}) collective-permute-start(bf16[16,3840]{1,0:T(8,128)(2,1)S(1)} %add_convert_fusion.5), channel_id=1, source_target_pairs={{0,6},{1,25},{2,4},{3,27},{4,2},{5,29},{6,0},{7,31},{8,14},{9,17},... | collective-permute-start | bytes 368648 | tf_op jit(solution)/shard_map/ppermute | solution.py:363
  13.3 0.5 %collective-permute-start.2 = (bf16[16,3840]{1,0:T(8,128)(2,1)S(1)}, bf16[16,3840]{1,0:T(8,128)(2,1)S(1)}, u32[]{:S(2)}, u32[]{:S(2)}) collective-permute-start(bf16[16,3840]{1,0:T(8,128)(2,1)S(1)} %add_convert_fusion.5), channel_id=1, source_target_pairs={{0,4},{1,17},{2,6},{3,19},{4,0},{5,21},{6,2},{7,23},{8,12},{9,25},... | collective-permute-start | bytes 368648 | tf_op jit(solution)/shard_map/ppermute | solution.py:363
  13.8 0.1 collective-permute-start.1
  13.9 2.2 %collective-permute-done.3 = bf16[16,3840]{1,0:T(8,128)(2,1)S(1)} collective-permute-done((bf16[16,3840]{1,0:T(8,128)(2,1)S(1)}, bf16[16,3840]{1,0:T(8,128)(2,1)S(1)}, u32[]{:S(2)}, u32[]{:S(2)}) %collective-permute-start.3) | collective-permute-done | bytes 122912 | tf_op jit(solution)/shard_map/ppermute | solution.py:363
  16.1 2.0 %collective-permute-done.2 = bf16[16,3840]{1,0:T(8,128)(2,1)S(1)} collective-permute-done((bf16[16,3840]{1,0:T(8,128)(2,1)S(1)}, bf16[16,3840]{1,0:T(8,128)(2,1)S(1)}, u32[]{:S(2)}, u32[]{:S(2)}) %collective-permute-start.2) | collective-permute-done | bytes 122912 | tf_op jit(solution)/shard_map/ppermute | solution.py:363
  18.2 0.5 %collective-permute-done.1 = bf16[16,3840]{1,0:T(8,128)(2,1)S(1)} collective-permute-done((bf16[16,3840]{1,0:T(8,128)(2,1)S(1)}, bf16[16,3840]{1,0:T(8,128)(2,1)S(1)}, u32[]{:S(2)}, u32[]{:S(2)}) %collective-permute-start.1) | collective-permute-done | bytes 122912 | tf_op jit(solution)/shard_map/ppermute | solution.py:363
  18.8 3.7 %collective-permute-start.6 = (bf16[16,3840]{1,0:T(8,128)(2,1)S(1)}, bf16[16,3840]{1,0:T(8,128)(2,1)S(1)}, u32[]{:S(2)}, u32[]{:S(2)}) collective-permute-start(bf16[16,3840]{1,0:T(8,128)(2,1)S(1)} %add_convert_fusion.4), channel_id=1, source_target_pairs={{0,24},{1,7},{2,26},{3,5},{4,28},{5,3},{6,30},{7,1},{8,16},{9,15},... | collective-permute-start | bytes 368648 | tf_op jit(solution)/shard_map/ppermute | solution.py:363
  22.4 0.8 %collective-permute-start.4 = (bf16[16,3840]{1,0:T(8,128)(2,1)S(1)}, bf16[16,3840]{1,0:T(8,128)(2,1)S(1)}, u32[]{:S(2)}, u32[]{:S(2)}) collective-permute-start(bf16[16,3840]{1,0:T(8,128)(2,1)S(1)} %add_convert_fusion.4), channel_id=1, source_target_pairs={{0,8},{1,3},{2,10},{3,1},{4,12},{5,7},{6,14},{7,5},{8,0},{9,11},{1... | collective-permute-start | bytes 368648 | tf_op jit(solution)/shard_map/ppermute | solution.py:363
  23.2 2.4 %collective-permute-done.6 = bf16[16,3840]{1,0:T(8,128)(2,1)S(1)} collective-permute-done((bf16[16,3840]{1,0:T(8,128)(2,1)S(1)}, bf16[16,3840]{1,0:T(8,128)(2,1)S(1)}, u32[]{:S(2)}, u32[]{:S(2)}) %collective-permute-start.6) | collective-permute-done | bytes 122912 | tf_op jit(solution)/shard_map/ppermute | solution.py:363
  25.6 3.1 %collective-permute-done.5 = bf16[16,3840]{1,0:T(8,128)(2,1)S(1)} collective-permute-done((bf16[16,3840]{1,0:T(8,128)(2,1)S(1)}, bf16[16,3840]{1,0:T(8,128)(2,1)S(1)}, u32[]{:S(2)}, u32[]{:S(2)}) %collective-permute-start.5) | collective-permute-done | bytes 122912 | tf_op jit(solution)/shard_map/ppermute | solution.py:363
  28.7 0.1 collective-permute-start.7
  28.8 1.3 %collective-permute-done.7.other_ref = bf16[16,3840]{1,0:T(8,128)(2,1)S(1)} collective-permute-done((bf16[16,3840]{1,0:T(8,128)(2,1)S(1)}, bf16[16,3840]{1,0:T(8,128)(2,1)S(1)}, u32[]{:S(2)}, u32[]{:S(2)}) %collective-permute-start.7) | collective-permute-done | bytes 122912 | tf_op jit(solution)/shard_map/ppermute | solution.py:389
  30.1 2.4 %phase_two.1 = (f32[16,3840]{1,0:T(8,128)S(1)}, bf16[16,3840]{1,0:T(8,128)(2,1)S(1)}) custom-call(s32[1]{0:T(128)} %bitcast.mine_ref, bf16[16,3840]{1,0:T(8,128)(2,1)S(1)} %add_convert_fusion.3.value_ref, bf16[16,3840]{1,0:T(8,128)(2,1)S(1)} %collective-permute-done.7.other_ref, bf16[224,768]{1,0:T(8,128)(2,1)S(1)} %get-tuple-element.14.normed_ref, ...), custom_call_target="tpu_custom_call" | custom-call | tf_op jit(solution)/shard_map/phase_two/pallas_call | solution.py:477
  32.5 0.2 collective-permute-start.8
  32.8 1.2 %collective-permute-done.8 = bf16[16,3840]{1,0:T(8,128)(2,1)S(1)} collective-permute-done((bf16[16,3840]{1,0:T(8,128)(2,1)S(1)}, bf16[16,3840]{1,0:T(8,128)(2,1)S(1)}, u32[]{:S(2)}, u32[]{:S(2)}) %collective-permute-start.8) | collective-permute-done | bytes 122912 | tf_op jit(solution)/shard_map/ppermute | solution.py:379
  34.0 1.8 %collective-permute-start.11 = (bf16[16,3840]{1,0:T(8,128)(2,1)S(1)}, bf16[16,3840]{1,0:T(8,128)(2,1)S(1)}, u32[]{:S(2)}, u32[]{:S(2)}) collective-permute-start(bf16[16,3840]{1,0:T(8,128)(2,1)S(1)} %add_convert_fusion.2), channel_id=1, source_target_pairs={{0,6},{1,25},{2,4},{3,27},{4,2},{5,29},{6,0},{7,31},{8,14},{9,17},... | collective-permute-start | bytes 368648 | tf_op jit(solution)/shard_map/ppermute | solution.py:363
  35.7 0.5 collective-permute-start.10
  36.3 1.3 %collective-permute-start.9 = (bf16[16,3840]{1,0:T(8,128)(2,1)S(1)}, bf16[16,3840]{1,0:T(8,128)(2,1)S(1)}, u32[]{:S(2)}, u32[]{:S(2)}) collective-permute-start(bf16[16,3840]{1,0:T(8,128)(2,1)S(1)} %add_convert_fusion.2), channel_id=1, source_target_pairs={{0,2},{1,9},{2,0},{3,11},{4,6},{5,13},{6,4},{7,15},{8,10},{9,1},{1... | collective-permute-start | bytes 368648 | tf_op jit(solution)/shard_map/ppermute | solution.py:363
  37.5 2.3 %collective-permute-done.11 = bf16[16,3840]{1,0:T(8,128)(2,1)S(1)} collective-permute-done((bf16[16,3840]{1,0:T(8,128)(2,1)S(1)}, bf16[16,3840]{1,0:T(8,128)(2,1)S(1)}, u32[]{:S(2)}, u32[]{:S(2)}) %collective-permute-start.11) | collective-permute-done | bytes 122912 | tf_op jit(solution)/shard_map/ppermute | solution.py:363
  39.8 0.8 %collective-permute-done.10 = bf16[16,3840]{1,0:T(8,128)(2,1)S(1)} collective-permute-done((bf16[16,3840]{1,0:T(8,128)(2,1)S(1)}, bf16[16,3840]{1,0:T(8,128)(2,1)S(1)}, u32[]{:S(2)}, u32[]{:S(2)}) %collective-permute-start.10) | collective-permute-done | bytes 122912 | tf_op jit(solution)/shard_map/ppermute | solution.py:363
  40.6 0.5 collective-permute-done.9
  41.2 2.5 %collective-permute-start.14 = (bf16[16,3840]{1,0:T(8,128)(2,1)S(1)}, bf16[16,3840]{1,0:T(8,128)(2,1)S(1)}, u32[]{:S(2)}, u32[]{:S(2)}) collective-permute-start(bf16[16,3840]{1,0:T(8,128)(2,1)S(1)} %add_convert_fusion.1), channel_id=1, source_target_pairs={{0,24},{1,7},{2,26},{3,5},{4,28},{5,3},{6,30},{7,1},{8,16},{9,15},... | collective-permute-start | bytes 368648 | tf_op jit(solution)/shard_map/ppermute | solution.py:363
  43.7 0.3 collective-permute-start.13
  44.0 1.6 %collective-permute-start.12 = (bf16[16,3840]{1,0:T(8,128)(2,1)S(1)}, bf16[16,3840]{1,0:T(8,128)(2,1)S(1)}, u32[]{:S(2)}, u32[]{:S(2)}) collective-permute-start(bf16[16,3840]{1,0:T(8,128)(2,1)S(1)} %add_convert_fusion.1), channel_id=1, source_target_pairs={{0,8},{1,3},{2,10},{3,1},{4,12},{5,7},{6,14},{7,5},{8,0},{9,11},{1... | collective-permute-start | bytes 368648 | tf_op jit(solution)/shard_map/ppermute | solution.py:363
  45.7 2.4 %collective-permute-done.14 = bf16[16,3840]{1,0:T(8,128)(2,1)S(1)} collective-permute-done((bf16[16,3840]{1,0:T(8,128)(2,1)S(1)}, bf16[16,3840]{1,0:T(8,128)(2,1)S(1)}, u32[]{:S(2)}, u32[]{:S(2)}) %collective-permute-start.14) | collective-permute-done | bytes 122912 | tf_op jit(solution)/shard_map/ppermute | solution.py:363
  48.1 2.8 %collective-permute-done.13 = bf16[16,3840]{1,0:T(8,128)(2,1)S(1)} collective-permute-done((bf16[16,3840]{1,0:T(8,128)(2,1)S(1)}, bf16[16,3840]{1,0:T(8,128)(2,1)S(1)}, u32[]{:S(2)}, u32[]{:S(2)}) %collective-permute-start.13) | collective-permute-done | bytes 122912 | tf_op jit(solution)/shard_map/ppermute | solution.py:363
  50.9 0.1 collective-permute-start.15
  51.0 1.3 %collective-permute-done.15.other_ref = bf16[16,3840]{1,0:T(8,128)(2,1)S(1)} collective-permute-done((bf16[16,3840]{1,0:T(8,128)(2,1)S(1)}, bf16[16,3840]{1,0:T(8,128)(2,1)S(1)}, u32[]{:S(2)}, u32[]{:S(2)}) %collective-permute-start.15) | collective-permute-done | bytes 122912 | tf_op jit(solution)/shard_map/ppermute | solution.py:389
  52.3 0.8 %phase_three.1 = (f32[32,768]{1,0:T(8,128)}, f32[32,3072]{1,0:T(8,128)}) custom-call(s32[1]{0:T(128)} %bitcast.mine_ref, bf16[16,3840]{1,0:T(8,128)(2,1)S(1)} %add_convert_fusion.value_ref, bf16[16,3840]{1,0:T(8,128)(2,1)S(1)} %collective-permute-done.15.other_ref), custom_call_target="tpu_custom_call" | custom-call | tf_op jit(solution)/shard_map/phase_three/pallas_call | solution.py:489
  (9 shorter events, 0.3 us)
Async XLA Ops:
  7.9 1.6 %collective-permute-start = (bf16[16,3840]{1,0:T(8,128)(2,1)S(1)}, bf16[16,3840]{1,0:T(8,128)(2,1)S(1)}, u32[]{:S(2)}, u32[]{:S(2)}) collective-permute-start(bf16[16,3840]{1,0:T(8,128)(2,1)S(1)} %get-tuple-element.13), channel_id=1, source_target_pairs={{0,1},{1,0},{2,3},{3,2},{4,5},{5,4},{6,7},{7,6},{8,9},{9,8},{10,11... | collective-permute-start | bytes 368648 | tf_op jit(solution)/shard_map/ppermute | solution.py:379
  9.4 6.7 %collective-permute-start.3 = (bf16[16,3840]{1,0:T(8,128)(2,1)S(1)}, bf16[16,3840]{1,0:T(8,128)(2,1)S(1)}, u32[]{:S(2)}, u32[]{:S(2)}) collective-permute-start(bf16[16,3840]{1,0:T(8,128)(2,1)S(1)} %add_convert_fusion.5), channel_id=1, source_target_pairs={{0,6},{1,25},{2,4},{3,27},{4,2},{5,29},{6,0},{7,31},{8,14},{9,17},... | collective-permute-start | bytes 368648 | tf_op jit(solution)/shard_map/ppermute | solution.py:363
  13.3 4.9 %collective-permute-start.2 = (bf16[16,3840]{1,0:T(8,128)(2,1)S(1)}, bf16[16,3840]{1,0:T(8,128)(2,1)S(1)}, u32[]{:S(2)}, u32[]{:S(2)}) collective-permute-start(bf16[16,3840]{1,0:T(8,128)(2,1)S(1)} %add_convert_fusion.5), channel_id=1, source_target_pairs={{0,4},{1,17},{2,6},{3,19},{4,0},{5,21},{6,2},{7,23},{8,12},{9,25},... | collective-permute-start | bytes 368648 | tf_op jit(solution)/shard_map/ppermute | solution.py:363
  13.8 4.9 %collective-permute-start.1 = (bf16[16,3840]{1,0:T(8,128)(2,1)S(1)}, bf16[16,3840]{1,0:T(8,128)(2,1)S(1)}, u32[]{:S(2)}, u32[]{:S(2)}) collective-permute-start(bf16[16,3840]{1,0:T(8,128)(2,1)S(1)} %add_convert_fusion.5), channel_id=1, source_target_pairs={{0,2},{1,9},{2,0},{3,11},{4,6},{5,13},{6,4},{7,15},{8,10},{9,1},{1... | collective-permute-start | bytes 368648 | tf_op jit(solution)/shard_map/ppermute | solution.py:363
  18.8 6.8 %collective-permute-start.6 = (bf16[16,3840]{1,0:T(8,128)(2,1)S(1)}, bf16[16,3840]{1,0:T(8,128)(2,1)S(1)}, u32[]{:S(2)}, u32[]{:S(2)}) collective-permute-start(bf16[16,3840]{1,0:T(8,128)(2,1)S(1)} %add_convert_fusion.4), channel_id=1, source_target_pairs={{0,24},{1,7},{2,26},{3,5},{4,28},{5,3},{6,30},{7,1},{8,16},{9,15},... | collective-permute-start | bytes 368648 | tf_op jit(solution)/shard_map/ppermute | solution.py:363
  22.4 6.2 %collective-permute-start.5 = (bf16[16,3840]{1,0:T(8,128)(2,1)S(1)}, bf16[16,3840]{1,0:T(8,128)(2,1)S(1)}, u32[]{:S(2)}, u32[]{:S(2)}) collective-permute-start(bf16[16,3840]{1,0:T(8,128)(2,1)S(1)} %add_convert_fusion.4), channel_id=1, source_target_pairs={{0,16},{1,5},{2,18},{3,7},{4,20},{5,1},{6,22},{7,3},{8,24},{9,13},... | collective-permute-start | bytes 368648 | tf_op jit(solution)/shard_map/ppermute | solution.py:363
  22.4 6.2 %collective-permute-start.4 = (bf16[16,3840]{1,0:T(8,128)(2,1)S(1)}, bf16[16,3840]{1,0:T(8,128)(2,1)S(1)}, u32[]{:S(2)}, u32[]{:S(2)}) collective-permute-start(bf16[16,3840]{1,0:T(8,128)(2,1)S(1)} %add_convert_fusion.4), channel_id=1, source_target_pairs={{0,8},{1,3},{2,10},{3,1},{4,12},{5,7},{6,14},{7,5},{8,0},{9,11},{1... | collective-permute-start | bytes 368648 | tf_op jit(solution)/shard_map/ppermute | solution.py:363
  28.7 1.4 %collective-permute-start.7 = (bf16[16,3840]{1,0:T(8,128)(2,1)S(1)}, bf16[16,3840]{1,0:T(8,128)(2,1)S(1)}, u32[]{:S(2)}, u32[]{:S(2)}) collective-permute-start(bf16[16,3840]{1,0:T(8,128)(2,1)S(1)} %add_convert_fusion.3.value_ref), channel_id=1, source_target_pairs={{0,1},{1,0},{2,3},{3,2},{4,5},{5,4},{6,7},{7,6},{8,9},{9,8},{10,11... | collective-permute-start | bytes 368648 | tf_op jit(solution)/shard_map/ppermute | solution.py:389
  32.5 1.4 %collective-permute-start.8 = (bf16[16,3840]{1,0:T(8,128)(2,1)S(1)}, bf16[16,3840]{1,0:T(8,128)(2,1)S(1)}, u32[]{:S(2)}, u32[]{:S(2)}) collective-permute-start(bf16[16,3840]{1,0:T(8,128)(2,1)S(1)} %get-tuple-element.19), channel_id=1, source_target_pairs={{0,1},{1,0},{2,3},{3,2},{4,5},{5,4},{6,7},{7,6},{8,9},{9,8},{10,11... | collective-permute-start | bytes 368648 | tf_op jit(solution)/shard_map/ppermute | solution.py:379
  34.0 5.8 %collective-permute-start.11 = (bf16[16,3840]{1,0:T(8,128)(2,1)S(1)}, bf16[16,3840]{1,0:T(8,128)(2,1)S(1)}, u32[]{:S(2)}, u32[]{:S(2)}) collective-permute-start(bf16[16,3840]{1,0:T(8,128)(2,1)S(1)} %add_convert_fusion.2), channel_id=1, source_target_pairs={{0,6},{1,25},{2,4},{3,27},{4,2},{5,29},{6,0},{7,31},{8,14},{9,17},... | collective-permute-start | bytes 368648 | tf_op jit(solution)/shard_map/ppermute | solution.py:363
  35.7 4.9 %collective-permute-start.10 = (bf16[16,3840]{1,0:T(8,128)(2,1)S(1)}, bf16[16,3840]{1,0:T(8,128)(2,1)S(1)}, u32[]{:S(2)}, u32[]{:S(2)}) collective-permute-start(bf16[16,3840]{1,0:T(8,128)(2,1)S(1)} %add_convert_fusion.2), channel_id=1, source_target_pairs={{0,4},{1,17},{2,6},{3,19},{4,0},{5,21},{6,2},{7,23},{8,12},{9,25},... | collective-permute-start | bytes 368648 | tf_op jit(solution)/shard_map/ppermute | solution.py:363
  36.3 4.9 %collective-permute-start.9 = (bf16[16,3840]{1,0:T(8,128)(2,1)S(1)}, bf16[16,3840]{1,0:T(8,128)(2,1)S(1)}, u32[]{:S(2)}, u32[]{:S(2)}) collective-permute-start(bf16[16,3840]{1,0:T(8,128)(2,1)S(1)} %add_convert_fusion.2), channel_id=1, source_target_pairs={{0,2},{1,9},{2,0},{3,11},{4,6},{5,13},{6,4},{7,15},{8,10},{9,1},{1... | collective-permute-start | bytes 368648 | tf_op jit(solution)/shard_map/ppermute | solution.py:363
  41.2 6.9 %collective-permute-start.14 = (bf16[16,3840]{1,0:T(8,128)(2,1)S(1)}, bf16[16,3840]{1,0:T(8,128)(2,1)S(1)}, u32[]{:S(2)}, u32[]{:S(2)}) collective-permute-start(bf16[16,3840]{1,0:T(8,128)(2,1)S(1)} %add_convert_fusion.1), channel_id=1, source_target_pairs={{0,24},{1,7},{2,26},{3,5},{4,28},{5,3},{6,30},{7,1},{8,16},{9,15},... | collective-permute-start | bytes 368648 | tf_op jit(solution)/shard_map/ppermute | solution.py:363
  43.7 7.1 %collective-permute-start.13 = (bf16[16,3840]{1,0:T(8,128)(2,1)S(1)}, bf16[16,3840]{1,0:T(8,128)(2,1)S(1)}, u32[]{:S(2)}, u32[]{:S(2)}) collective-permute-start(bf16[16,3840]{1,0:T(8,128)(2,1)S(1)} %add_convert_fusion.1), channel_id=1, source_target_pairs={{0,16},{1,5},{2,18},{3,7},{4,20},{5,1},{6,22},{7,3},{8,24},{9,13},... | collective-permute-start | bytes 368648 | tf_op jit(solution)/shard_map/ppermute | solution.py:363
  44.0 6.8 %collective-permute-start.12 = (bf16[16,3840]{1,0:T(8,128)(2,1)S(1)}, bf16[16,3840]{1,0:T(8,128)(2,1)S(1)}, u32[]{:S(2)}, u32[]{:S(2)}) collective-permute-start(bf16[16,3840]{1,0:T(8,128)(2,1)S(1)} %add_convert_fusion.1), channel_id=1, source_target_pairs={{0,8},{1,3},{2,10},{3,1},{4,12},{5,7},{6,14},{7,5},{8,0},{9,11},{1... | collective-permute-start | bytes 368648 | tf_op jit(solution)/shard_map/ppermute | solution.py:363
  50.9 1.4 %collective-permute-start.15 = (bf16[16,3840]{1,0:T(8,128)(2,1)S(1)}, bf16[16,3840]{1,0:T(8,128)(2,1)S(1)}, u32[]{:S(2)}, u32[]{:S(2)}) collective-permute-start(bf16[16,3840]{1,0:T(8,128)(2,1)S(1)} %add_convert_fusion.value_ref), channel_id=1, source_target_pairs={{0,1},{1,0},{2,3},{3,2},{4,5},{5,4},{6,7},{7,6},{8,9},{9,8},{10,11... | collective-permute-start | bytes 368648 | tf_op jit(solution)/shard_map/ppermute | solution.py:389

commit v7 on v6

--- a/solution.py
+++ b/solution.py
@@ -18,7 +18,6 @@
 
 
 def phase_one(
-    mine_ref,
     images_hbm,
     cotangent_hbm,
     taps_hbm,
@@ -191,7 +190,7 @@
     sums = jnp.dot(thin.astype(jnp.bfloat16), normed, preferred_element_type=jnp.float32)
     low[:, :channels] = sums[:half]
     high[:, :channels] = sums[half:]
-    mine = mine_ref[0]
+    mine = lax.rem(linear_index(), 2)
 
     @pl.when(mine == 0)
     def _():
@@ -248,11 +247,11 @@
 
 
 def phase_two(
-    mine_ref, value_ref, other_ref, normed_ref, activated_ref, grad_ref, hid_ref, keep_ref, give_ref
+    value_ref, other_ref, normed_ref, activated_ref, grad_ref, hid_ref, keep_ref, give_ref
 ):
     channels = normed_ref.shape[1]
     half = value_ref.shape[0]
-    mine = mine_ref[0]
+    mine = lax.rem(linear_index(), 2)
     value = value_ref[...]
     other = other_ref[...]
     low = jnp.where(mine == 0, value, other)
@@ -278,10 +277,10 @@
 
 
 def phase_three(
-    factor, mine_ref, value_ref, other_ref, second_hbm, first_hbm, second, first, sems
+    factor, value_ref, other_ref, second_hbm, first_hbm, second, first, sems
 ):
     half, channels = value_ref.shape[0], second.shape[1]
-    mine = mine_ref[0]
+    mine = lax.rem(linear_index(), 2)
     copies = (
         pltpu.make_async_copy(first, first_hbm, sems.at[0]),
         pltpu.make_async_copy(second, second_hbm, sems.at[1]),
@@ -372,7 +371,7 @@
     return [(source, source ^ 1) for source in range(count)]
 
 
-def exchange(keep, give, mine):
+def exchange(keep, give):
     n_outer, n_inner = lax.axis_size("outer"), lax.axis_size("inner")
     count = n_outer * n_inner
     steps = plan(n_outer, n_inner)[1:]
@@ -392,7 +391,6 @@
 
 VMEM = pl.BlockSpec(memory_space=pltpu.VMEM)
 HBM = pl.BlockSpec(memory_space=pltpu.HBM)
-SMEM = pl.BlockSpec(memory_space=pltpu.SMEM)
 
 
 def stay(value):
@@ -422,7 +420,6 @@
     rows, half, total = extent * ROW, rank // 2, width + hidden_units
     slabs = width // LANES
     bf16, f32 = jnp.bfloat16, jnp.float32
-    mine = (linear_index() % 2).astype(jnp.int32).reshape(1)
     keep, give, normed, activated, grad, hid = pl.pallas_call(
         phase_one,
         out_shape=(
@@ -433,7 +430,7 @@
             jax.ShapeDtypeStruct((rows, width), bf16),
             jax.ShapeDtypeStruct((rows, hidden_units), bf16),
         ),
-        in_specs=[SMEM] + [HBM] * 12,
+        in_specs=[HBM] * 12,
         out_specs=(VMEM,) * 6,
         scratch_shapes=[
             pltpu.VMEM(images.shape[1:], bf16),
@@ -459,7 +456,6 @@
         compiler_params=pltpu.CompilerParams(vmem_limit_bytes=40 * 1024 * 1024),
         name="phase_one",
     )(
-        mine,
         stay(images),
         stay(cotangent),
         stay(conv_weight),
@@ -473,26 +469,26 @@
         stay(right_first.T),
         stay(right_second.T),
     )
-    value, other = exchange(keep, give, mine)
+    value, other = exchange(keep, give)
     keep, give = pl.pallas_call(
         phase_two,
         out_shape=(
             jax.ShapeDtypeStruct((half, total), f32),
             jax.ShapeDtypeStruct((half, total), bf16),
         ),
-        in_specs=[SMEM] + [VMEM] * 6,
+        in_specs=[VMEM] * 6,
         out_specs=(VMEM, VMEM),
         compiler_params=pltpu.CompilerParams(vmem_limit_bytes=40 * 1024 * 1024),
         name="phase_two",
-    )(mine, value, other, normed, activated, grad, hid)
-    value, other = exchange(keep, give, mine)
+    )(value, other, normed, activated, grad, hid)
+    value, other = exchange(keep, give)
     second, first = pl.pallas_call(
         functools.partial(phase_three, 0.5 * scale),
         out_shape=(
             jax.ShapeDtypeStruct((rank, width), f32),
             jax.ShapeDtypeStruct((rank, hidden_units), f32),
         ),
-        in_specs=[SMEM, VMEM, VMEM],
+        in_specs=[VMEM, VMEM],
         out_specs=(HBM, HBM),
         scratch_shapes=[
             pltpu.VMEM((rank, width), f32),
@@ -501,7 +497,7 @@
         ],
         compiler_params=pltpu.CompilerParams(vmem_limit_bytes=8 * 1024 * 1024),
         name="phase_three",
-    )(mine, value, other)
+    )(value, other)
     return (first.T, second.T)
 
 

time: 53.3 us -> 53.4 us (level)
  no operation moved by 1% of the time
where the time goes in v7:
time: 53.4 us; the launch traced here: 53.2 us
  waiting for transfers between devices  23.8 us (45%)
  starting transfers between devices  17.9 us (34%)
  Pallas kernels  10.5 us (20%)
  between operations  0.7 us (1%)
    ppermute x12, waiting for transfers between devices, partner(): return lax.ppermute(sent, ('outer', 'inner'), perm).astype(jnp.float32)  19 us
    ppermute x12, starting transfers between devices, partner(): return lax.ppermute(sent, ('outer', 'inner'), perm).astype(jnp.float32)  16.9 us
    pallas_call x1, Pallas kernels, shards(): pl.pallas_call(phase_one, out_shape=(jax.ShapeDtypeStruct((half, total),...  7.29 us
    ppermute x2, waiting for transfers between devices, exchange(): other = lax.ppermute(value, ('outer', 'inner'), pair_perm(count))  2.65 us
    pallas_call x1, Pallas kernels, shards(): pl.pallas_call(phase_two, out_shape=(jax.ShapeDtypeStruct((half, total),...  2.39 us
    ppermute x2, waiting for transfers between devices, exchange(): got = lax.ppermute(give, ('outer', 'inner'), pair_perm(count))  2.16 us
  transfers between devices with their start and end apart: 16, of which 14 were waited for; matrix products, arithmetic and copies ran while one was open for 0% of the time, Pallas kernels for 0%

profile of v7, /device:TPU:0, one launch (start us, length us, event | category | flops | bytes accessed | tf_op | source)
XLA Modules:
  0.0 53.2 jit_solution(13806330191556341966)
XLA Ops:
  0.6 7.3 %phase_one.1 = (f32[16,3840]{1,0:T(8,128)S(1)}, bf16[16,3840]{1,0:T(8,128)(2,1)S(1)}, bf16[224,768]{1,0:T(8,128)(2,1)S(1)}, bf16[224,3072]{1,0:T(8,128)(2,1)S(1)...) custom-call(bf16[1,14,14,768]{3,2,1,0:T(8,128)(2,1)} %images_hbm.1, ...), custom_call_target="tpu_custom_call" | custom-call | tf_op jit(solution)/shard_map/phase_one/pallas_call | solution.py:423
  7.9 0.6 %collective-permute-start = (bf16[16,3840]{1,0:T(8,128)(2,1)S(1)}, bf16[16,3840]{1,0:T(8,128)(2,1)S(1)}, u32[]{:S(2)}, u32[]{:S(2)}) collective-permute-start(bf16[16,3840]{1,0:T(8,128)(2,1)S(1)} %get-tuple-element.13), channel_id=1, source_target_pairs={{0,1},{1,0},{2,3},{3,2},{4,5},{5,4},{6,7},{7,6},{8,9},{9,8},{10,11... | collective-permute-start | bytes 368648 | tf_op jit(solution)/shard_map/ppermute | solution.py:378
  8.5 1.0 %collective-permute-done = bf16[16,3840]{1,0:T(8,128)(2,1)S(1)} collective-permute-done((bf16[16,3840]{1,0:T(8,128)(2,1)S(1)}, bf16[16,3840]{1,0:T(8,128)(2,1)S(1)}, u32[]{:S(2)}, u32[]{:S(2)}) %collective-permute-start) | collective-permute-done | bytes 122912 | tf_op jit(solution)/shard_map/ppermute | solution.py:378
  9.5 3.8 %collective-permute-start.3 = (bf16[16,3840]{1,0:T(8,128)(2,1)S(1)}, bf16[16,3840]{1,0:T(8,128)(2,1)S(1)}, u32[]{:S(2)}, u32[]{:S(2)}) collective-permute-start(bf16[16,3840]{1,0:T(8,128)(2,1)S(1)} %add_convert_fusion.5), channel_id=1, source_target_pairs={{0,6},{1,25},{2,4},{3,27},{4,2},{5,29},{6,0},{7,31},{8,14},{9,17},... | collective-permute-start | bytes 368648 | tf_op jit(solution)/shard_map/ppermute | solution.py:362
  13.4 0.5 collective-permute-start.2
  13.9 0.1 collective-permute-start.1
  14.0 2.2 %collective-permute-done.3 = bf16[16,3840]{1,0:T(8,128)(2,1)S(1)} collective-permute-done((bf16[16,3840]{1,0:T(8,128)(2,1)S(1)}, bf16[16,3840]{1,0:T(8,128)(2,1)S(1)}, u32[]{:S(2)}, u32[]{:S(2)}) %collective-permute-start.3) | collective-permute-done | bytes 122912 | tf_op jit(solution)/shard_map/ppermute | solution.py:362
  16.2 2.0 %collective-permute-done.2 = bf16[16,3840]{1,0:T(8,128)(2,1)S(1)} collective-permute-done((bf16[16,3840]{1,0:T(8,128)(2,1)S(1)}, bf16[16,3840]{1,0:T(8,128)(2,1)S(1)}, u32[]{:S(2)}, u32[]{:S(2)}) %collective-permute-start.2) | collective-permute-done | bytes 122912 | tf_op jit(solution)/shard_map/ppermute | solution.py:362
  18.2 0.5 collective-permute-done.1
  18.8 3.7 %collective-permute-start.6 = (bf16[16,3840]{1,0:T(8,128)(2,1)S(1)}, bf16[16,3840]{1,0:T(8,128)(2,1)S(1)}, u32[]{:S(2)}, u32[]{:S(2)}) collective-permute-start(bf16[16,3840]{1,0:T(8,128)(2,1)S(1)} %add_convert_fusion.4), channel_id=1, source_target_pairs={{0,24},{1,7},{2,26},{3,5},{4,28},{5,3},{6,30},{7,1},{8,16},{9,15},... | collective-permute-start | bytes 368648 | tf_op jit(solution)/shard_map/ppermute | solution.py:362
  22.5 0.8 %collective-permute-start.4 = (bf16[16,3840]{1,0:T(8,128)(2,1)S(1)}, bf16[16,3840]{1,0:T(8,128)(2,1)S(1)}, u32[]{:S(2)}, u32[]{:S(2)}) collective-permute-start(bf16[16,3840]{1,0:T(8,128)(2,1)S(1)} %add_convert_fusion.4), channel_id=1, source_target_pairs={{0,8},{1,3},{2,10},{3,1},{4,12},{5,7},{6,14},{7,5},{8,0},{9,11},{1... | collective-permute-start | bytes 368648 | tf_op jit(solution)/shard_map/ppermute | solution.py:362
  23.3 2.4 %collective-permute-done.6 = bf16[16,3840]{1,0:T(8,128)(2,1)S(1)} collective-permute-done((bf16[16,3840]{1,0:T(8,128)(2,1)S(1)}, bf16[16,3840]{1,0:T(8,128)(2,1)S(1)}, u32[]{:S(2)}, u32[]{:S(2)}) %collective-permute-start.6) | collective-permute-done | bytes 122912 | tf_op jit(solution)/shard_map/ppermute | solution.py:362
  25.7 3.1 %collective-permute-done.5 = bf16[16,3840]{1,0:T(8,128)(2,1)S(1)} collective-permute-done((bf16[16,3840]{1,0:T(8,128)(2,1)S(1)}, bf16[16,3840]{1,0:T(8,128)(2,1)S(1)}, u32[]{:S(2)}, u32[]{:S(2)}) %collective-permute-start.5) | collective-permute-done | bytes 122912 | tf_op jit(solution)/shard_map/ppermute | solution.py:362
  28.8 0.1 collective-permute-start.7
  28.9 1.3 %collective-permute-done.7.other_ref = bf16[16,3840]{1,0:T(8,128)(2,1)S(1)} collective-permute-done((bf16[16,3840]{1,0:T(8,128)(2,1)S(1)}, bf16[16,3840]{1,0:T(8,128)(2,1)S(1)}, u32[]{:S(2)}, u32[]{:S(2)}) %collective-permute-start.7) | collective-permute-done | bytes 122912 | tf_op jit(solution)/shard_map/ppermute | solution.py:388
  30.2 2.4 %phase_two.1 = (f32[16,3840]{1,0:T(8,128)S(1)}, bf16[16,3840]{1,0:T(8,128)(2,1)S(1)}) custom-call(bf16[16,3840]{1,0:T(8,128)(2,1)S(1)} %add_convert_fusion.3.value_ref, bf16[16,3840]{1,0:T(8,128)(2,1)S(1)} %collective-permute-done.7.other_ref, bf16[224,768]{1,0:T(8,128)(2,1)S(1)} %get-tuple-element.14.normed_ref, ...), custom_call_target="tpu_custom_call" | custom-call | tf_op jit(solution)/shard_map/phase_two/pallas_call | solution.py:473
  32.6 0.2 collective-permute-start.8
  32.8 1.2 %collective-permute-done.8 = bf16[16,3840]{1,0:T(8,128)(2,1)S(1)} collective-permute-done((bf16[16,3840]{1,0:T(8,128)(2,1)S(1)}, bf16[16,3840]{1,0:T(8,128)(2,1)S(1)}, u32[]{:S(2)}, u32[]{:S(2)}) %collective-permute-start.8) | collective-permute-done | bytes 122912 | tf_op jit(solution)/shard_map/ppermute | solution.py:378
  34.0 1.7 %collective-permute-start.11 = (bf16[16,3840]{1,0:T(8,128)(2,1)S(1)}, bf16[16,3840]{1,0:T(8,128)(2,1)S(1)}, u32[]{:S(2)}, u32[]{:S(2)}) collective-permute-start(bf16[16,3840]{1,0:T(8,128)(2,1)S(1)} %add_convert_fusion.2), channel_id=1, source_target_pairs={{0,6},{1,25},{2,4},{3,27},{4,2},{5,29},{6,0},{7,31},{8,14},{9,17},... | collective-permute-start | bytes 368648 | tf_op jit(solution)/shard_map/ppermute | solution.py:362
  35.8 0.5 %collective-permute-start.10 = (bf16[16,3840]{1,0:T(8,128)(2,1)S(1)}, bf16[16,3840]{1,0:T(8,128)(2,1)S(1)}, u32[]{:S(2)}, u32[]{:S(2)}) collective-permute-start(bf16[16,3840]{1,0:T(8,128)(2,1)S(1)} %add_convert_fusion.2), channel_id=1, source_target_pairs={{0,4},{1,17},{2,6},{3,19},{4,0},{5,21},{6,2},{7,23},{8,12},{9,25},... | collective-permute-start | bytes 368648 | tf_op jit(solution)/shard_map/ppermute | solution.py:362
  36.3 1.3 %collective-permute-start.9 = (bf16[16,3840]{1,0:T(8,128)(2,1)S(1)}, bf16[16,3840]{1,0:T(8,128)(2,1)S(1)}, u32[]{:S(2)}, u32[]{:S(2)}) collective-permute-start(bf16[16,3840]{1,0:T(8,128)(2,1)S(1)} %add_convert_fusion.2), channel_id=1, source_target_pairs={{0,2},{1,9},{2,0},{3,11},{4,6},{5,13},{6,4},{7,15},{8,10},{9,1},{1... | collective-permute-start | bytes 368648 | tf_op jit(solution)/shard_map/ppermute | solution.py:362
  37.6 2.3 %collective-permute-done.11 = bf16[16,3840]{1,0:T(8,128)(2,1)S(1)} collective-permute-done((bf16[16,3840]{1,0:T(8,128)(2,1)S(1)}, bf16[16,3840]{1,0:T(8,128)(2,1)S(1)}, u32[]{:S(2)}, u32[]{:S(2)}) %collective-permute-start.11) | collective-permute-done | bytes 122912 | tf_op jit(solution)/shard_map/ppermute | solution.py:362
  39.9 0.8 %collective-permute-done.10 = bf16[16,3840]{1,0:T(8,128)(2,1)S(1)} collective-permute-done((bf16[16,3840]{1,0:T(8,128)(2,1)S(1)}, bf16[16,3840]{1,0:T(8,128)(2,1)S(1)}, u32[]{:S(2)}, u32[]{:S(2)}) %collective-permute-start.10) | collective-permute-done | bytes 122912 | tf_op jit(solution)/shard_map/ppermute | solution.py:362
  40.7 0.5 %collective-permute-done.9 = bf16[16,3840]{1,0:T(8,128)(2,1)S(1)} collective-permute-done((bf16[16,3840]{1,0:T(8,128)(2,1)S(1)}, bf16[16,3840]{1,0:T(8,128)(2,1)S(1)}, u32[]{:S(2)}, u32[]{:S(2)}) %collective-permute-start.9) | collective-permute-done | bytes 122912 | tf_op jit(solution)/shard_map/ppermute | solution.py:362
  41.3 2.5 %collective-permute-start.14 = (bf16[16,3840]{1,0:T(8,128)(2,1)S(1)}, bf16[16,3840]{1,0:T(8,128)(2,1)S(1)}, u32[]{:S(2)}, u32[]{:S(2)}) collective-permute-start(bf16[16,3840]{1,0:T(8,128)(2,1)S(1)} %add_convert_fusion.1), channel_id=1, source_target_pairs={{0,24},{1,7},{2,26},{3,5},{4,28},{5,3},{6,30},{7,1},{8,16},{9,15},... | collective-permute-start | bytes 368648 | tf_op jit(solution)/shard_map/ppermute | solution.py:362
  43.8 0.3 collective-permute-start.13
  44.1 1.6 %collective-permute-start.12 = (bf16[16,3840]{1,0:T(8,128)(2,1)S(1)}, bf16[16,3840]{1,0:T(8,128)(2,1)S(1)}, u32[]{:S(2)}, u32[]{:S(2)}) collective-permute-start(bf16[16,3840]{1,0:T(8,128)(2,1)S(1)} %add_convert_fusion.1), channel_id=1, source_target_pairs={{0,8},{1,3},{2,10},{3,1},{4,12},{5,7},{6,14},{7,5},{8,0},{9,11},{1... | collective-permute-start | bytes 368648 | tf_op jit(solution)/shard_map/ppermute | solution.py:362
  45.7 2.4 %collective-permute-done.14 = bf16[16,3840]{1,0:T(8,128)(2,1)S(1)} collective-permute-done((bf16[16,3840]{1,0:T(8,128)(2,1)S(1)}, bf16[16,3840]{1,0:T(8,128)(2,1)S(1)}, u32[]{:S(2)}, u32[]{:S(2)}) %collective-permute-start.14) | collective-permute-done | bytes 122912 | tf_op jit(solution)/shard_map/ppermute | solution.py:362
  48.2 2.8 %collective-permute-done.13 = bf16[16,3840]{1,0:T(8,128)(2,1)S(1)} collective-permute-done((bf16[16,3840]{1,0:T(8,128)(2,1)S(1)}, bf16[16,3840]{1,0:T(8,128)(2,1)S(1)}, u32[]{:S(2)}, u32[]{:S(2)}) %collective-permute-start.13) | collective-permute-done | bytes 122912 | tf_op jit(solution)/shard_map/ppermute | solution.py:362
  51.0 0.1 collective-permute-start.15
  51.1 1.3 %collective-permute-done.15.other_ref = bf16[16,3840]{1,0:T(8,128)(2,1)S(1)} collective-permute-done((bf16[16,3840]{1,0:T(8,128)(2,1)S(1)}, bf16[16,3840]{1,0:T(8,128)(2,1)S(1)}, u32[]{:S(2)}, u32[]{:S(2)}) %collective-permute-start.15) | collective-permute-done | bytes 122912 | tf_op jit(solution)/shard_map/ppermute | solution.py:388
  52.4 0.8 %phase_three.1 = (f32[32,768]{1,0:T(8,128)}, f32[32,3072]{1,0:T(8,128)}) custom-call(bf16[16,3840]{1,0:T(8,128)(2,1)S(1)} %add_convert_fusion.value_ref, bf16[16,3840]{1,0:T(8,128)(2,1)S(1)} %collective-permute-done.15.other_ref), custom_call_target="tpu_custom_call" | custom-call | tf_op jit(solution)/shard_map/phase_three/pallas_call | solution.py:485
  (9 shorter events, 0.3 us)
Async XLA Ops:
  7.9 1.6 %collective-permute-start = (bf16[16,3840]{1,0:T(8,128)(2,1)S(1)}, bf16[16,3840]{1,0:T(8,128)(2,1)S(1)}, u32[]{:S(2)}, u32[]{:S(2)}) collective-permute-start(bf16[16,3840]{1,0:T(8,128)(2,1)S(1)} %get-tuple-element.13), channel_id=1, source_target_pairs={{0,1},{1,0},{2,3},{3,2},{4,5},{5,4},{6,7},{7,6},{8,9},{9,8},{10,11... | collective-permute-start | bytes 368648 | tf_op jit(solution)/shard_map/ppermute | solution.py:378
  9.5 6.7 %collective-permute-start.3 = (bf16[16,3840]{1,0:T(8,128)(2,1)S(1)}, bf16[16,3840]{1,0:T(8,128)(2,1)S(1)}, u32[]{:S(2)}, u32[]{:S(2)}) collective-permute-start(bf16[16,3840]{1,0:T(8,128)(2,1)S(1)} %add_convert_fusion.5), channel_id=1, source_target_pairs={{0,6},{1,25},{2,4},{3,27},{4,2},{5,29},{6,0},{7,31},{8,14},{9,17},... | collective-permute-start | bytes 368648 | tf_op jit(solution)/shard_map/ppermute | solution.py:362
  13.4 4.9 %collective-permute-start.2 = (bf16[16,3840]{1,0:T(8,128)(2,1)S(1)}, bf16[16,3840]{1,0:T(8,128)(2,1)S(1)}, u32[]{:S(2)}, u32[]{:S(2)}) collective-permute-start(bf16[16,3840]{1,0:T(8,128)(2,1)S(1)} %add_convert_fusion.5), channel_id=1, source_target_pairs={{0,4},{1,17},{2,6},{3,19},{4,0},{5,21},{6,2},{7,23},{8,12},{9,25},... | collective-permute-start | bytes 368648 | tf_op jit(solution)/shard_map/ppermute | solution.py:362
  13.9 4.9 %collective-permute-start.1 = (bf16[16,3840]{1,0:T(8,128)(2,1)S(1)}, bf16[16,3840]{1,0:T(8,128)(2,1)S(1)}, u32[]{:S(2)}, u32[]{:S(2)}) collective-permute-start(bf16[16,3840]{1,0:T(8,128)(2,1)S(1)} %add_convert_fusion.5), channel_id=1, source_target_pairs={{0,2},{1,9},{2,0},{3,11},{4,6},{5,13},{6,4},{7,15},{8,10},{9,1},{1... | collective-permute-start | bytes 368648 | tf_op jit(solution)/shard_map/ppermute | solution.py:362
  18.8 6.8 %collective-permute-start.6 = (bf16[16,3840]{1,0:T(8,128)(2,1)S(1)}, bf16[16,3840]{1,0:T(8,128)(2,1)S(1)}, u32[]{:S(2)}, u32[]{:S(2)}) collective-permute-start(bf16[16,3840]{1,0:T(8,128)(2,1)S(1)} %add_convert_fusion.4), channel_id=1, source_target_pairs={{0,24},{1,7},{2,26},{3,5},{4,28},{5,3},{6,30},{7,1},{8,16},{9,15},... | collective-permute-start | bytes 368648 | tf_op jit(solution)/shard_map/ppermute | solution.py:362
  22.5 6.2 %collective-permute-start.5 = (bf16[16,3840]{1,0:T(8,128)(2,1)S(1)}, bf16[16,3840]{1,0:T(8,128)(2,1)S(1)}, u32[]{:S(2)}, u32[]{:S(2)}) collective-permute-start(bf16[16,3840]{1,0:T(8,128)(2,1)S(1)} %add_convert_fusion.4), channel_id=1, source_target_pairs={{0,16},{1,5},{2,18},{3,7},{4,20},{5,1},{6,22},{7,3},{8,24},{9,13},... | collective-permute-start | bytes 368648 | tf_op jit(solution)/shard_map/ppermute | solution.py:362
  22.5 6.2 %collective-permute-start.4 = (bf16[16,3840]{1,0:T(8,128)(2,1)S(1)}, bf16[16,3840]{1,0:T(8,128)(2,1)S(1)}, u32[]{:S(2)}, u32[]{:S(2)}) collective-permute-start(bf16[16,3840]{1,0:T(8,128)(2,1)S(1)} %add_convert_fusion.4), channel_id=1, source_target_pairs={{0,8},{1,3},{2,10},{3,1},{4,12},{5,7},{6,14},{7,5},{8,0},{9,11},{1... | collective-permute-start | bytes 368648 | tf_op jit(solution)/shard_map/ppermute | solution.py:362
  28.8 1.4 %collective-permute-start.7 = (bf16[16,3840]{1,0:T(8,128)(2,1)S(1)}, bf16[16,3840]{1,0:T(8,128)(2,1)S(1)}, u32[]{:S(2)}, u32[]{:S(2)}) collective-permute-start(bf16[16,3840]{1,0:T(8,128)(2,1)S(1)} %add_convert_fusion.3.value_ref), channel_id=1, source_target_pairs={{0,1},{1,0},{2,3},{3,2},{4,5},{5,4},{6,7},{7,6},{8,9},{9,8},{10,11... | collective-permute-start | bytes 368648 | tf_op jit(solution)/shard_map/ppermute | solution.py:388
  32.6 1.4 %collective-permute-start.8 = (bf16[16,3840]{1,0:T(8,128)(2,1)S(1)}, bf16[16,3840]{1,0:T(8,128)(2,1)S(1)}, u32[]{:S(2)}, u32[]{:S(2)}) collective-permute-start(bf16[16,3840]{1,0:T(8,128)(2,1)S(1)} %get-tuple-element.19), channel_id=1, source_target_pairs={{0,1},{1,0},{2,3},{3,2},{4,5},{5,4},{6,7},{7,6},{8,9},{9,8},{10,11... | collective-permute-start | bytes 368648 | tf_op jit(solution)/shard_map/ppermute | solution.py:378
  34.0 5.8 %collective-permute-start.11 = (bf16[16,3840]{1,0:T(8,128)(2,1)S(1)}, bf16[16,3840]{1,0:T(8,128)(2,1)S(1)}, u32[]{:S(2)}, u32[]{:S(2)}) collective-permute-start(bf16[16,3840]{1,0:T(8,128)(2,1)S(1)} %add_convert_fusion.2), channel_id=1, source_target_pairs={{0,6},{1,25},{2,4},{3,27},{4,2},{5,29},{6,0},{7,31},{8,14},{9,17},... | collective-permute-start | bytes 368648 | tf_op jit(solution)/shard_map/ppermute | solution.py:362
  35.8 4.9 %collective-permute-start.10 = (bf16[16,3840]{1,0:T(8,128)(2,1)S(1)}, bf16[16,3840]{1,0:T(8,128)(2,1)S(1)}, u32[]{:S(2)}, u32[]{:S(2)}) collective-permute-start(bf16[16,3840]{1,0:T(8,128)(2,1)S(1)} %add_convert_fusion.2), channel_id=1, source_target_pairs={{0,4},{1,17},{2,6},{3,19},{4,0},{5,21},{6,2},{7,23},{8,12},{9,25},... | collective-permute-start | bytes 368648 | tf_op jit(solution)/shard_map/ppermute | solution.py:362
  36.3 4.9 %collective-permute-start.9 = (bf16[16,3840]{1,0:T(8,128)(2,1)S(1)}, bf16[16,3840]{1,0:T(8,128)(2,1)S(1)}, u32[]{:S(2)}, u32[]{:S(2)}) collective-permute-start(bf16[16,3840]{1,0:T(8,128)(2,1)S(1)} %add_convert_fusion.2), channel_id=1, source_target_pairs={{0,2},{1,9},{2,0},{3,11},{4,6},{5,13},{6,4},{7,15},{8,10},{9,1},{1... | collective-permute-start | bytes 368648 | tf_op jit(solution)/shard_map/ppermute | solution.py:362
  41.3 6.9 %collective-permute-start.14 = (bf16[16,3840]{1,0:T(8,128)(2,1)S(1)}, bf16[16,3840]{1,0:T(8,128)(2,1)S(1)}, u32[]{:S(2)}, u32[]{:S(2)}) collective-permute-start(bf16[16,3840]{1,0:T(8,128)(2,1)S(1)} %add_convert_fusion.1), channel_id=1, source_target_pairs={{0,24},{1,7},{2,26},{3,5},{4,28},{5,3},{6,30},{7,1},{8,16},{9,15},... | collective-permute-start | bytes 368648 | tf_op jit(solution)/shard_map/ppermute | solution.py:362
  43.8 7.1 %collective-permute-start.13 = (bf16[16,3840]{1,0:T(8,128)(2,1)S(1)}, bf16[16,3840]{1,0:T(8,128)(2,1)S(1)}, u32[]{:S(2)}, u32[]{:S(2)}) collective-permute-start(bf16[16,3840]{1,0:T(8,128)(2,1)S(1)} %add_convert_fusion.1), channel_id=1, source_target_pairs={{0,16},{1,5},{2,18},{3,7},{4,20},{5,1},{6,22},{7,3},{8,24},{9,13},... | collective-permute-start | bytes 368648 | tf_op jit(solution)/shard_map/ppermute | solution.py:362
  44.1 6.8 %collective-permute-start.12 = (bf16[16,3840]{1,0:T(8,128)(2,1)S(1)}, bf16[16,3840]{1,0:T(8,128)(2,1)S(1)}, u32[]{:S(2)}, u32[]{:S(2)}) collective-permute-start(bf16[16,3840]{1,0:T(8,128)(2,1)S(1)} %add_convert_fusion.1), channel_id=1, source_target_pairs={{0,8},{1,3},{2,10},{3,1},{4,12},{5,7},{6,14},{7,5},{8,0},{9,11},{1... | collective-permute-start | bytes 368648 | tf_op jit(solution)/shard_map/ppermute | solution.py:362
  51.0 1.4 %collective-permute-start.15 = (bf16[16,3840]{1,0:T(8,128)(2,1)S(1)}, bf16[16,3840]{1,0:T(8,128)(2,1)S(1)}, u32[]{:S(2)}, u32[]{:S(2)}) collective-permute-start(bf16[16,3840]{1,0:T(8,128)(2,1)S(1)} %add_convert_fusion.value_ref), channel_id=1, source_target_pairs={{0,1},{1,0},{2,3},{3,2},{4,5},{5,4},{6,7},{7,6},{8,9},{9,8},{10,11... | collective-permute-start | bytes 368648 | tf_op jit(solution)/shard_map/ppermute | solution.py:388
